TPU v7x, 32 devices: a whole 2x2x4 slice. The times are simulated.
32 devices in a mesh: batch: 4 (over z), seq: 8 (over y, x, core).
Axes of the slice: x: 2, y: 2, z: 4, core: 2. Of those that a mesh axis runs over, the one named last changes fastest.
Arguments:
- hidden: bfloat16 [4, 1024, 1536], P('batch', 'seq'), may hold values from -6 to 6
- norm_gain: bfloat16 [1536], P(('batch', 'seq')), may hold values from 0.5 to 1.5
- w_gate_in: bfloat16 [1536, 3072], P(('batch', 'seq')), may hold values from -0.15625 to 0.15625
- w_conv_in: bfloat16 [1536, 3328], P(('batch', 'seq')), may hold values from -0.15625 to 0.15625
- w_step: bfloat16 [1536, 48], P(('batch', 'seq')), may hold values from -0.375 to 0.375
- conv_weight: bfloat16 [4, 3328], P(None, ('batch', 'seq')), may hold values from -3 to 3
- conv_bias: bfloat16 [3328], P(('batch', 'seq')), may hold values from -3 to 3
- step_bias: float32 [48], replicated, may hold values from -4 to -1
- decay_log: float32 [48], replicated, may hold values from -6 to 0
- skip_gain: float32 [48], replicated, may hold values from 0.5 to 2
- gate_gain: bfloat16 [3072], P(('batch', 'seq')), may hold values from 0.5 to 1.5
- w_out: bfloat16 [3072, 1536], P(('batch', 'seq')), may hold values from -0.109375 to 0.109375
- cotangent: bfloat16 [4, 1024, 1536], P('batch', 'seq'), may hold values from -6 to 6
Outputs:
- output: bfloat16 [4, 1024, 1536], P('batch', 'seq')
- grad_hidden: float32 [4, 1024, 1536], P('batch', 'seq')
- grad_norm_gain: float32 [1536], P(('batch', 'seq'))
- grad_w_gate_in: float32 [1536, 3072], P(('batch', 'seq'))
- grad_w_conv_in: float32 [1536, 3328], P(('batch', 'seq'))
- grad_w_step: float32 [1536, 48], P(('batch', 'seq'))
- grad_conv_weight: float32 [4, 3328], P(None, ('batch', 'seq'))
- grad_conv_bias: float32 [3328], P(('batch', 'seq'))
- grad_step_bias: float32 [48], replicated
- grad_decay_log: float32 [48], replicated
- grad_skip_gain: float32 [48], replicated
- grad_gate_gain: float32 [3072], P(('batch', 'seq'))
- grad_w_out: float32 [3072, 1536], P(('batch', 'seq'))
All inputs are finite; a program needn't handle non-finite values.
Results may differ from a plain program's by a relative error of at most 0.01.
Values may be sent and summed in bfloat16 or wider, within the bound.
No kernel may reach another device: no remote copies, remote signals or barrier semaphores. Data moves between devices by JAX's collectives and lax.ppermute only.
A program may use at most 256 MiB of HBM per device.

v0:
```python
import jax
import jax.numpy as jnp
from jax import lax
from jax.sharding import PartitionSpec as P

norm_epsilon = 1e-05


def shifted(value, axis, steps):
    count = lax.axis_size(axis)
    first, last = (max(0, -steps), min(count, count - steps))
    return lax.ppermute(value, axis, [(source, source + steps) for source in range(first, last)])


def prefix(array, axis, combine, identity, reverse):
    devices, place = (lax.axis_size(axis), lax.axis_index(axis))
    everything = jax.tree.map(lambda part: lax.all_gather(part, axis), array)
    start = jax.tree.map(
        lambda part, zero: jnp.broadcast_to(jnp.asarray(zero, part.dtype), part.shape),
        array,
        identity,
    )

    def hop(k, before):
        at = devices - 1 - k if reverse else k
        reached = at > place if reverse else at < place
        new = combine(before, jax.tree.map(lambda part: part[at], everything))
        return jax.tree.map(lambda a, b: jnp.where(reached, a, b), new, before)

    return lax.fori_loop(0, devices, hop, start)


def for_sending(array):
    return jax.tree.map(lambda a: a.astype(jnp.bfloat16) if a.dtype == jnp.float32 else a, array)


def narrow_product(pattern, former, latter):
    return jnp.einsum(pattern, former, latter, preferred_element_type=jnp.float32)


def wide_product(pattern, former, latter):
    return jnp.einsum(pattern, former, latter, precision=lax.Precision.HIGHEST)


def silu_slope(inputs):
    logistic = jax.nn.sigmoid(inputs)
    return logistic * (1.0 + inputs * (1.0 - logistic))


def upper_table(length):
    rows = lax.broadcasted_iota(jnp.int32, (length, length), 0)
    cols = lax.broadcasted_iota(jnp.int32, (length, length), 1)
    return (rows <= cols).astype(jnp.float32)


def running_total(step_size, head_rate):
    table = upper_table(step_size.shape[0])
    return jnp.dot((step_size * head_rate[None, :]).T, table, precision=lax.Precision.HIGHEST)


def span_parts(value_b, key_b, query_b, step_size, head_rate):
    length = step_size.shape[0]
    cumulative = running_total(step_size, head_rate)
    row_index = lax.broadcasted_iota(jnp.int32, (1, length, length), 1)
    col_index = lax.broadcasted_iota(jnp.int32, (1, length, length), 2)
    causal = row_index >= col_index
    spread = cumulative[:, :, None] - cumulative[:, None, :]
    decays = jnp.where(causal, jnp.exp(jnp.where(causal, spread, 0.0)), 0.0)
    affinity = jnp.dot(query_b, key_b.T, preferred_element_type=jnp.float32)
    step_rows = step_size.T
    scores = affinity[None] * decays * step_rows[:, None, :]
    mixing = scores.astype(jnp.bfloat16)
    within = narrow_product("hts,shp->thp", mixing, value_b)
    tail_decay = jnp.exp(cumulative[:, -1:] - cumulative) * step_rows
    weighted = (tail_decay.T[:, :, None] * value_b.astype(jnp.float32)).astype(jnp.bfloat16)
    span_state = narrow_product("shp,sn->hpn", weighted, key_b)
    total_decay = jnp.exp(cumulative[:, -1])
    return (within, span_state, total_decay, cumulative, decays, affinity, scores, mixing, weighted)


def span_inter(query_b, cumulative, carried):
    base = wide_product("tn,hpn->thp", query_b.astype(jnp.float32), carried)
    return jnp.exp(cumulative).T[:, :, None] * base


def carried_grad(query_b, cumulative, grad_y):
    scaled = grad_y * jnp.exp(cumulative).T[:, :, None]
    return wide_product("thp,tn->hpn", scaled, query_b.astype(jnp.float32))


def span_backward(
    value_b, key_b, query_b, step_size, carried, grad_y, grad_state, grad_total, head_rate
):
    parts = span_parts(value_b, key_b, query_b, step_size, head_rate)
    total_decay, cumulative, decays, affinity, scores, mixing, weighted = parts[2:]
    length = step_size.shape[0]
    query_f = query_b.astype(jnp.float32)
    key_f = key_b.astype(jnp.float32)
    value_f = value_b.astype(jnp.float32)
    step_rows = step_size.T
    growth = jnp.exp(cumulative)
    base = wide_product("tn,hpn->thp", query_f, carried)
    grad_cumul = growth * jnp.sum(grad_y * base, axis=2).T
    grad_query = wide_product("thp,hpn->tn", grad_y * growth.T[:, :, None], carried)
    grad_low = grad_y.astype(jnp.bfloat16)
    grad_mixing = narrow_product("thp,shp->hts", grad_low, value_b)
    grad_value = narrow_product("hts,thp->shp", mixing, grad_low)
    grad_affinity = jnp.sum(grad_mixing * decays * step_rows[:, None, :], axis=0)
    grad_steps = jnp.sum(grad_mixing * affinity[None] * decays, axis=1)
    through = grad_mixing * scores
    grad_cumul = grad_cumul + jnp.sum(through, axis=2) - jnp.sum(through, axis=1)
    grad_query = grad_query + wide_product("ts,sn->tn", grad_affinity, key_f)
    grad_key = wide_product("ts,tn->sn", grad_affinity, query_f)
    grad_weighted = wide_product("hpn,sn->shp", grad_state, key_f)
    grad_key = grad_key + wide_product("shp,hpn->sn", weighted.astype(jnp.float32), grad_state)
    grad_end = jnp.sum(grad_weighted * value_f, axis=2).T
    tail_only = jnp.exp(cumulative[:, -1:] - cumulative)
    grad_value = grad_value + grad_weighted * (tail_only * step_rows).T[:, :, None]
    grad_steps = grad_steps + grad_end * tail_only
    push = grad_end * tail_only * step_rows
    last_flag = lax.broadcasted_iota(jnp.int32, (1, length), 1) == length - 1
    last_term = (jnp.sum(push, axis=1) + grad_total * total_decay)[:, None]
    grad_cumul = grad_cumul - push + jnp.where(last_flag, last_term, 0.0)
    grad_log = jnp.dot(grad_cumul, upper_table(length).T, precision=lax.Precision.HIGHEST)
    grad_steps = grad_steps + grad_log * head_rate[:, None]
    grad_rate = jnp.sum(grad_log * step_rows, axis=1)
    return (grad_value, grad_key, grad_query, grad_steps.T, grad_rate)


def conv_apply(padded, kernel_f, bias_f, length):
    time_axis = padded.ndim - 2
    total = bias_f
    for offset in range(kernel_f.shape[0]):
        total = total + kernel_f[offset] * lax.slice_in_dim(
            padded, offset, offset + length, axis=time_axis
        )
    return total


def conv_back(grad_mixed, padded, kernel_f):
    length = grad_mixed.shape[-2]
    kernel_taps = kernel_f.shape[0]
    time_axis = grad_mixed.ndim - 2
    leading = tuple(range(grad_mixed.ndim - 1))
    grad_kernel = jnp.stack(
        [
            jnp.sum(
                grad_mixed * lax.slice_in_dim(padded, offset, offset + length, axis=time_axis),
                axis=leading,
            )
            for offset in range(kernel_taps)
        ]
    )
    grad_padded = jnp.zeros(padded.shape, jnp.float32)
    for offset in range(kernel_taps):
        widths = [(0, 0)] * grad_mixed.ndim
        widths[time_axis] = (offset, kernel_taps - 1 - offset)
        grad_padded = grad_padded + jnp.pad(grad_mixed * kernel_f[offset], widths)
    return (grad_kernel, grad_padded)


def combine_states(earlier, later):
    return (earlier[0] * later[0], later[0][:, :, None, None] * earlier[1] + later[1])


def local(
    hidden,
    norm_gain,
    w_gate_in,
    w_conv_in,
    w_step,
    conv_weight,
    conv_bias,
    step_bias,
    decay_log,
    skip_gain,
    gate_gain,
    w_out,
    cotangent,
):
    seq_count, length, model_width = hidden.shape
    gathered = (
        lax.all_gather(norm_gain, ("batch", "seq"), axis=0, tiled=True),
        lax.all_gather(w_gate_in, ("batch", "seq"), axis=0, tiled=True),
        lax.all_gather(w_conv_in, ("batch", "seq"), axis=0, tiled=True),
        lax.all_gather(w_step, ("batch", "seq"), axis=0, tiled=True),
        lax.all_gather(conv_weight, ("batch", "seq"), axis=1, tiled=True),
        lax.all_gather(conv_bias, ("batch", "seq"), axis=0, tiled=True),
        lax.all_gather(gate_gain, ("batch", "seq"), axis=0, tiled=True),
        lax.all_gather(w_out, ("batch", "seq"), axis=0, tiled=True),
    )
    (
        norm_full,
        gate_in_full,
        conv_in_full,
        step_full,
        kernel_full,
        bias_full,
        gain_full,
        out_full,
    ) = gathered
    inner_width = gate_in_full.shape[1]
    head_count = step_full.shape[1]
    head_width = inner_width // head_count
    channels = conv_in_full.shape[1]
    state_width = (channels - inner_width) // 2
    kernel_taps = kernel_full.shape[0]
    row_count = seq_count * length
    head_rate = -jnp.exp(decay_log)
    tokens_f = hidden.reshape(row_count, model_width).astype(jnp.float32)
    inv_rms = lax.rsqrt(jnp.mean(tokens_f * tokens_f, axis=1, keepdims=True) + norm_epsilon)
    unit = tokens_f * inv_rms
    normed = (unit * norm_full.astype(jnp.float32)[None]).astype(jnp.bfloat16)
    gate_pre = jnp.dot(normed, gate_in_full, preferred_element_type=jnp.float32)
    conv_pre = (
        jnp.dot(normed, conv_in_full, preferred_element_type=jnp.float32)
        .astype(jnp.bfloat16)
        .reshape(seq_count, length, channels)
    )
    raw_step = jnp.dot(normed, step_full, preferred_element_type=jnp.float32)
    rim = shifted(conv_pre[:, length - (kernel_taps - 1) :, :], "seq", 1)
    extended = jnp.concatenate([rim, conv_pre], axis=1).astype(jnp.float32)
    mixed_in = conv_apply(
        extended, kernel_full.astype(jnp.float32), bias_full.astype(jnp.float32), length
    )
    conv_out = jax.nn.silu(mixed_in).astype(jnp.bfloat16)
    value_b = conv_out[:, :, :inner_width].reshape(seq_count, length, head_count, head_width)
    key_b = conv_out[:, :, inner_width : inner_width + state_width]
    query_b = conv_out[:, :, inner_width + state_width :]
    step_size = jax.nn.softplus(raw_step + step_bias[None]).reshape(seq_count, length, head_count)

    def local_forward(value_piece, key_piece, query_piece, step_piece):
        parts = span_parts(value_piece, key_piece, query_piece, step_piece, head_rate)
        return (parts[0], parts[1], parts[2], parts[3])

    within, span_state, total_decay, cumulative = jax.vmap(local_forward)(
        value_b, key_b, query_b, step_size
    )
    identity = (jnp.ones_like(total_decay), jnp.zeros_like(span_state))
    _, carried = prefix((total_decay, span_state), "seq", combine_states, identity, False)
    inter = jax.vmap(span_inter)(query_b, cumulative, carried)
    value_f = value_b.astype(jnp.float32)
    ssm_out = within + inter + skip_gain[None, None, :, None] * value_f
    flat_out = ssm_out.reshape(row_count, inner_width)
    gate_silu = jax.nn.silu(gate_pre)
    gated = flat_out * gate_silu
    inv_gate = lax.rsqrt(jnp.mean(gated * gated, axis=1, keepdims=True) + norm_epsilon)
    normed_gate = gated * inv_gate
    projected_in = (normed_gate * gain_full.astype(jnp.float32)[None]).astype(jnp.bfloat16)
    output = (
        tokens_f + jnp.dot(projected_in, out_full, preferred_element_type=jnp.float32)
    ).astype(jnp.bfloat16)
    backward_weights = (
        lax.all_gather(norm_gain, ("batch", "seq"), axis=0, tiled=True),
        lax.all_gather(w_gate_in, ("batch", "seq"), axis=0, tiled=True),
        lax.all_gather(w_conv_in, ("batch", "seq"), axis=0, tiled=True),
        lax.all_gather(w_step, ("batch", "seq"), axis=0, tiled=True),
        lax.all_gather(conv_weight, ("batch", "seq"), axis=1, tiled=True),
        lax.all_gather(gate_gain, ("batch", "seq"), axis=0, tiled=True),
        lax.all_gather(w_out, ("batch", "seq"), axis=0, tiled=True),
    )
    norm_back, gate_in_back, conv_in_back, step_back, kernel_back, gain_back, out_back = (
        backward_weights
    )
    incoming = cotangent.reshape(row_count, model_width)
    grad_proj = jnp.dot(incoming, out_back.T, preferred_element_type=jnp.float32)
    grad_w_out = jnp.dot(projected_in.T, incoming, preferred_element_type=jnp.float32)
    grad_gate_gain = jnp.sum(grad_proj * normed_gate, axis=0)
    grad_ngate = grad_proj * gain_back.astype(jnp.float32)[None]
    grad_gated = inv_gate * (
        grad_ngate - normed_gate * jnp.mean(grad_ngate * normed_gate, axis=1, keepdims=True)
    )
    grad_flat = grad_gated * gate_silu
    grad_gate_pre = (grad_gated * flat_out * silu_slope(gate_pre)).astype(jnp.bfloat16)
    grad_ssm = grad_flat.reshape(seq_count, length, head_count, head_width)
    grad_skip = jnp.sum(grad_ssm * value_f, axis=(0, 1, 3))
    grad_carried = jax.vmap(carried_grad)(query_b, cumulative, grad_ssm)
    _, grad_state = prefix((total_decay, grad_carried), "seq", combine_states, identity, True)
    grad_total = jnp.sum(grad_state * carried, axis=(2, 3))

    def local_backward(
        value_piece,
        key_piece,
        query_piece,
        step_piece,
        carried_piece,
        grad_piece,
        state_piece,
        total_piece,
    ):
        return span_backward(
            value_piece,
            key_piece,
            query_piece,
            step_piece,
            carried_piece,
            grad_piece,
            state_piece,
            total_piece,
            head_rate,
        )

    grad_value, grad_key, grad_query, grad_steps, grad_rate = jax.vmap(local_backward)(
        value_b, key_b, query_b, step_size, carried, grad_ssm, grad_state, grad_total
    )
    grad_value = grad_value + grad_ssm * skip_gain[None, None, :, None]
    grad_conv_out = jnp.concatenate(
        [grad_value.reshape(seq_count, length, inner_width), grad_key, grad_query], axis=2
    )
    grad_mixed = grad_conv_out * silu_slope(mixed_in)
    grad_bias = jnp.sum(grad_mixed, axis=(0, 1))
    grad_kernel, grad_padded = conv_back(grad_mixed, extended, kernel_back.astype(jnp.float32))
    back_rim = shifted(for_sending(grad_padded[:, : kernel_taps - 1, :]), "seq", -1)
    grad_core = grad_padded[:, kernel_taps - 1 :, :]
    split_at = length - (kernel_taps - 1)
    grad_core = jnp.concatenate(
        [grad_core[:, :split_at], grad_core[:, split_at:] + back_rim], axis=1
    )
    grad_pre = grad_core.astype(jnp.bfloat16).reshape(row_count, channels)
    grad_raw = grad_steps.reshape(row_count, head_count) * jax.nn.sigmoid(
        raw_step + step_bias[None]
    )
    grad_step_bias = jnp.sum(grad_raw, axis=0)
    grad_raw_low = grad_raw.astype(jnp.bfloat16)
    grad_decay_log = jnp.sum(grad_rate, axis=0) * head_rate
    grad_w_gate_in = jnp.dot(normed.T, grad_gate_pre, preferred_element_type=jnp.float32)
    grad_w_conv_in = jnp.dot(normed.T, grad_pre, preferred_element_type=jnp.float32)
    grad_w_step = jnp.dot(normed.T, grad_raw_low, preferred_element_type=jnp.float32)
    grad_normed = jnp.dot(grad_gate_pre, gate_in_back.T, preferred_element_type=jnp.float32)
    grad_normed = grad_normed + jnp.dot(
        grad_pre, conv_in_back.T, preferred_element_type=jnp.float32
    )
    grad_normed = grad_normed + jnp.dot(
        grad_raw_low, step_back.T, preferred_element_type=jnp.float32
    )
    grad_norm_gain = jnp.sum(grad_normed * unit, axis=0)
    grad_unit = grad_normed * norm_back.astype(jnp.float32)[None]
    grad_tokens = inv_rms * (grad_unit - unit * jnp.mean(grad_unit * unit, axis=1, keepdims=True))
    grad_hidden = (incoming.astype(jnp.float32) + grad_tokens).reshape(
        seq_count, length, model_width
    )
    partial_grads = (
        grad_norm_gain,
        grad_w_gate_in,
        grad_w_conv_in,
        grad_w_step,
        grad_kernel,
        grad_bias,
        grad_gate_gain,
        grad_w_out,
    )
    shares = (
        lax.psum_scatter(partial_grads[0], ("batch", "seq"), scatter_dimension=0, tiled=True),
        lax.psum_scatter(partial_grads[1], ("batch", "seq"), scatter_dimension=0, tiled=True),
        lax.psum_scatter(partial_grads[2], ("batch", "seq"), scatter_dimension=0, tiled=True),
        lax.psum_scatter(partial_grads[3], ("batch", "seq"), scatter_dimension=0, tiled=True),
        lax.psum_scatter(partial_grads[4], ("batch", "seq"), scatter_dimension=1, tiled=True),
        lax.psum_scatter(partial_grads[5], ("batch", "seq"), scatter_dimension=0, tiled=True),
        lax.psum_scatter(partial_grads[6], ("batch", "seq"), scatter_dimension=0, tiled=True),
        lax.psum_scatter(partial_grads[7], ("batch", "seq"), scatter_dimension=0, tiled=True),
    )
    head_sums = lax.psum((grad_step_bias, grad_decay_log, grad_skip), ("batch", "seq"))
    return (
        output.reshape(seq_count, length, model_width),
        grad_hidden,
        shares[0],
        shares[1],
        shares[2],
        shares[3],
        shares[4],
        shares[5],
        head_sums[0],
        head_sums[1],
        head_sums[2],
        shares[6],
        shares[7],
    )


def solution(mesh):
    return jax.shard_map(
        local,
        mesh=mesh,
        in_specs=(
            P("batch", "seq", None),
            P(("batch", "seq")),
            P(("batch", "seq"), None),
            P(("batch", "seq"), None),
            P(("batch", "seq"), None),
            P(None, ("batch", "seq")),
            P(("batch", "seq")),
            P(),
            P(),
            P(),
            P(("batch", "seq")),
            P(("batch", "seq"), None),
            P("batch", "seq", None),
        ),
        out_specs=(
            P("batch", "seq", None),
            P("batch", "seq", None),
            P(("batch", "seq")),
            P(("batch", "seq"), None),
            P(("batch", "seq"), None),
            P(("batch", "seq"), None),
            P(None, ("batch", "seq")),
            P(("batch", "seq")),
            P(),
            P(),
            P(),
            P(("batch", "seq")),
            P(("batch", "seq"), None),
        ),
        check_vma=False,
    )
```

profile of v0, /device:TPU:0, one launch (start us, length us, event | category | flops | bytes accessed | tf_op | source)
XLA Modules:
  0.0 1432.7 jit_solution(5790302102180864530)
XLA Ops:
  10.5 43.0 %all-reduce.12 = (bf16[1536]{0:T(1024)(128)(2,1)S(1)}, bf16[3328]{0:T(1024)(128)(2,1)S(1)}, bf16[3072]{0:T(1024)(128)(2,1)}) all-reduce(bf16[1536]{0:T(1024)(128)(2,1)S(1)} %dynamic-update-slice.1, bf16[3328]{0:T(1024)(128)(2,1)S(1)} %dynamic-update-slice, ...), channel_id=1, replica_groups=mesh['batch'=4,'seq'=8] {'batch','seq'}, use_global_device_ids=true, to_apply=%add.5 | all-reduce | flops 7936 | bytes 31744
  53.5 42.3 %all-gather.3 = bf16[32,104,4]{1,2,0:T(4,128)(2,1)S(1)} all-gather(bf16[1,104,4]{1,2,0:T(4,128)(2,1)} %bitcast.330), channel_id=1, replica_groups=mesh['batch'=4,'seq'=8] {'batch','seq'}, dimensions={0}, use_global_device_ids=true | all-gather | bytes 27456 | tf_op jit(solution)/shard_map/all_gather | solution.py:187
  95.9 38.0 %all_gather.53 = bf16[1536,48]{1,0:T(8,128)(2,1)S(1)} all-gather(bf16[48,48]{1,0:T(8,128)(2,1)} %param.21), channel_id=1, replica_groups=mesh['batch'=4,'seq'=8] {'batch','seq'}, dimensions={0}, use_global_device_ids=true | all-gather | bytes 152064 | tf_op jit(solution)/shard_map/all_gather | solution.py:186
  138.6 5.5 fusion.2
  161.4 10.6 all-gather
  182.4 43.2 %all-gather.16.cloned.1.call-done = f32[384,64,128]{2,1,0:T(8,128)} async-done(((f32[48,64,128]{2,1,0:T(8,128)}), f32[384,64,128]{2,1,0:T(8,128)}) %all-gather.16.cloned.1.call-update) | async-done | bytes 12582928 | tf_op jit(solution)/shard_map/all_gather | solution.py:17
  225.6 19.5 %while.30 = (s32[]{:T(128)}, f32[1,48,64,128]{3,2,1,0:T(8,128)S(1)}, s32[]{:T(128)}, f32[8,1,48]{2,1,0:T(1,128)}, f32[8,1,48,64,128]{4,3,2,1,0:T(8,128)}, /*index=5*/s32[]{:T(128)}, s32[]{:T(128)}) while((s32[]{:T(128)}, f32[1,48,64,128]{3,2,1,0:T(8,128)S(1)}, s32[]{:T(128)}, f32[8,1,48]{2,1,0:T(1,128)}, ...), condition=%wide.region_2.3_spmd.clone, body=%wide.region_1.2_spmd.clone.sunk | while | flops 1572868 | bytes 4719281 | solution.py:30
  252.9 57.2 %all-gather.12.cloned.1.call-done = bf16[1536,3072]{1,0:T(8,128)(2,1)} async-done(((bf16[48,3072]{1,0:T(8,128)(2,1)}), bf16[1536,3072]{1,0:T(8,128)(2,1)}) %all-gather.12.cloned.1.call-update) | async-done | bytes 9437200 | tf_op jit(solution)/shard_map/all_gather | solution.py:184
  310.1 7.5 multiply_reduce_fusion.11
  317.6 75.3 %all-gather.14.cloned.1.call-done = bf16[3072,1536]{1,0:T(8,128)(2,1)} async-done(((bf16[96,1536]{1,0:T(8,128)(2,1)}), bf16[3072,1536]{1,0:T(8,128)(2,1)}) %all-gather.14.cloned.1.call-update) | async-done | bytes 9437200 | tf_op jit(solution)/shard_map/all_gather | solution.py:190
  393.0 8.2 multiply_reduce_fusion.6
  408.9 3.5 fusion.59
  416.9 4.4 fusion.27
  421.3 5.4 fusion.8
  429.5 4.1 fusion.121
  433.6 49.5 %all-gather.18.cloned.1.call-done = f32[384,64,128]{2,1,0:T(8,128)} async-done(((f32[48,64,128]{2,1,0:T(8,128)}), f32[384,64,128]{2,1,0:T(8,128)}) %all-gather.18.cloned.1.call-update) | async-done | bytes 12582928 | tf_op jit(solution)/shard_map/all_gather | solution.py:17
  483.1 31.1 %while.31 = (s32[]{:T(128)}, f32[1,48,64,128]{3,2,1,0:T(8,128)}, s32[]{:T(128)}, f32[8,1,48]{2,1,0:T(1,128)}, f32[8,1,48,64,128]{4,3,2,1,0:T(8,128)}, /*index=5*/s32[]{:T(128)}, s32[]{:T(128)}, s32[]{:T(128)}, s32[]{:T(128)}) while((s32[]{:T(128)}, f32[1,48,64,128]{3,2,1,0:T(8,128)}, s32[]{:T(128)}, f32[8,1,48]{2,1,0:T(1,128)}, ...), condition=%wide.region_6.7_spmd.clone, body=%wide.region_5.6_spmd.clone.sunk | while | flops 1572872 | bytes 4719343 | solution.py:30
  487.4 3.3 fusion.145
  491.3 3.3 fusion.145
  499.1 3.3 fusion.145
  503.1 3.3 fusion.145
  526.5 3.8 multiply_reduce_fusion.5
  538.0 3.4 convolution_add_fusion.1
  544.7 8.0 fusion.110
  554.2 7.9 fusion.45
  563.2 8.8 fusion.44
  572.0 6.0 fusion.6
  579.2 91.8 %all-reduce.15.cloned.1.call-done = (f32[1536]{0:T(1024)}, f32[4,3328]{1,0:T(4,128)}, f32[3328]{0:T(1024)}, f32[48]{0:T(128)}, f32[48]{0:T(128)}, /*index=5*/f32[48]{0:T(128)}, f32[3072]{0:T(1024)}) async-done(((f32[1536]{0:T(1024)}, f32[4,3328]{1,0:T(4,128)}, f32[3328]{0:T(1024)}, f32[48]{0:T(128)}, f32[48]{0:T(128)}, /*index=5*/f32[48]{0:T(128)}, f32[3072]{0:T(1024)}), (f32[1536]{0:T(1024)}, ...) | async-done | bytes 85584
  676.2 97.7 %reduce-scatter.10.cloned.1.call-done = f32[48,48]{1,0:T(8,128)} async-done(((f32[1536,48]{1,0:T(8,128)}), f32[48,48]{1,0:T(8,128)}) %reduce-scatter.10.cloned.1.call-update) | async-done | bytes 9232 | tf_op jit(solution)/shard_map/reduce_scatter | solution.py:356
  773.9 212.9 %reduce-scatter.6.cloned.1.call-done = f32[48,3072]{1,0:T(8,128)} async-done(((f32[1536,3072]{1,0:T(8,128)}), f32[48,3072]{1,0:T(8,128)}) %reduce-scatter.6.cloned.1.call-update) | async-done | bytes 589840 | tf_op jit(solution)/shard_map/reduce_scatter | solution.py:354
  986.8 213.1 %reduce-scatter.12.cloned.1.call-done = f32[96,1536]{1,0:T(8,128)} async-done(((f32[3072,1536]{1,0:T(8,128)}), f32[96,1536]{1,0:T(8,128)}) %reduce-scatter.12.cloned.1.call-update) | async-done | bytes 589840 | tf_op jit(solution)/shard_map/reduce_scatter | solution.py:360
  1199.9 222.0 %reduce-scatter.8.cloned.1.call-done = f32[48,3328]{1,0:T(8,128)} async-done(((f32[1536,3328]{1,0:T(8,128)}), f32[48,3328]{1,0:T(8,128)}) %reduce-scatter.8.cloned.1.call-update) | async-done | bytes 638992 | tf_op jit(solution)/shard_map/reduce_scatter | solution.py:355
  (268 shorter events, 130.6 us)
Async XLA Ops:
  7.2 131.4 %copy-start.4 = (bf16[1,128,1536]{2,1,0:T(8,128)(2,1)S(1)}, bf16[1,128,1536]{2,1,0:T(8,128)(2,1)}, u32[]{:S(2)}) copy-start(bf16[1,128,1536]{2,1,0:T(8,128)(2,1)} %param.17) | copy-start | bytes 1179652
  7.2 131.0 %all-gather.10.cloned.1.call-start = ((), (), s32[]{:S(2)}) async-start(), calls=%async_computation.4 | async-start | bytes 10543104 | tf_op jit(solution)/shard_map/all_gather | solution.py:185
  7.9 217.7 %all-gather.16.cloned.1.call-start = ((), (), s32[]{:S(2)}) async-start(), calls=%async_computation.11 | async-start | bytes 14155776 | tf_op jit(solution)/shard_map/all_gather | solution.py:17
  135.2 8.9 copy-start.39
  137.5 6.5 copy-start.36
  138.2 8.4 copy-start.34
  144.1 4.2 collective-permute-start
  155.0 155.1 %all-gather.12.cloned.1.call-start = ((), (), s32[]{:S(2)}) async-start(), calls=%async_computation.5 | async-start | bytes 9732096 | tf_op jit(solution)/shard_map/all_gather | solution.py:184
  155.8 237.2 %all-gather.14.cloned.1.call-start = ((), (), s32[]{:S(2)}) async-start(), calls=%async_computation.6 | async-start | bytes 9732096 | tf_op jit(solution)/shard_map/all_gather | solution.py:190
  156.3 326.7 %all-gather.18.cloned.1.call-start = ((), (), s32[]{:S(2)}) async-start(), calls=%async_computation.12 | async-start | bytes 14155776 | tf_op jit(solution)/shard_map/all_gather | solution.py:17
  172.7 74.3 %copy-start.42 = (f32[48,128]{1,0:T(8,128)}, f32[48,128]{1,0:T(8,128)S(1)}, u32[]{:S(2)}) copy-start(f32[48,128]{1,0:T(8,128)S(1)} %fusion.107) | copy-start | bytes 73732
  249.8 60.3 %copy-start.40 = (f32[128]{0:T(128)S(1)}, f32[128]{0:T(128)}, u32[]{:S(2)}) copy-start(f32[128]{0:T(128)} %copy-done.39) | copy-start | bytes 1540
  393.0 8.2 copy-start.2
  393.0 8.2 copy-start.7
  393.0 8.2 copy-start.20
  393.0 8.2 copy-start.29
  412.3 258.7 %all-reduce.15.cloned.1.call-start = ((), (), s32[]{:S(2)}) async-start(), calls=%async_computation.13 | async-start | bytes 183296
  416.9 12.5 slice-start.3
  421.3 7.1 copy-start.14
  421.3 7.0 copy-start.17
  421.3 8.1 slice-start.4
  421.3 8.1 slice-start.5
  526.5 11.5 slice-start
  526.5 11.5 slice-start.1
  530.8 7.2 slice-start.2
  532.7 5.2 copy-start.9
  533.3 4.6 collective-permute-start.1
  543.3 230.6 %reduce-scatter.10.cloned.1.call-start = ((), (), s32[]{:S(2)}) async-start(), calls=%async_computation.9 | async-start | bytes 811008 | tf_op jit(solution)/shard_map/reduce_scatter | solution.py:356
  544.7 442.2 %reduce-scatter.6.cloned.1.call-start = ((), (), s32[]{:S(2)}) async-start(), calls=%async_computation.7 | async-start | bytes 19464192 | tf_op jit(solution)/shard_map/reduce_scatter | solution.py:354
  552.7 647.2 %reduce-scatter.12.cloned.1.call-start = ((), (), s32[]{:S(2)}) async-start(), calls=%async_computation.10 | async-start | bytes 19464192 | tf_op jit(solution)/shard_map/reduce_scatter | solution.py:360
  562.1 859.9 %reduce-scatter.8.cloned.1.call-start = ((), (), s32[]{:S(2)}) async-start(), calls=%async_computation.8 | async-start | bytes 21086208 | tf_op jit(solution)/shard_map/reduce_scatter | solution.py:355
  572.0 6.0 copy-start.22
  (44 other events, 111.2 us)
Sparse Core Ops, SparseCore 0:
  10.9 89.1 all-gather.9
  155.1 70.4 all-gather.15
  228.5 81.5 all-gather.11
  312.8 80.0 all-gather.13
  412.5 70.5 all-gather.17
  543.4 127.5 all-reduce.14
  676.7 97.1 reduce-scatter.9
  780.9 205.8 reduce-scatter.5
  993.8 206.0 reduce-scatter.11
  1206.8 215.1 reduce-scatter.7
where the time goes:
time: 1440 us; the launch traced here: 1430 us
  waiting for transfers between devices  1060 us (74%)
  blocking collectives  134 us (9%)
  matrix products  96.4 us (7%)
  other arithmetic  64.1 us (4%)
  local copies, waits for them, and re-layouts  53.3 us (4%)
  between operations  15.6 us (1%)
    reduce_scatter x1, waiting for transfers between devices, local(): lax.psum_scatter(partial_grads[2], ('batch', 'seq'), scatter_dimension=0,...  222 us
    reduce_scatter x1, waiting for transfers between devices, local(): lax.psum_scatter(partial_grads[7], ('batch', 'seq'), scatter_dimension=0,...  213 us
    reduce_scatter x1, waiting for transfers between devices, local(): lax.psum_scatter(partial_grads[1], ('batch', 'seq'), scatter_dimension=0,...  213 us
    reduce_scatter x1, waiting for transfers between devices, local(): lax.psum_scatter(partial_grads[3], ('batch', 'seq'), scatter_dimension=0,...  97.7 us
    unnamed x11, waiting for transfers between devices  93.8 us
    all_gather x2, waiting for transfers between devices, prefix(): everything = jax.tree.map(lambda part: lax.all_gather(part, axis), array)  92.7 us
    all_gather x1, waiting for transfers between devices, local(): lax.all_gather(w_out, ('batch', 'seq'), axis=0, tiled=True)  75.3 us
    all_gather x1, waiting for transfers between devices, local(): lax.all_gather(w_gate_in, ('batch', 'seq'), axis=0, tiled=True)  57.2 us
  transfers between devices with their start and end apart: 12, of which 9 were waited for; matrix products, arithmetic and copies ran while one was open for 8% of the time, Pallas kernels for 0%

commit v1 on v0

--- a/solution.py
+++ b/solution.py
@@ -1,6 +1,11 @@
+import functools
+import typing
+
 import jax
 import jax.numpy as jnp
 from jax import lax
+from jax.experimental import pallas as pl
+from jax.experimental.pallas import tpu as pltpu
 from jax.sharding import PartitionSpec as P
 
 norm_epsilon = 1e-05
@@ -377,9 +382,1086 @@
     )
 
 
+bf16 = jnp.bfloat16
+f32 = jnp.float32
+EXACT = lax.Precision.HIGHEST
+LANES = 128
+
+
+def mm(former, latter, dims=((1,), (0,))):
+    return lax.dot_general(former, latter, (dims, ((), ())), preferred_element_type=f32)
+
+
+def mm_exact(former, latter, dims=((1,), (0,))):
+    return lax.dot_general(
+        former, latter, (dims, ((), ())), precision=EXACT, preferred_element_type=f32
+    )
+
+
+def halves(array):
+    high = array.astype(bf16)
+    return high, (array - high.astype(f32)).astype(bf16)
+
+
+def iota(shape, axis):
+    return lax.broadcasted_iota(jnp.int32, shape, axis)
+
+
+def head_map(own, head_width):
+    return (iota((LANES, own), 0) == iota((LANES, own), 1) // head_width).astype(f32)
+
+
+def triangle_sum(table, array):
+    high, low = halves(array)
+    table = table.astype(bf16)
+    return mm(jnp.concatenate([table, table], axis=1), jnp.concatenate([high, low], axis=0))
+
+
+def twice(array):
+    return jnp.concatenate([array, array], axis=1)
+
+
+def stacked_halves(array):
+    return jnp.concatenate(halves(array), axis=0)
+
+
+def step_tables(raw, rate):
+    span = raw.shape[0]
+    step = jnp.maximum(raw, 0.0) + jnp.log1p(jnp.exp(-jnp.abs(raw)))
+    return step, triangle_sum(iota((span, span), 0) >= iota((span, span), 1), step * rate)
+
+
+def pair_masked(array, head_width):
+    low = iota(array.shape, 1) < head_width
+    zero = jnp.zeros_like(array)
+    return jnp.concatenate([jnp.where(low, array, zero), jnp.where(low, zero, array)], axis=0)
+
+
+def by_pair_lanes(array, pair, head_width):
+    shape = (array.shape[0], 2 * head_width)
+    first = jnp.broadcast_to(array[:, 2 * pair : 2 * pair + 1], shape)
+    second = jnp.broadcast_to(array[:, 2 * pair + 1 : 2 * pair + 2], shape)
+    return jnp.where(iota(shape, 1) < head_width, first, second)
+
+
+def place(i, rank):
+    m = lax.bitwise_xor(i, rank)
+    return 4 * lax.bitwise_and(m, 1) + lax.shift_right_logical(m, 1)
+
+
+def span_at(place_index, rank):
+    m = 2 * lax.bitwise_and(place_index, 3) + lax.shift_right_logical(place_index, 2)
+    return lax.bitwise_xor(m, rank)
+
+
+def project_kernel(
+    where_ref, t0, t1, t2, t3, t4, t5, t6, t7, gain_ref, w0, w1, w2, w3, shared_ref,
+    normed_ref, pre_ref, raw_ref, weight_ref, *, states,
+):
+    step = pl.program_id(0)
+    plane = where_ref[1]
+    span, width = t0.shape
+    own = w0.shape[1]
+    block = width // 4
+
+    @pl.when(step == 0)
+    def _():
+        for o, w in enumerate((w0, w1, w2, w3)):
+            weight_ref[o * block : (o + 1) * block, :own] = w[...]
+        weight_ref[:, own:] = shared_ref[...]
+
+    parts = (t0, t1, t2, t3, t4, t5, t6, t7)
+    for half in range(4):
+
+        @pl.when(step == half)
+        def _(half=half):
+            for i in range(2):
+                part = parts[2 * half + i]
+                tokens = part[...].astype(f32)
+                inv_rms = lax.rsqrt(jnp.mean(tokens * tokens, axis=1, keepdims=True) + norm_epsilon)
+                for o in range(4):
+                    at = pl.multiple_of(lax.bitwise_and(plane - o + 4, 3) * block, LANES)
+                    value = part[:, pl.ds(at, block)].astype(f32) * inv_rms
+                    value = (value * gain_ref[:, pl.ds(at, block)]).astype(bf16)
+                    normed_ref[i * span : (i + 1) * span, o * block : (o + 1) * block] = value
+
+    product = mm(normed_ref[...], weight_ref[...])
+    local = own + 2 * states
+    pre_ref[...] = product[:, :local].astype(bf16)
+    raw_ref[...] = product[:, local:]
+
+
+def forward_kernel(
+    where_ref, pre_ref, raw_ref, taps_ref, heads_ref, rows_ref,
+    mixed_ref, conv_ref, inter_ref, ssm_ref, state_ref,
+    ext, state, *, n_taps, head_width, states,
+):
+    span, own = ssm_ref.shape[1:]
+
+    @pl.when(pl.program_id(0) == 0)
+    def _():
+        ext[0:8, :] = jnp.zeros((8, ext.shape[1]), f32)
+        state[...] = jnp.zeros_like(state)
+
+    ext[8 : 8 + span, :] = pre_ref[0].astype(f32)
+    mixed = taps_ref[n_taps : n_taps + 1, :]
+    for k in range(n_taps):
+        first = 8 - (n_taps - 1) + k
+        mixed = mixed + taps_ref[k : k + 1, :] * ext[first : first + span, :]
+    mixed_ref[0] = mixed
+    ext[0:8, :] = ext[span : span + 8, :]
+    conv = (mixed * jax.nn.sigmoid(mixed)).astype(bf16)
+    conv_ref[0] = conv
+    key, query = conv[:, own : own + states], conv[:, own + states :]
+    step, cum = step_tables(raw_ref[0] + heads_ref[0:1, :], heads_ref[1:2, :])
+    cum_t, step_t = cum.T, step.T
+    affinity = mm(query, key, ((1,), (1,)))
+    causal = iota((span, span), 0) >= iota((span, span), 1)
+    entering = state[...]
+    state_ref[0] = entering
+    base = mm(twice(query), stacked_halves(entering))
+    weighted, kept = [], []
+    for pair in range(own // (2 * head_width)):
+        lanes = slice(2 * pair * head_width, 2 * (pair + 1) * head_width)
+        value = conv_ref[0, :, lanes]
+        mixing = []
+        for h in (2 * pair, 2 * pair + 1):
+            decay = jnp.exp(jnp.where(causal, cum[:, h : h + 1] - cum_t[h : h + 1, :], -1e30))
+            mixing.append((affinity * decay * step_t[h : h + 1, :]).astype(bf16))
+        cum_pair = by_pair_lanes(cum, pair, head_width)
+        growth = jnp.exp(cum_pair)
+        tailed = jnp.exp(cum_pair[span - 1 : span, :] - cum_pair) * by_pair_lanes(step, pair, head_width)
+        inter = growth * base[:, lanes]
+        inter_ref[0, :, lanes] = inter
+        value_f = value.astype(f32)
+        within = mm(jnp.concatenate(mixing, axis=1), pair_masked(value, head_width))
+        ssm_ref[0, :, lanes] = within + inter + rows_ref[1:2, lanes] * value_f
+        weighted.append((tailed * value_f).astype(bf16))
+        kept.append(growth[span - 1 : span, :])
+    weighted, kept = jnp.concatenate(weighted, axis=1), jnp.concatenate(kept, axis=1)
+    state[...] = kept * entering + mm(key, weighted, ((0,), (0,)))
+
+
+def gate_kernel(
+    where_ref, normed_ref, g0, g1, g2, g3, c0, c1, c2, c3, c4, c5, c6, c7, out_ref, rows_ref, ssm_ref,
+    gate_ref, ngate_ref, sums_ref, mine_ref, other_ref, weight_ref, cot_ref,
+):
+    step = pl.program_id(0)
+    block = g0.shape[0]
+    span = c0.shape[0]
+
+    @pl.when(step == 0)
+    def _():
+        for o, w in enumerate((g0, g1, g2, g3)):
+            weight_ref[o * block : (o + 1) * block, :] = w[...]
+
+    parts = (c0, c1, c2, c3, c4, c5, c6, c7)
+    for half in range(4):
+
+        @pl.when(step == half)
+        def _(half=half):
+            for i in range(2):
+                cot_ref[i * span : (i + 1) * span, :] = parts[2 * half + i][...]
+
+    gate = mm(normed_ref[...], weight_ref[...])
+    gate_ref[...] = gate
+    gated = ssm_ref[...] * (gate * jax.nn.sigmoid(gate))
+    gain = rows_ref[0:1, :]
+    ngate = mm(cot_ref[...], out_ref[...], ((1,), (1,))) * gain
+    ngate_ref[...] = ngate
+    squares, cross = gated * gated, ngate * gated
+    for i in range(2):
+        rows = slice(i * span, (i + 1) * span)
+        sums = []
+        for product in (squares[rows], cross[rows]):
+            folded = product[:, :LANES] + product[:, LANES : 2 * LANES] + product[:, 2 * LANES :]
+            sums.append(jnp.sum(folded.T, axis=0, keepdims=True))
+        row = iota((8, LANES), 0)
+        sums_ref[span_at(2 * step + i, where_ref[0])] = jnp.where(row == 0, sums[0], sums[1])
+    part = mm((gated * gain).astype(bf16), out_ref[...]).astype(bf16)
+
+    @pl.when(step < 2)
+    def _():
+        mine_ref[...] = part
+
+    @pl.when(step >= 2)
+    def _():
+        other_ref[...] = part
+
+
+def gate_back_kernel(
+    where_ref, sums_ref, ssm_ref, gate_ref, ngate_ref, rows_ref,
+    grad_ref, grad_gate_ref, projected_ref, lent_ref, *, inner, third,
+):
+    step = pl.program_id(0)
+    rows, own = ssm_ref.shape
+    core = lax.bitwise_and(where_ref[0], 1)
+    lent_ref[...] = jnp.zeros_like(lent_ref)
+    span = LANES
+    for i in range(rows // span):
+        at = slice(i * span, (i + 1) * span)
+        sums = sums_ref[span_at(rows // span * step + i, where_ref[0])]
+        sums = jnp.concatenate([sums, jnp.zeros((LANES - 8, LANES), f32)], axis=0).T
+        inv_gate = lax.rsqrt(sums[:, 0:1] / inner + norm_epsilon)
+        mean = inv_gate * sums[:, 1:2] / inner
+        inv_gate = jnp.broadcast_to(inv_gate, (span, own))
+        ssm, gate = ssm_ref[at], gate_ref[at]
+        logistic = jax.nn.sigmoid(gate)
+        silu = gate * logistic
+        normed = ssm * silu * inv_gate
+        grad_gated = inv_gate * (ngate_ref[at] - normed * mean)
+        grad_ref[at] = grad_gated * silu
+        slope = logistic * (1.0 + gate * (1.0 - logistic))
+        grad_gate_ref[at] = (grad_gated * ssm * slope).astype(bf16)
+        projected_ref[at] = (normed * rows_ref[0:1, :]).astype(bf16)
+    for k in range(2):
+
+        @pl.when(core == k)
+        def _(k=k):
+            for plane, first, _, count in local_slices(k, 2 * third):
+                if count == 4 * third:
+                    source = first + 3 * third if k == 0 else first
+                    to = plane // 2 * third
+                    lent_ref[:, to : to + third] = projected_ref[:, source : source + third]
+
+
+def early_grads_kernel(
+    where_ref, normed_ref, grad_gate_ref, projected_ref, borrowed_ref, c0, c1, c2, c3, c4, c5, c6, c7,
+    b0, b1, b2, b3, cot_ref, rows_ref, total_ref, *, third,
+):
+    step = pl.program_id(0)
+    core, plane = lax.bitwise_and(where_ref[0], 1), where_ref[1]
+    span = c0.shape[0]
+    rows = 3 * third
+    block = normed_ref.shape[1]
+    half = normed_ref.shape[0] // 2
+
+    def swap(to, lent):
+        rows_ref[:half, to] = borrowed_ref[half:, lent]
+        rows_ref[half:, to] = borrowed_ref[:half, lent]
+
+    @pl.when(step == 0)
+    def _():
+        for i, part in enumerate((c0, c1, c2, c3, c4, c5, c6, c7)):
+            cot_ref[i * span : (i + 1) * span, :] = part[...]
+        for k in range(2):
+
+            @pl.when(core == k)
+            def _(k=k):
+                for at_plane, at, _, count in local_slices(k, 2 * third):
+                    to = at_plane * rows
+                    lent = slice(at_plane // 2 * third, (at_plane // 2 + 1) * third)
+                    if count == rows + third:
+                        own_at = at if k == 0 else at + third
+                        rows_ref[:, to : to + rows] = projected_ref[:, own_at : own_at + rows]
+                    elif k == 0:
+                        rows_ref[:, to : to + count] = projected_ref[:, at : at + count]
+                        swap(slice(to + count, to + rows), lent)
+                    else:
+                        rows_ref[:, to + third : to + rows] = projected_ref[:, at : at + count]
+                        swap(slice(to, to + third), lent)
+
+        total_ref[...] = mm(rows_ref[...], cot_ref[...], ((0,), (0,))).astype(bf16)
+
+    gate = mm(normed_ref[...], grad_gate_ref[...], ((0,), (0,))).astype(bf16)
+    first = pl.multiple_of(rows * lax.bitwise_and(plane - step + 4, 3), third)
+    for o, out_ref in enumerate((b0, b1, b2, b3)):
+
+        @pl.when(step == o)
+        def _(out_ref=out_ref):
+            out_ref[:block, :] = gate
+            for g in range(4):
+                own = total_ref[pl.ds(first, rows), g * block : (g + 1) * block]
+                out_ref[block + g * rows : block + (g + 1) * rows, :] = own
+
+
+def backward_kernel(
+    where_ref, grad_ref, inter_ref, state_ref, conv_ref, pre_ref, mixed_ref, raw_ref,
+    taps_ref, heads_ref, rows_ref,
+    grad_pre_ref, grad_taps_ref, grad_heads_ref,
+    ext, grad_state, next_state, *, n_taps, head_width, states,
+):
+    span, own = grad_ref.shape[1:]
+
+    @pl.when(pl.program_id(0) == 0)
+    def _():
+        ext[span : span + 8, :] = jnp.zeros((8, ext.shape[1]), f32)
+        grad_state[...] = jnp.zeros_like(grad_state)
+        next_state[...] = jnp.zeros_like(next_state)
+        grad_taps_ref[...] = jnp.zeros_like(grad_taps_ref)
+        grad_heads_ref[...] = jnp.zeros_like(grad_heads_ref)
+
+    key, query = conv_ref[0, :, own : own + states], conv_ref[0, :, own + states :]
+    rate = heads_ref[1:2, :]
+    raw = raw_ref[0] + heads_ref[0:1, :]
+    step, cum = step_tables(raw, rate)
+    cum_t, step_t = cum.T, step.T
+    tail = jnp.exp(cum[span - 1 : span, :] - cum)
+    affinity = mm(query, key, ((1,), (1,)))
+    causal = iota((span, span), 0) >= iota((span, span), 1)
+    after = grad_state[...]
+    after_halves = stacked_halves(after)
+    grad_weighted = mm(twice(key), after_halves)
+    grad_affinity = jnp.zeros((span, span), f32)
+    direct_t = jnp.zeros((span, span), f32)
+    grad_cum = jnp.zeros((span, LANES), f32)
+    row, lane = iota((span, span), 0), iota((span, LANES), 1)
+    weighted, grown, grown_rest, kept = [], [], [], []
+    products = [[], [], []]
+    mixed = mixed_ref[0]
+    logistic = jax.nn.sigmoid(mixed)
+    slope = logistic * (1.0 + mixed * (1.0 - logistic))
+    for pair in range(own // (2 * head_width)):
+        lanes = slice(2 * pair * head_width, 2 * (pair + 1) * head_width)
+        value, grad_y = conv_ref[0, :, lanes], grad_ref[0, :, lanes]
+        value_f, grad_low = value.astype(f32), grad_y.astype(bf16)
+        cum_pair = by_pair_lanes(cum, pair, head_width)
+        growth = jnp.exp(cum_pair)
+        tailed = jnp.exp(cum_pair[span - 1 : span, :] - cum_pair) * by_pair_lanes(step, pair, head_width)
+        kept.append(growth[span - 1 : span, :])
+        high, low = halves(grad_y * growth)
+        grown.append(high)
+        grown_rest.append(low)
+        weighted.append((tailed * value_f).astype(bf16))
+        grad_mixing = mm(grad_low, pair_masked(value, head_width), ((1,), (1,)))
+        mixing = []
+        for i in (0, 1):
+            h = 2 * pair + i
+            given = grad_mixing[:, i * span : (i + 1) * span]
+            decay = jnp.exp(jnp.where(causal, cum[:, h : h + 1] - cum_t[h : h + 1, :], -1e30))
+            grad_affinity = grad_affinity + given * decay * step_t[h : h + 1, :]
+            table = affinity * decay
+            scores = table * step_t[h : h + 1, :]
+            mixing.append(scores.astype(bf16))
+            direct_t = jnp.where(row == h, jnp.sum(given * table, axis=0, keepdims=True), direct_t)
+            grad_cum = jnp.where(lane == h, jnp.sum(given * scores, axis=1, keepdims=True), grad_cum)
+        grad_value = mm(jnp.concatenate(mixing, axis=0), pair_masked(grad_low, head_width), ((0,), (0,)))
+        by_state = grad_weighted[:, lanes]
+        grad_value = grad_value + tailed * by_state + rows_ref[1:2, lanes] * grad_y
+        ext[0:span, lanes] = grad_value * slope[:, lanes]
+        products[0].append(by_state * value_f)
+        products[1].append(grad_y * inter_ref[0, :, lanes])
+        products[2].append(jnp.sum(grad_y * value_f, axis=0, keepdims=True))
+    weighted, grown = jnp.concatenate(weighted, axis=1), jnp.concatenate(grown, axis=1)
+    grown_rest, kept = jnp.concatenate(grown_rest, axis=1), jnp.concatenate(kept, axis=1)
+    grad_affinity = grad_affinity.astype(bf16)
+    grad_query = mm(grown, state_ref[0].astype(bf16), ((1,), (1,))) + mm(grad_affinity, key)
+    grad_key = mm(weighted, after_halves[:states], ((1,), (1,))) + mm(grad_affinity, query, ((0,), (0,)))
+    ext[0:span, own : own + states] = grad_key * slope[:, own : own + states]
+    ext[0:span, own + states :] = grad_query * slope[:, own + states :]
+    to_lanes = head_map(own, head_width).astype(bf16)
+    last = jnp.sum(after * next_state[...], axis=0, keepdims=True)
+    by_head = jnp.concatenate(
+        [
+            jnp.concatenate(products[0], axis=1),
+            jnp.concatenate(products[1], axis=1),
+            jnp.broadcast_to(jnp.concatenate(products[2], axis=1), (8, own)),
+            jnp.broadcast_to(last, (8, own)),
+        ],
+        axis=0,
+    )
+    high, low = halves(by_head)
+    by_head = mm(high, to_lanes, ((1,), (1,))) + mm(low, to_lanes, ((1,), (1,)))
+    direct = direct_t.T + by_head[:span] * tail
+    grad_cum = grad_cum + by_head[span : 2 * span] - step * direct
+    last = by_head[2 * span + 8 : 2 * span + 9]
+    grad_cum = grad_cum + jnp.where(iota(grad_cum.shape, 0) == span - 1, last, 0.0)
+    grad_log = triangle_sum(iota((span, span), 0) <= iota((span, span), 1), grad_cum)
+    grad_raw = (direct + grad_log * rate) * jax.nn.sigmoid(raw)
+    grad_heads_ref[0:1, :] += jnp.sum(grad_raw, axis=0, keepdims=True)
+    grad_heads_ref[1:2, :] += jnp.sum(grad_log * step, axis=0, keepdims=True) * rate
+    grad_heads_ref[2:3, :] += by_head[2 * span : 2 * span + 1]
+    pre = pre_ref[0].astype(f32)
+    grad_pre = jnp.zeros(pre.shape, f32)
+    for k in range(n_taps):
+        ahead = ext[n_taps - 1 - k : n_taps - 1 - k + span, :]
+        grad_pre = grad_pre + ahead * taps_ref[k : k + 1, :]
+        grad_taps_ref[k : k + 1, :] += jnp.sum(ahead * pre, axis=0, keepdims=True)
+    grad_taps_ref[n_taps : n_taps + 1, :] += jnp.sum(ext[0:span, :], axis=0, keepdims=True)
+    ext[span : span + 8, :] = ext[0:8, :]
+    grad_pre_ref[0, :, : own + 2 * states] = grad_pre.astype(bf16)
+    grad_pre_ref[0, :, own + 2 * states :] = grad_raw.astype(bf16)
+    grad_state[...] = kept * after + mm(
+        jnp.concatenate([query, query], axis=0), jnp.concatenate([grown, grown_rest], axis=0), ((0,), (0,))
+    )
+    next_state[...] = state_ref[0]
+
+
+def input_grad_kernel(gate_ref, rest_ref, w_gate_ref, w_rest_ref, mine_ref, other_ref):
+    half = mine_ref.shape[0]
+    total = mm(gate_ref[...], w_gate_ref[...], ((1,), (1,))) + mm(rest_ref[...], w_rest_ref[...], ((1,), (1,)))
+    mine_ref[...] = total[:half].astype(bf16)
+    other_ref[...] = total[half:].astype(bf16)
+
+
+def input_grad_call(gate, rest, w_gate, w_rest):
+    half, width, block = gate.shape[0] // 2, w_gate.shape[0], w_gate.shape[0] // 3
+    return pl.pallas_call(
+        input_grad_kernel,
+        out_shape=[jax.ShapeDtypeStruct((half, width), bf16)] * 2,
+        grid=(3,),
+        in_specs=[pl.BlockSpec(a.shape, lambda i: (0, 0)) for a in (gate, rest)]
+        + [pl.BlockSpec((block, a.shape[1]), lambda i: (i, 0)) for a in (w_gate, w_rest)],
+        out_specs=[pl.BlockSpec((half, block), lambda i: (0, i))] * 2,
+    )(gate, rest, w_gate, w_rest)
+
+
+def by_span(shape, order):
+    return pl.BlockSpec((1, *shape), lambda i, where: (order(i, where), 0, 0))
+
+
+def spans_call(kernel, where, spans, inputs, outputs, scratch=()):
+    in_specs = [
+        by_span(a.shape[1:], order) if order else pl.BlockSpec(a.shape, lambda i, where, n=a.ndim: (0,) * n)
+        for a, order in inputs
+    ]
+    out_specs = [
+        by_span(shape, order) if order else pl.BlockSpec(shape, lambda i, where, n=len(shape): (0,) * n)
+        for shape, _, order in outputs
+    ]
+    out_shape = [
+        jax.ShapeDtypeStruct(
+            (spans, *shape) if order else shape, dtype
+        )
+        for shape, dtype, order in outputs
+    ]
+    return pl.pallas_call(
+        kernel,
+        out_shape=out_shape,
+        grid_spec=pltpu.PrefetchScalarGridSpec(
+            num_scalar_prefetch=1,
+            grid=(spans,),
+            in_specs=in_specs,
+            out_specs=out_specs,
+            scratch_shapes=list(scratch),
+        ),
+        compiler_params=pltpu.CompilerParams(dimension_semantics=("arbitrary",)),
+    )(where, *[a for a, _ in inputs])
+
+
+def in_time(i, where):
+    return i
+
+
+def in_reverse(i, where):
+    return 7 - i
+
+
+def relative(i, where):
+    return place(i, where[0])
+
+
+def relative_reverse(i, where):
+    return place(7 - i, where[0])
+
+
+class Columns(typing.NamedTuple):
+    shape: tuple
+
+
+def rows_call(kernel, where, steps, rows, inputs, outputs, scratch=()):
+    def spec(shape, index):
+        if isinstance(index, Columns):
+            return pl.BlockSpec(index.shape, lambda i, where: (0, i))
+        if index is None:
+            return pl.BlockSpec(shape, lambda i, where, n=len(shape): (0,) * n)
+        return pl.BlockSpec((rows, *shape[1:]), lambda i, where: (index(i), 0))
+
+    return pl.pallas_call(
+        kernel,
+        out_shape=[jax.ShapeDtypeStruct(shape, dtype) for shape, dtype, _ in outputs],
+        grid_spec=pltpu.PrefetchScalarGridSpec(
+            num_scalar_prefetch=1,
+            grid=(steps,),
+            in_specs=[spec(a.shape, index) for a, index in inputs],
+            out_specs=[spec(shape, index) for shape, _, index in outputs],
+            scratch_shapes=list(scratch),
+        ),
+    )(where, *[a for a, _ in inputs])
+
+
+def each(i):
+    return i
+
+
+def lower(i):
+    return lax.min(i, 1)
+
+
+def upper(i):
+    return lax.max(i - 2, 0)
+
+
+def local_slices(core, width):
+    at, slices = 0, []
+    for plane in range(4):
+        count = 2 * width if plane % 2 == core else width
+        slices.append((plane, at, 0 if core == 0 else 3 * width - count, count))
+        at += count
+    return slices
+
+
+def pack_kernel(
+    gate_ref, conv_ref, step_ref, norm_ref, gain_ref, bias_ref, taps_ref,
+    cols_ref, message_ref, *, head_width,
+):
+    inner = gate_ref.shape[1]
+    group = 3 * head_width
+    for chip in range(4):
+        for core in range(2):
+            for plane, at, start, count in local_slices(core, head_width):
+                source = group * (4 * plane + chip) + start
+                for first, ref in ((0, conv_ref), (cols_ref.shape[2] // 2, gate_ref)):
+                    to = slice(first + at, first + at + count)
+                    cols_ref[2 * chip + core, :, to] = ref[:, source : source + count]
+    rest = conv_ref.shape[1] - inner
+    rows = gate_ref.shape[0]
+    message_ref[...] = jnp.zeros_like(message_ref)
+    message_ref[:rows, :rest] = conv_ref[:, inner:]
+    message_ref[:rows, rest : rest + step_ref.shape[1]] = step_ref[...]
+    vectors = jnp.zeros((8, LANES), f32)
+
+    def put(vectors, ref, at):
+        value = ref[...].astype(f32)
+        value = jnp.pad(value, ((at, 8 - at - value.shape[0]), (0, LANES - value.shape[1])))
+        return vectors + value
+
+    for ref, at in ((norm_ref, 0), (gain_ref, 1), (bias_ref, 2), (taps_ref, 3)):
+        vectors = put(vectors, ref, at)
+    message_ref[rows:, :LANES] = vectors.astype(bf16)
+
+
+def setup_kernel(
+    where_ref, mine_ref, other_ref, heads_ref,
+    shared_ref, norm_ref, taps_ref, channels_ref, head_rows_ref, pick_ref,
+    gain_all, taps_all, held, *, n_taps, head_width,
+):
+    rank, plane = where_ref[0], where_ref[1]
+    padded = shared_ref.shape[1]
+    rows = norm_ref.shape[1] // 32
+    block = 8 * rows
+    rows_in, rows_out = norm_ref.shape[1] // 32, gain_all.shape[1] // 32
+    piece = taps_all.shape[1] // 32
+    inner = gain_all.shape[1]
+    own = channels_ref.shape[1]
+    for p in range(8):
+        source = lax.bitwise_xor(rank, 2 * (p % 4) + p // 4)
+        part_ref, top = (mine_ref, other_ref)[p // 4], p % 4 * (rows + 8)
+        for o in range(4):
+            at = pl.multiple_of(o * block + source * rows, 16)
+            lanes = slice(o * padded, (o + 1) * padded)
+            shared_ref[pl.ds(at, rows), :] = part_ref[top : top + rows, lanes]
+            device = 8 * lax.bitwise_and(plane - o + 4, 3) + source
+            held[device] = part_ref[top + rows : top + rows + 8, o * padded : o * padded + LANES].astype(f32)
+    for i in range(32):
+        vectors = held[i]
+        norm_ref[:, i * rows_in : (i + 1) * rows_in] = vectors[0:1, :rows_in]
+        gain_all[:, i * rows_out : (i + 1) * rows_out] = vectors[1:2, :rows_out]
+        taps_all[:, i * piece : (i + 1) * piece] = vectors[:, :piece]
+    taps_ref[...] = jnp.zeros_like(taps_ref)
+    channels_ref[...] = jnp.zeros_like(channels_ref)
+    taps_ref[0:n_taps, own:] = taps_all[3 : 3 + n_taps, inner:]
+    taps_ref[n_taps : n_taps + 1, own:] = taps_all[2:3, inner:]
+    for r in range(8):
+
+        @pl.when(rank == r)
+        def _(r=r):
+            chip, core = r // 2, r % 2
+            local, heads = iota((LANES, LANES), 0), iota((LANES, LANES), 1)
+            chosen = jnp.zeros((LANES, LANES), jnp.bool_)
+            for plane, at, start, count in local_slices(core, head_width):
+                source = 3 * head_width * (4 * plane + chip) + start
+                taps_ref[0:n_taps, at : at + count] = taps_all[3 : 3 + n_taps, source : source + count]
+                taps_ref[n_taps : n_taps + 1, at : at + count] = taps_all[2:3, source : source + count]
+                channels_ref[0:1, at : at + count] = gain_all[:, source : source + count]
+                for j in range(count // head_width):
+                    chosen |= (local == at // head_width + j) & (heads == source // head_width + j)
+            pick_ref[...] = chosen.astype(f32)
+
+    states = (padded - LANES) // 2
+    chosen = pick_ref[...].astype(bf16)
+    shared_ref[:, 2 * states :] = mm(shared_ref[:, 2 * states :], chosen, ((1,), (1,))).astype(bf16)
+    head_rows = mm_exact(heads_ref[...], pick_ref[...], ((1,), (1,)))
+    used = iota((1, LANES), 1) < own // head_width
+    head_rows_ref[...] = jnp.zeros_like(head_rows_ref)
+    head_rows_ref[0:1, :] = head_rows[0:1]
+    head_rows_ref[1:2, :] = jnp.where(used, -jnp.exp(head_rows[1:2]), 0.0)
+    channels_ref[1:2, :] = mm_exact(head_rows, head_map(own, head_width))[2:3]
+
+
+def out_rows_kernel(where_ref, p0, p1, p2, p3, borrowed_ref, out_ref):
+    rank, plane = where_ref[0], where_ref[1]
+    core = lax.bitwise_and(rank, 1)
+    rows = p0.shape[0]
+    third = rows // 3
+    for o, part in enumerate((p0, p1, p2, p3)):
+        at_plane = lax.bitwise_and(plane - o + 4, 3)
+        for k in range(2):
+            for slices_plane, at, _, count in local_slices(k, 2 * third):
+
+                @pl.when((core == k) & (at_plane == slices_plane))
+                def _(o=o, part=part, k=k, at=at, count=count):
+                    if count == rows + third and k == 0:
+                        out_ref[at : at + rows, :] = part[...]
+                        out_ref[at + rows : at + count, :] = borrowed_ref[o // 2]
+                    elif count == rows + third:
+                        out_ref[at : at + third, :] = borrowed_ref[o // 2]
+                        out_ref[at + third : at + count, :] = part[...]
+                    elif k == 0:
+                        out_ref[at : at + count, :] = part[: 2 * third, :]
+                    else:
+                        out_ref[at : at + count, :] = part[third:, :]
+
+
+def lend_kernel(where_ref, p0, p1, p2, p3, out_ref):
+    core, plane = lax.bitwise_and(where_ref[0], 1), where_ref[1]
+    third = out_ref.shape[1]
+    odd = lax.bitwise_and(plane + 1 + core, 1)
+    for o, part in enumerate((p0, p1, p2, p3)):
+        for k in range(2):
+
+            @pl.when((odd == o % 2) & (core == k))
+            def _(o=o, part=part, k=k):
+                out_ref[o // 2] = part[2 * third :, :] if k == 0 else part[:third, :]
+
+
+def total_of(refs, rows=slice(None)):
+    total = refs[0][rows].astype(f32)
+    for ref in refs[1:]:
+        total = total + ref[rows].astype(f32)
+    return total
+
+
+def as_row(column, count):
+    return jnp.broadcast_to(column, (column.shape[0], LANES)).T[:1, :count]
+
+
+def early_rows_kernel(p0, p1, p2, w_ref, gain_ref, gate_ref, out_ref, dot_ref):
+    block = gate_ref.shape[0]
+    rows = out_ref.shape[0]
+    gate_ref[...] = total_of((p0, p1, p2), slice(0, block)).astype(bf16)
+    for g in range(4):
+        at = block + g * rows
+        out_ref[:, g * block : (g + 1) * block] = total_of((p0, p1, p2), slice(at, at + rows))
+    dot = jnp.sum(w_ref[...].astype(f32) * out_ref[...], axis=1, keepdims=True)
+    dot_ref[...] = as_row(dot, rows) / gain_ref[...].astype(f32)
+
+
+def late_rows_kernel(gate_ref, c0, c1, c2, c3, out_ref):
+    own = gate_ref.shape[1]
+    rows = out_ref.shape[1]
+    for r in range(8):
+        at = slice(r * rows, (r + 1) * rows)
+        out_ref[r, :, :own] = gate_ref[at, :]
+        out_ref[r, :, own:] = total_of((c0, c1, c2, c3), at).astype(bf16)
+
+
+def columns_kernel(
+    table_ref, w_gate_ref, w_conv_ref, w_step_ref, gain_ref, s0, s1, s2, s3,
+    gate_ref, conv_ref, dot_ref, step_ref, taps_ref, bias_ref, step_bias_ref, decay_ref, skip_ref, *, head_width,
+):
+    group = 3 * head_width
+    inner = 16 * group
+    half = table_ref.shape[2] // 2
+    for chip in range(4):
+        for core in range(2):
+            for plane, at, start, count in local_slices(core, head_width):
+                to = slice(group * (4 * plane + chip) + start, group * (4 * plane + chip) + start + count)
+                gate_ref[:, to] = table_ref[2 * chip + core, :, at : at + count].astype(f32)
+                conv_ref[:, to] = table_ref[2 * chip + core, :, half + at : half + at + count].astype(f32)
+    rows = gate_ref.shape[0]
+    rest = conv_ref.shape[1] - inner
+    shared = total_of((s0, s1, s2, s3))
+    conv_ref[:, inner:] = shared[:rows, :rest]
+    step_ref[...] = shared[:rows, rest : rest + step_ref.shape[1]]
+    small = shared[rows:, :LANES] + shared[rows:, LANES : 2 * LANES]
+    at = 0
+    for ref in (taps_ref, bias_ref, step_bias_ref, decay_ref, skip_ref):
+        ref[...] = small[at : at + ref.shape[0], : ref.shape[1]]
+        at += ref.shape[0]
+    total = jnp.sum(w_step_ref[...].astype(f32) * step_ref[...], axis=1, keepdims=True)
+    for weight_ref, grad_ref in ((w_gate_ref, gate_ref), (w_conv_ref, conv_ref)):
+        total = total + jnp.sum(weight_ref[...].astype(f32) * grad_ref[...], axis=1, keepdims=True)
+    dot_ref[...] = as_row(total, rows) / gain_ref[...].astype(f32)
+
+
+def tokens_out_kernel(
+    where_ref, o0, o1, o2, o3, g0, g1, g2, g3, hidden_ref, cot_ref, sums_ref, norm_ref,
+    output_ref, grad_ref, held, *, inner,
+):
+    rank, plane = where_ref[0], where_ref[1]
+    tokens = hidden_ref[...].astype(f32)
+    sums = jnp.concatenate([sums_ref[rank], jnp.zeros((LANES - 8, LANES), f32)], axis=0).T
+    inv_gate = lax.rsqrt(sums[:, 0:1] / inner + norm_epsilon)
+    output_ref[...] = (tokens + inv_gate * total_of((o0, o1, o2, o3))).astype(bf16)
+    inv_rms = lax.rsqrt(jnp.mean(tokens * tokens, axis=1, keepdims=True) + norm_epsilon)
+    width = tokens.shape[1]
+    block = width // 4
+    grad_ref[...] = total_of((g0, g1, g2, g3))
+    for p in range(4):
+        at = pl.multiple_of(block * lax.bitwise_and(plane - p + 4, 3), LANES)
+        lanes = slice(p * block, (p + 1) * block)
+        held[:, lanes] = grad_ref[:, pl.ds(at, block)] * norm_ref[:, lanes]
+    grad_unit, unit = held[...], tokens * inv_rms
+    mean = jnp.mean(grad_unit * unit, axis=1, keepdims=True)
+    grad_ref[...] = cot_ref[...].astype(f32) + inv_rms * (grad_unit - unit * mean)
+
+
+def once(kernel, inputs, outputs, where=None, scratch=()):
+    specs = lambda shapes: [pl.BlockSpec(s, lambda *_, n=len(s): (0,) * n) for s in shapes]
+    out_shape = [jax.ShapeDtypeStruct(shape, dtype) for shape, dtype in outputs]
+    grid_spec = pltpu.PrefetchScalarGridSpec(
+        num_scalar_prefetch=0 if where is None else 1,
+        grid=(1,),
+        in_specs=specs([a.shape for a in inputs]),
+        out_specs=specs([shape for shape, _ in outputs]),
+        scratch_shapes=list(scratch),
+    )
+    call = pl.pallas_call(kernel, out_shape=out_shape, grid_spec=grid_spec)
+    return call(*([] if where is None else [where]), *inputs)
+
+
+def hop(value, distance):
+    count = lax.axis_size("seq")
+    pairs = [(i, i ^ distance) for i in range(count)]
+    return lax.ppermute(value, "seq", pairs)
+
+
+def plane_hop(value, distance):
+    count = lax.axis_size("batch")
+    pairs = [(i, (i + distance) % count) for i in range(count)]
+    return lax.ppermute(value, "batch", pairs)
+
+
+def planes_gather(value, direct=False):
+    one, three = plane_hop(value, 1), plane_hop(value, -1)
+    two = plane_hop(value, 2) if direct else plane_hop(one, 1)
+    return [value, one, two, three]
+
+
+def planes_parts(blocks):
+    near, far = plane_hop(blocks[1], -1), plane_hop(blocks[2], 1)
+    sent = (blocks[3].astype(f32) + far.astype(f32)).astype(blocks[3].dtype)
+    return [blocks[0], near, plane_hop(sent, 1)]
+
+
+def planes_direct(blocks):
+    return [blocks[0]] + [plane_hop(blocks[o], -o) for o in (1, 2, 3)]
+
+
+def plane_gather(value):
+    chips = [value] + [hop(value, distance) for distance in (2, 4, 6)]
+    return chips + [hop(part, 1) for part in chips]
+
+
+def small_gather(value):
+    mine = jnp.concatenate([value] + [hop(value, distance) for distance in (2, 4, 6)])
+    return mine, hop(mine, 1)
+
+
+def plane_parts(mine, other):
+    count = mine.shape[0] // 4
+    other = hop(other, 1)
+    half = []
+    for j in range(4):
+        rows = slice(j * count, (j + 1) * count)
+        half.append((mine[rows].astype(f32) + other[rows].astype(f32)).astype(bf16))
+    return half[:1] + [hop(half[j], 2 * j) for j in (1, 2, 3)]
+
+
+def plane_total(value):
+    value = value + hop(value, 1)
+    return value + hop(value, 2) + hop(value, 4) + hop(value, 6)
+
+
+def local_group(index, core, width):
+    plane, at = jnp.zeros_like(index), jnp.zeros_like(index)
+    for k in range(2):
+        for slices_plane, first, start, count in local_slices(k, width):
+            inside = (core == k) & (index >= first) & (index < first + count)
+            plane = jnp.where(inside, slices_plane, plane)
+            at = jnp.where(inside, index - first + start, at)
+    return plane, at
+
+
+def shared_back_kernel(where_ref, rows_ref, taps_ref, heads_ref, pick_ref, out_ref, *, head_width, piece, first_lane):
+    rank, plane = where_ref[0], where_ref[1]
+    rows = out_ref.shape[2] - 8
+    local = taps_ref.shape[1]
+    own = 6 * head_width
+    inner = 8 * own
+    core, chip = lax.bitwise_and(rank, 1), lax.shift_right_logical(rank, 1)
+    at = iota((local, LANES), 0)
+    at_plane, offset = local_group(at, core, head_width)
+    column = jnp.where(at < own, 3 * head_width * (4 * at_plane + chip) + offset, inner + at - own)
+    heads = mm_exact(heads_ref[...], pick_ref[...])
+    heads = jnp.concatenate([jnp.zeros((5, LANES), f32), heads[:3]], axis=0)
+    high, low = halves(taps_ref[...])
+    both = jnp.concatenate([high, low], axis=0)
+    target = LANES * (column // piece) + column % piece - iota((local, LANES), 1)
+    head_halves = halves(heads)
+    for o in range(4):
+        first = 8 * lax.bitwise_and(plane - o + 4, 3)
+        for r in range(8):
+            chosen = (target == LANES * (first + r)).astype(bf16)
+            spread = mm(both, chosen)
+            place_at = place(r, rank)
+            own_rows = slice((8 * o + r) * rows, (8 * o + r + 1) * rows)
+            out_ref[place_at, o, :rows, : 2 * LANES] = rows_ref[own_rows, first_lane : first_lane + 2 * LANES]
+            steps = mm(rows_ref[own_rows, first_lane + 2 * LANES :], pick_ref[...].astype(bf16))
+            out_ref[place_at, o, :rows, 2 * LANES :] = steps.astype(bf16)
+            for half in (0, 1):
+                value = spread[8 * half : 8 * half + 8].astype(bf16) + head_halves[half]
+                out_ref[place_at, o, rows:, half * LANES : (half + 1) * LANES] = value
+            out_ref[place_at, o, rows:, 2 * LANES :] = jnp.zeros((8, out_ref.shape[3] - 2 * LANES), bf16)
+
+
+def split_local(
+    hidden,
+    norm_gain,
+    w_gate_in,
+    w_conv_in,
+    w_step,
+    conv_weight,
+    conv_bias,
+    step_bias,
+    decay_log,
+    skip_gain,
+    gate_gain,
+    w_out,
+    cotangent,
+):
+    plane, rank = lax.axis_index("batch"), lax.axis_index("seq")
+    planes, ranks = lax.axis_size("batch"), lax.axis_size("seq")
+    _, span, width = hidden.shape
+    rows_in, inner = w_gate_in.shape
+    channels = w_conv_in.shape[1]
+    heads = w_step.shape[1]
+    head_width = inner // heads
+    states = (channels - inner) // 2
+    taps = conv_weight.shape[0]
+    own = inner // ranks
+    rows_out = w_out.shape[0]
+    tokens = ranks * span
+    block = width // planes
+    piece = conv_bias.shape[0]
+    devices = planes * ranks
+    padded = -(-(2 * states + heads) // LANES) * LANES
+    local = own + 2 * states
+    third = rows_out // 3
+    fixed = None
+    where = jnp.stack([rank, plane]).astype(jnp.int32)
+
+    out_parts = planes_gather(w_out)
+    cols, message = once(
+        functools.partial(pack_kernel, head_width=head_width),
+        [w_gate_in, w_conv_in, w_step, norm_gain[None], gate_gain[None], conv_bias[None], conv_weight],
+        [((ranks, rows_in, 2 * own), bf16), ((rows_in + 8, padded), bf16)],
+    )
+    cols = lax.all_to_all(cols, "seq", 0, 0).reshape(ranks * rows_in, 2 * own)
+    message = jnp.concatenate(planes_gather(message, True), axis=1)
+    tokens_rel, cot_rel = plane_gather(hidden[0]), plane_gather(cotangent[0])
+    shared_mine, shared_other = small_gather(message)
+    conv_w, gate_w = planes_gather(cols[:, :own]), planes_gather(cols[:, own:], True)
+    head_values = jnp.pad(jnp.stack([step_bias, decay_log, skip_gain]), ((0, 5), (0, LANES - heads)))
+    shared_w, norm_full, taps_rows, channel_rows, head_rows, head_table = rows_call(
+        functools.partial(setup_kernel, n_taps=taps, head_width=head_width),
+        where,
+        1,
+        None,
+        [(a, fixed) for a in (shared_mine, shared_other, head_values)],
+        [
+            ((width, padded), bf16, fixed),
+            ((1, width), f32, fixed),
+            ((8, local), f32, fixed),
+            ((8, own), f32, fixed),
+            ((8, LANES), f32, fixed),
+            ((LANES, LANES), f32, fixed),
+        ],
+        [
+            pltpu.VMEM((1, inner), f32),
+            pltpu.VMEM((8, channels), f32),
+            pltpu.VMEM((devices, 8, LANES), f32),
+        ],
+    )
+    (lent_rows,) = once(lend_kernel, out_parts, [((2, third, width), bf16)], where)
+    borrowed = hop(lent_rows, 1)
+    (out_w,) = once(out_rows_kernel, [*out_parts, borrowed], [((own, width), bf16)], where)
+
+    sizes = dict(n_taps=taps, head_width=head_width, states=states)
+    rows = tokens // 4
+    norm_full, out_w = lax.optimization_barrier((norm_full, out_w))
+    normed, pre, raw, rest_w = rows_call(
+        functools.partial(project_kernel, states=states),
+        where,
+        4,
+        rows,
+        [(a, fixed) for a in (*tokens_rel, norm_full, *conv_w, shared_w)],
+        [
+            ((tokens, width), bf16, each),
+            ((tokens, local), bf16, each),
+            ((tokens, LANES), f32, each),
+            ((width, own + padded), bf16, fixed),
+        ],
+    )
+    pre, raw = pre.reshape(ranks, span, local), raw.reshape(ranks, span, LANES)
+    mixed, conv, inter, ssm, entering = spans_call(
+        functools.partial(forward_kernel, **sizes),
+        where,
+        ranks,
+        [(pre, relative), (raw, relative)]
+        + [(a, fixed) for a in (taps_rows, head_rows, channel_rows)],
+        [
+            ((span, local), f32, in_time),
+            ((span, local), bf16, in_time),
+            ((span, own), f32, in_time),
+            ((span, own), f32, relative),
+            ((states, own), f32, in_time),
+        ],
+        [pltpu.VMEM((span + 8, local), f32), pltpu.VMEM((states, own), f32)],
+    )
+    ssm = ssm.reshape(tokens, own)
+    gate, ngate, sums, part_mine, part_other, gate_all = rows_call(
+        gate_kernel,
+        where,
+        4,
+        rows,
+        [(normed, each)]
+        + [(a, fixed) for a in (*gate_w, *cot_rel, out_w, channel_rows)]
+        + [(ssm, each)],
+        [
+            ((tokens, own), f32, each),
+            ((tokens, own), f32, each),
+            ((ranks, 8, LANES), f32, fixed),
+            ((tokens // 2, width), bf16, lower),
+            ((tokens // 2, width), bf16, upper),
+            ((width, own), bf16, fixed),
+        ],
+        [pltpu.VMEM((rows, width), bf16)],
+    )
+    sums = plane_total(sums)
+    out_own = plane_parts(part_mine, part_other)
+
+    grad_y, grad_gate, projected, lent = rows_call(
+        functools.partial(gate_back_kernel, inner=inner, third=third),
+        where,
+        4,
+        rows,
+        [(sums, fixed), (ssm, each), (gate, each), (ngate, each), (channel_rows, fixed)],
+        [
+            ((tokens, own), f32, each),
+            ((tokens, own), bf16, each),
+            ((tokens, own), bf16, each),
+            ((tokens, LANES), bf16, each),
+        ],
+    )
+    borrowed = hop(lent, 1)
+    early = rows_call(
+        functools.partial(early_grads_kernel, third=third),
+        where,
+        4,
+        None,
+        [(normed, Columns((tokens, block)))]
+        + [(a, fixed) for a in (grad_gate, projected, borrowed, *cot_rel)],
+        [((block + 4 * rows_out, block), bf16, fixed)] * 4,
+        [
+            pltpu.VMEM((tokens, width), bf16),
+            pltpu.VMEM((tokens, own), bf16),
+            pltpu.VMEM((own, width), bf16),
+        ],
+    )
+    early = planes_parts(early)
+    grad_rest, grad_taps, grad_heads = spans_call(
+        functools.partial(backward_kernel, **sizes),
+        where,
+        ranks,
+        [(grad_y.reshape(ranks, span, own), relative_reverse)]
+        + [(a, in_reverse) for a in (inter, entering, conv)]
+        + [(pre, relative_reverse), (mixed, in_reverse), (raw, relative_reverse)]
+        + [(a, fixed) for a in (taps_rows, head_rows, channel_rows)],
+        [
+            ((span, own + padded), bf16, relative_reverse),
+            ((8, local), f32, fixed),
+            ((8, LANES), f32, fixed),
+        ],
+        [
+            pltpu.VMEM((span + 8, local), f32),
+            pltpu.VMEM((states, own), f32),
+            pltpu.VMEM((states, own), f32),
+        ],
+    )
+    grad_rest = grad_rest.reshape(tokens, own + padded)
+    d_rest = jnp.dot(normed.T, grad_rest, preferred_element_type=f32).astype(bf16)
+    d_conv = planes_direct([d_rest[o * block : (o + 1) * block, :own] for o in range(planes)])
+    (d_shared,) = once(
+        functools.partial(shared_back_kernel, head_width=head_width, piece=piece, first_lane=own),
+        [d_rest, grad_taps, grad_heads, head_table],
+        [((ranks, planes, rows_in + 8, padded), bf16)],
+        where,
+    )
+    gate_all, d_shared = lax.optimization_barrier((gate_all, d_shared))
+    mine, other = input_grad_call(grad_gate, grad_rest, gate_all, rest_w)
+    grad_own = plane_parts(mine, other)
+    d_shared = d_shared.reshape(2, ranks // 2 * planes, rows_in + 8, padded)
+    d_shared = plane_parts(d_shared[0], d_shared[1])
+    d_shared = sum(part.astype(f32) for part in d_shared)
+    d_shared = planes_direct([d_shared[o] for o in range(planes)])
+
+    d_gate, d_out, d_gain = once(
+        early_rows_kernel,
+        [*early, w_out, gate_gain[None]],
+        [((block, own), bf16), ((rows_out, width), f32), ((1, rows_out), f32)],
+    )
+    (d_in,) = once(late_rows_kernel, [d_gate, *d_conv], [((ranks, rows_in, 2 * own), bf16)])
+    d_in = lax.all_to_all(d_in, "seq", 0, 0)
+    output, grad_hidden = once(
+        functools.partial(tokens_out_kernel, inner=inner),
+        [*out_own, *grad_own, hidden[0], cotangent[0], sums, norm_full],
+        [((span, width), bf16), ((span, width), f32)],
+        where,
+        [pltpu.VMEM((span, width), f32)],
+    )
+    d_gate, d_conv, d_norm, d_step, *small = once(
+        functools.partial(columns_kernel, head_width=head_width),
+        [d_in, w_gate_in, w_conv_in, w_step, norm_gain[None], *d_shared],
+        [
+            ((rows_in, inner), f32),
+            ((rows_in, channels), f32),
+            ((1, rows_in), f32),
+            ((rows_in, heads), f32),
+            ((taps, piece), f32),
+            ((1, piece), f32),
+            ((1, heads), f32),
+            ((1, heads), f32),
+            ((1, heads), f32),
+        ],
+    )
+    return (
+        output[None],
+        grad_hidden[None],
+        d_norm[0],
+        d_gate,
+        d_conv,
+        d_step,
+        small[0],
+        small[1][0],
+        small[2][0],
+        small[3][0],
+        small[4][0],
+        d_gain[0],
+        d_out,
+    )
+
+
+def split_block(*args):
+    return split_local(*args)
+
+
 def solution(mesh):
+    split = (mesh.shape["batch"], mesh.shape["seq"]) == (4, 8)
+    body = split_block if split else local
     return jax.shard_map(
-        local,
+        body,
         mesh=mesh,
         in_specs=(
             P("batch", "seq", None),

time: 1440 us -> 314 us (0.22)
  waiting for transfers between devices: 1060 us -> 106 us
  blocking collectives: 134 us -> 0 us
  Pallas kernels: 0 us -> 103 us
  matrix products: 96.4 us -> 5.36 us
  starting transfers between devices: 4.28 us -> 76.3 us
  other arithmetic: 64.1 us -> 10.8 us
  local copies, waits for them, and re-layouts: 53.3 us -> 10 us
  between operations: 15.6 us -> 1.09 us
    reduce_scatter x4 -> x0, waiting for transfers between devices: 746 us -> none  [the longest x1 222 us: local(): lax.psum_scatter(partial_grads[2], ('batch', 'seq'), scatter_dimension=0,...]
    all_gather x5 -> x0, waiting for transfers between devices: 225 us -> none  [the longest x2 92.7 us: prefix(): everything = jax.tree.map(lambda part: lax.all_gather(part, axis), array)]
    ppermute x2 -> x57, waiting for transfers between devices: 0.01 us -> 106 us  [the longest x36 56.4 us: hop(): return lax.ppermute(value, 'seq', pairs)]
    pallas_call x0 -> x16, Pallas kernels: none -> 103 us  [the longest x5 42.9 us: rows_call(): pl.pallas_call(kernel, out_shape=[jax.ShapeDtypeStruct(shape, dtype) for...]
    unnamed x11 -> x0, waiting for transfers between devices: 93.8 us -> none
    dot_general x26 -> x1, matrix products: 96.4 us -> 5.36 us  [split_local(): jnp.dot(normed.T, grad_rest, preferred_element_type=f32).astype(bf16)]
    all_gather x3 -> x0, blocking collectives: 90.9 us -> none  [the longest x1 42.3 us: local(): lax.all_gather(conv_weight, ('batch', 'seq'), axis=1, tiled=True)]
    ppermute x2 -> x57, starting transfers between devices: 3.66 us -> 69.3 us  [the longest x21 38.2 us: plane_hop(): return lax.ppermute(value, 'batch', pairs)]
  transfers between devices with their start and end apart: 12 -> 59, of which waited for: 9 -> 26; matrix products, arithmetic and copies ran while one was open for 8% -> 6% of each run, Pallas kernels for 0% -> 22%
where the time goes in v1:
time: 314 us; the launch traced here: 312 us
  waiting for transfers between devices  106 us (34%)
  Pallas kernels  103 us (33%)
  starting transfers between devices  76.3 us (24%)
  other arithmetic  10.8 us (3%)
  local copies, waits for them, and re-layouts  10 us (3%)
  matrix products  5.36 us (2%)
    ppermute x36, waiting for transfers between devices, hop(): return lax.ppermute(value, 'seq', pairs)  56.4 us
    ppermute x21, waiting for transfers between devices, plane_hop(): return lax.ppermute(value, 'batch', pairs)  49.2 us
    pallas_call x5, Pallas kernels, rows_call(): pl.pallas_call(kernel, out_shape=[jax.ShapeDtypeStruct(shape, dtype) for...  42.9 us
    ppermute x21, starting transfers between devices, plane_hop(): return lax.ppermute(value, 'batch', pairs)  38.2 us
    ppermute x36, starting transfers between devices, hop(): return lax.ppermute(value, 'seq', pairs)  31.1 us
    pallas_call x2, Pallas kernels, spans_call(): pl.pallas_call(kernel, out_shape=out_shape, grid_spec=pltpu.PrefetchScala...  27.2 us
    pallas_call x8, Pallas kernels, once(): return call(*([] if where is None else [where]), *inputs)  25.4 us
    pallas_call x1, Pallas kernels, input_grad_call(): pl.pallas_call(input_grad_kernel, out_shape=[jax.ShapeDtypeStruct((half,...  7.84 us
  transfers between devices with their start and end apart: 59, of which 26 were waited for; matrix products, arithmetic and copies ran while one was open for 6% of the time, Pallas kernels for 22%

profile of v1, /device:TPU:0, one launch (start us, length us, event | category | flops | bytes accessed | tf_op | source)
XLA Modules:
  0.0 312.5 jit_solution(8081725339857839643)
XLA Ops:
  16.7 3.5 %collective-permute-start.16 = (bf16[96,1536]{1,0:T(8,128)(2,1)}, bf16[96,1536]{1,0:T(8,128)(2,1)S(1)}, u32[]{:S(2)}, u32[]{:S(2)}) collective-permute-start(bf16[96,1536]{1,0:T(8,128)(2,1)} %w_ref.1), channel_id=1, source_target_pairs={{0,24},{8,0},{16,8},{24,16},{1,25},{9,1},{17,9},{25,17},{2,26},{10... | collective-permute-start | bytes 884744 | tf_op jit(solution)/shard_map/ppermute | solution.py:1133
  25.3 3.1 collective-permute-done.14.p1
  32.9 3.5 %all-to-all-start = ((bf16[8,48,768]{2,1,0:T(8,128)(2,1)}), bf16[8,48,768]{2,1,0:T(8,128)(2,1)S(1)}, u32[]{:S(2)}, u32[]{:S(2)}) async-start(bf16[8,48,768]{2,1,0:T(8,128)(2,1)} %get-tuple-element.70), calls=%async_computation | async-start | bytes 1179648 | tf_op jit(solution)/shard_map/all_to_all | solution.py:1261
  38.5 3.3 %collective-permute-done.1.t2 = bf16[128,1536]{1,0:T(8,128)(2,1)} collective-permute-done((bf16[128,1536]{1,0:T(8,128)(2,1)}, bf16[128,1536]{1,0:T(8,128)(2,1)}, u32[]{:S(2)}, u32[]{:S(2)}) %collective-permute-start.1) | collective-permute-done | bytes 393248 | tf_op jit(solution)/shard_map/ppermute | solution.py:1127
  46.2 3.8 %collective-permute-done.24.c1 = bf16[128,1536]{1,0:T(8,128)(2,1)S(1)} collective-permute-done((bf16[128,1536]{1,0:T(8,128)(2,1)}, bf16[128,1536]{1,0:T(8,128)(2,1)S(1)}, u32[]{:S(2)}, u32[]{:S(2)}) %collective-permute-start.24) | collective-permute-done | bytes 393248 | tf_op jit(solution)/shard_map/ppermute | solution.py:1127
  51.4 13.2 %collective-permute-done.25.c2 = bf16[128,1536]{1,0:T(8,128)(2,1)S(1)} collective-permute-done((bf16[128,1536]{1,0:T(8,128)(2,1)S(1)}, bf16[128,1536]{1,0:T(8,128)(2,1)S(1)}, u32[]{:S(2)}, u32[]{:S(2)}) %collective-permute-start.25) | collective-permute-done | bytes 393248 | tf_op jit(solution)/shard_map/ppermute | solution.py:1127
  73.2 4.7 %collective-permute-done.18.w1 = bf16[384,384]{1,0:T(8,128)(2,1)} collective-permute-done((bf16[384,384]{1,0:T(8,128)(2,1)}, bf16[384,384]{1,0:T(8,128)(2,1)}, u32[]{:S(2)}, u32[]{:S(2)}) %collective-permute-start.18) | collective-permute-done | bytes 294944 | tf_op jit(solution)/shard_map/ppermute | solution.py:1133
  78.6 5.6 %collective-permute-done.20.w3 = bf16[384,384]{1,0:T(8,128)(2,1)S(1)} collective-permute-done((bf16[384,384]{1,0:T(8,128)(2,1)}, bf16[384,384]{1,0:T(8,128)(2,1)S(1)}, u32[]{:S(2)}, u32[]{:S(2)}) %collective-permute-start.20) | collective-permute-done | bytes 294944 | tf_op jit(solution)/shard_map/ppermute | solution.py:1133
  86.7 4.0 %collective-permute-done.19.w2 = bf16[384,384]{1,0:T(8,128)(2,1)S(1)} collective-permute-done((bf16[384,384]{1,0:T(8,128)(2,1)}, bf16[384,384]{1,0:T(8,128)(2,1)S(1)}, u32[]{:S(2)}, u32[]{:S(2)}) %collective-permute-start.19) | collective-permute-done | bytes 294944 | tf_op jit(solution)/shard_map/ppermute | solution.py:1133
  93.2 3.2 %shard_map.231.out_ref = bf16[384,1536]{1,0:T(8,128)(2,1)} custom-call(s32[2]{0:T(128)} %pad_add_fusion.where_ref, bf16[96,1536]{1,0:T(8,128)(2,1)} %w_ref.1, bf16[96,1536]{1,0:T(8,128)(2,1)} %collective-permute-done.14.p1, bf16[96,1536]{1,0:T(8,128)(2,1)} %collective-permute-done.15.p2, bf16[96,1536]{1,0:T(8,128)(2,1)} %copy-done.16, ...), custom_call_target="tpu_custom_call" | custom-call | tf_op jit(solution)/shard_map/pallas_call | solution.py:1121
  96.5 3.9 %shard_map.229 = (bf16[1536,384]{1,0:T(8,128)(2,1)}, f32[1,1536]{1,0:T(1,128)}, f32[8,640]{1,0:T(8,128)}, f32[8,384]{1,0:T(8,128)}, f32[8,128]{1,0:T(8,128)}, /*index=5*/f32[128,128]{1,0:T(8,128)}) custom-call(s32[2]{0:T(128)} %pad_add_fusion.where_ref, bf16[224,1536]{1,0:T(8,128)(2,1)} %copy-done.4, bf16[224,1536]{1,0:T(8,128)(2,1)} %collective-permute-done.13.other_ref, ...), custom_call_target="tpu_custom_call" | custom-call | tf_op jit(solution)/shard_map/pallas_call | solution.py:870
  100.4 9.9 %shard_map.232 = (bf16[1024,1536]{1,0:T(8,128)(2,1)}, bf16[1024,640]{1,0:T(8,128)(2,1)}, f32[1024,128]{1,0:T(8,128)}, bf16[1536,768]{1,0:T(8,128)(2,1)}) custom-call(s32[2]{0:T(128)} %pad_add_fusion.where_ref, bf16[128,1536]{1,0:T(8,128)(2,1)} %bitcast.66, bf16[128,1536]{1,0:T(8,128)(2,1)} %collective-permute-done.t1, ...), custom_call_target="tpu_custom_call" | custom-call | tf_op jit(solution)/shard_map/pallas_call | solution.py:870
  110.4 9.9 %shard_map.233 = (f32[8,128,640]{2,1,0:T(8,128)}, bf16[8,128,640]{2,1,0:T(8,128)(2,1)}, f32[8,128,384]{2,1,0:T(8,128)}, f32[8,128,384]{2,1,0:T(8,128)}, f32[8,128,384]{2,1,0:T(8,128)}) custom-call(s32[2]{0:T(128)} %pad_add_fusion.where_ref, bf16[8,128,640]{2,1,0:T(8,128)(2,1)} %bitcast.49, f32[8,128,128]{2,1,0:T(8,128)} %bitcast.59, ...), custom_call_target="tpu_custom_call" | custom-call | tf_op jit(solution)/shard_map/pallas_call | solution.py:828
  121.2 12.1 %shard_map.234 = (f32[1024,384]{1,0:T(8,128)}, f32[1024,384]{1,0:T(8,128)}, f32[8,8,128]{2,1,0:T(8,128)}, bf16[512,1536]{1,0:T(8,128)(2,1)}, bf16[512,1536]{1,0:T(8,128)(2,1)}, /*index=5*/bf16[1536,384]{1,0:T(8,128)(2,1)}) custom-call(s32[2]{0:T(128)} %pad_add_fusion.where_ref, bf16[1024,1536]{1,0:T(8,128)(2,1)} %get-tuple-element.72.normed_ref, ...), custom_call_target="tpu_custom_call" | custom-call | tf_op jit(solution)/shard_map/pallas_call | solution.py:870
  143.3 6.4 %shard_map.235 = (f32[1024,384]{1,0:T(8,128)}, bf16[1024,384]{1,0:T(8,128)(2,1)}, bf16[1024,384]{1,0:T(8,128)(2,1)}, bf16[1024,128]{1,0:T(8,128)(2,1)}) custom-call(s32[2]{0:T(128)} %pad_add_fusion.where_ref, f32[8,8,128]{2,1,0:T(8,128)} %add_add_fusion.sums_ref, f32[1024,384]{1,0:T(8,128)} %bitcast.48, f32[1024,384]{1,0:T(8,128)} %get-tuple-element.83.gate_ref, ...), custom_call_target="tpu_custom_call" | custom-call | tf_op jit(solution)/shard_map/pallas_call | solution.py:870
  149.7 17.3 %shard_map.236 = (bf16[8,128,768]{2,1,0:T(8,128)(2,1)}, f32[8,640]{1,0:T(8,128)}, f32[8,128]{1,0:T(8,128)}) custom-call(s32[2]{0:T(128)} %pad_add_fusion.where_ref, f32[8,128,384]{2,1,0:T(8,128)} %bitcast.61, f32[8,128,384]{2,1,0:T(8,128)} %get-tuple-element.87.inter_ref, f32[8,128,384]{2,1,0:T(8,128)} %get-tuple-element.88.state_ref, ...), custom_call_target="tpu_custom_call" | custom-call | tf_op jit(solution)/shard_map/pallas_call | solution.py:828
  167.8 10.5 %shard_map.240 = (bf16[768,384]{1,0:T(8,128)(2,1)}, bf16[768,384]{1,0:T(8,128)(2,1)}, bf16[768,384]{1,0:T(8,128)(2,1)}, bf16[768,384]{1,0:T(8,128)(2,1)}) custom-call(s32[2]{0:T(128)} %pad_add_fusion.where_ref, bf16[1024,1536]{1,0:T(8,128)(2,1)} %get-tuple-element.72.normed_ref, bf16[1024,384]{1,0:T(8,128)(2,1)} %get-tuple-element.85.gate_ref.grad_gate_ref, ...), custom_call_target="tpu_custom_call" | custom-call | tf_op jit(solution)/shard_map/pallas_call | solution.py:870
  178.6 5.4 %convolution_convert_fusion.rows_ref = bf16[1536,768]{1,0:T(8,128)(2,1)} fusion(bf16[1024,1536]{1,0:T(8,128)(2,1)S(1)} %copy-done, bf16[1024,768]{1,0:T(8,128)(2,1)} %bitcast.68), kind=kOutput, calls=%fused_computation | convolution fusion | flops 2417098752 | bytes 7077888 | tf_op jit(solution)/shard_map/dot_general | solution.py:1394
  184.0 5.0 %shard_map.237 = bf16[8,4,56,384]{3,2,1,0:T(8,128)(2,1)} custom-call(s32[2]{0:T(128)} %pad_add_fusion.where_ref, bf16[1536,768]{1,0:T(8,128)(2,1)} %convolution_convert_fusion.rows_ref, f32[8,640]{1,0:T(8,128)} %get-tuple-element.93.taps_ref, f32[8,128]{1,0:T(8,128)} %get-tuple-element.94.heads_ref, f32[128,128]{1,0:T(8,128)} %get-tuple-element.95.pick_ref), custom_call_target="tpu_custom_call" | custom-call | tf_op jit(solution)/shard_map/pallas_call | solution.py:1121
  191.5 7.8 %shard_map.238 = (bf16[512,1536]{1,0:T(8,128)(2,1)}, bf16[512,1536]{1,0:T(8,128)(2,1)}) custom-call(bf16[1024,384]{1,0:T(8,128)(2,1)} %get-tuple-element.85.gate_ref.grad_gate_ref, bf16[1024,768]{1,0:T(8,128)(2,1)} %bitcast.69, bf16[1536,384]{1,0:T(8,128)(2,1)} %get-tuple-element.96.w_gate_ref, bf16[1536,768]{1,0:T(8,128)(2,1)} %get-tuple-element.97.w_rest_ref), custom_call_target="tpu_custom_call" | custom-call | tf_op jit(solution)/shard_map/pallas_call | solution.py:799
  199.4 3.4 %collective-permute-start.44 = (bf16[768,384]{1,0:T(8,128)(2,1)}, bf16[768,384]{1,0:T(8,128)(2,1)}, u32[]{:S(2)}, u32[]{:S(2)}) collective-permute-start(bf16[768,384]{1,0:T(8,128)(2,1)} %get-tuple-element.105), channel_id=1, source_target_pairs={{0,24},{8,0},{16,8},{24,16},{1,25},{9,1},{17,9},{25,17},{2,26},{10... | collective-permute-start | bytes 1769480 | tf_op jit(solution)/shard_map/ppermute | solution.py:1133
  206.0 10.9 %collective-permute-done.44.p1 = bf16[768,384]{1,0:T(8,128)(2,1)} collective-permute-done((bf16[768,384]{1,0:T(8,128)(2,1)}, bf16[768,384]{1,0:T(8,128)(2,1)}, u32[]{:S(2)}, u32[]{:S(2)}) %collective-permute-start.44) | collective-permute-done | bytes 589856 | tf_op jit(solution)/shard_map/ppermute | solution.py:1133
  222.4 4.3 %collective-permute-start.47 = (bf16[384,384]{1,0:T(8,128)(2,1)}, bf16[384,384]{1,0:T(8,128)(2,1)S(1)}, u32[]{:S(2)}, u32[]{:S(2)}) collective-permute-start(bf16[384,384]{1,0:T(8,128)(2,1)} %get-tuple-element.131), channel_id=1, source_target_pairs={{0,24},{8,0},{16,8},{24,16},{1,25},{9,1},{17,9},{25,17},{2,26},{10... | collective-permute-start | bytes 884744 | tf_op jit(solution)/shard_map/ppermute | solution.py:1133
  226.7 3.3 %collective-permute-done.46.p2 = bf16[768,384]{1,0:T(8,128)(2,1)S(1)} collective-permute-done((bf16[768,384]{1,0:T(8,128)(2,1)S(1)}, bf16[768,384]{1,0:T(8,128)(2,1)S(1)}, u32[]{:S(2)}, u32[]{:S(2)}) %collective-permute-start.46) | collective-permute-done | bytes 589856 | tf_op jit(solution)/shard_map/ppermute | solution.py:1133
  236.0 8.2 %collective-permute-start.54 = (f32[56,384]{1,0:T(8,128)}, f32[56,384]{1,0:T(8,128)S(1)}, u32[]{:S(2)}, u32[]{:S(2)}) collective-permute-start(f32[56,384]{1,0:T(8,128)} %get-tuple-element.140), channel_id=1, source_target_pairs={{0,24},{8,0},{16,8},{24,16},{1,25},{9,1},{17,9},{25,17},{2,26},{10... | collective-permute-start | bytes 258056 | tf_op jit(solution)/shard_map/ppermute | solution.py:1133
  244.2 12.8 %collective-permute-done.48.c2 = bf16[384,384]{1,0:T(8,128)(2,1)S(1)} collective-permute-done((bf16[384,384]{1,0:T(8,128)(2,1)}, bf16[384,384]{1,0:T(8,128)(2,1)S(1)}, u32[]{:S(2)}, u32[]{:S(2)}) %collective-permute-start.48) | collective-permute-done | bytes 294944 | tf_op jit(solution)/shard_map/ppermute | solution.py:1133
  260.1 3.5 %all-to-all-start.1 = ((bf16[8,48,768]{2,1,0:T(8,128)(2,1)}), bf16[8,48,768]{2,1,0:T(8,128)(2,1)S(1)}, u32[]{:S(2)}, u32[]{:S(2)}) async-start(bf16[8,48,768]{2,1,0:T(8,128)(2,1)} %shard_map.242), calls=%async_computation.1 | async-start | bytes 1179648 | tf_op jit(solution)/shard_map/all_to_all | solution.py:1416
  275.9 6.2 %collective-permute-done.32.o1 = bf16[128,1536]{1,0:T(8,128)(2,1)S(1)} collective-permute-done((bf16[128,1536]{1,0:T(8,128)(2,1)S(1)}, bf16[128,1536]{1,0:T(8,128)(2,1)S(1)}, u32[]{:S(2)}, u32[]{:S(2)}) %collective-permute-start.32) | collective-permute-done | bytes 393248 | tf_op jit(solution)/shard_map/ppermute | solution.py:1127
  287.1 4.4 %collective-permute-done.34.o3 = bf16[128,1536]{1,0:T(8,128)(2,1)S(1)} collective-permute-done((bf16[128,1536]{1,0:T(8,128)(2,1)S(1)}, bf16[128,1536]{1,0:T(8,128)(2,1)S(1)}, u32[]{:S(2)}, u32[]{:S(2)}) %collective-permute-start.34) | collective-permute-done | bytes 393248 | tf_op jit(solution)/shard_map/ppermute | solution.py:1127
  291.5 7.6 %collective-permute-done.40.g1 = bf16[128,1536]{1,0:T(8,128)(2,1)} collective-permute-done((bf16[128,1536]{1,0:T(8,128)(2,1)}, bf16[128,1536]{1,0:T(8,128)(2,1)}, u32[]{:S(2)}, u32[]{:S(2)}) %collective-permute-start.40) | collective-permute-done | bytes 393248 | tf_op jit(solution)/shard_map/ppermute | solution.py:1127
  299.1 8.8 %collective-permute-done.42.g3 = bf16[128,1536]{1,0:T(8,128)(2,1)} collective-permute-done((bf16[128,1536]{1,0:T(8,128)(2,1)S(1)}, bf16[128,1536]{1,0:T(8,128)(2,1)}, u32[]{:S(2)}, u32[]{:S(2)}) %collective-permute-start.42) | collective-permute-done | bytes 393248 | tf_op jit(solution)/shard_map/ppermute | solution.py:1127
  307.9 4.6 %shard_map.239 = (bf16[128,1536]{1,0:T(8,128)(2,1)}, f32[128,1536]{1,0:T(8,128)}) custom-call(s32[2]{0:T(128)} %pad_add_fusion.where_ref, bf16[128,1536]{1,0:T(8,128)(2,1)} %get-tuple-element.128.o0, bf16[128,1536]{1,0:T(8,128)(2,1)} %copy-done.19, bf16[128,1536]{1,0:T(8,128)(2,1)} %copy-done.20, bf16[128,1536]{1,0:T(8,128)(2,1)} %copy-done.21, ...), custom_call_target="tpu_custom_call" | custom-call | tf_op jit(solution)/shard_map/pallas_call | solution.py:1121
  (193 shorter events, 97.3 us)
Async XLA Ops:
  22.6 19.2 %collective-permute-start.1 = (bf16[128,1536]{1,0:T(8,128)(2,1)}, bf16[128,1536]{1,0:T(8,128)(2,1)}, u32[]{:S(2)}, u32[]{:S(2)}) collective-permute-start(bf16[128,1536]{1,0:T(8,128)(2,1)} %bitcast.63), channel_id=1, source_target_pairs={{0,4},{1,5},{2,6},{3,7},{4,0},{5,1},{6,2},{7,3},{8,12},{9,13},{10,... | collective-permute-start | bytes 1179656 | tf_op jit(solution)/shard_map/ppermute | solution.py:1127
  24.3 20.5 %collective-permute-start.2 = (bf16[128,1536]{1,0:T(8,128)(2,1)}, bf16[128,1536]{1,0:T(8,128)(2,1)}, u32[]{:S(2)}, u32[]{:S(2)}) collective-permute-start(bf16[128,1536]{1,0:T(8,128)(2,1)} %bitcast.64), channel_id=1, source_target_pairs={{0,6},{1,7},{2,4},{3,5},{4,2},{5,3},{6,0},{7,1},{8,14},{9,15},{10,... | collective-permute-start | bytes 1179656 | tf_op jit(solution)/shard_map/ppermute | solution.py:1127
  28.3 16.6 %collective-permute-start.3 = (bf16[128,1536]{1,0:T(8,128)(2,1)}, bf16[128,1536]{1,0:T(8,128)(2,1)S(1)}, u32[]{:S(2)}, u32[]{:S(2)}) collective-permute-start(bf16[128,1536]{1,0:T(8,128)(2,1)} %bitcast.65), channel_id=1, source_target_pairs={{0,1},{1,0},{2,3},{3,2},{4,5},{5,4},{6,7},{7,6},{8,9},{9,8},{10,11... | collective-permute-start | bytes 1179656 | tf_op jit(solution)/shard_map/ppermute | solution.py:1127
  31.3 18.7 %collective-permute-start.24 = (bf16[128,1536]{1,0:T(8,128)(2,1)}, bf16[128,1536]{1,0:T(8,128)(2,1)S(1)}, u32[]{:S(2)}, u32[]{:S(2)}) collective-permute-start(bf16[128,1536]{1,0:T(8,128)(2,1)} %bitcast.51), channel_id=1, source_target_pairs={{0,2},{1,3},{2,0},{3,1},{4,6},{5,7},{6,4},{7,5},{8,10},{9,11},{10,... | collective-permute-start | bytes 1179656 | tf_op jit(solution)/shard_map/ppermute | solution.py:1127
  32.9 32.3 %all-to-all-start = ((bf16[8,48,768]{2,1,0:T(8,128)(2,1)}), bf16[8,48,768]{2,1,0:T(8,128)(2,1)S(1)}, u32[]{:S(2)}, u32[]{:S(2)}) async-start(bf16[8,48,768]{2,1,0:T(8,128)(2,1)} %get-tuple-element.70), calls=%async_computation | async-start | bytes 1179648 | tf_op jit(solution)/shard_map/all_to_all | solution.py:1261
  36.5 28.1 %collective-permute-start.25 = (bf16[128,1536]{1,0:T(8,128)(2,1)S(1)}, bf16[128,1536]{1,0:T(8,128)(2,1)S(1)}, u32[]{:S(2)}, u32[]{:S(2)}) collective-permute-start(bf16[128,1536]{1,0:T(8,128)(2,1)S(1)} %bitcast.55), channel_id=1, source_target_pairs={{0,4},{1,5},{2,6},{3,7},{4,0},{5,1},{6,2},{7,3},{8,12},{9,13},{10,... | collective-permute-start | bytes 1179656 | tf_op jit(solution)/shard_map/ppermute | solution.py:1127
  41.8 22.8 %collective-permute-start.26 = (bf16[128,1536]{1,0:T(8,128)(2,1)S(1)}, bf16[128,1536]{1,0:T(8,128)(2,1)S(1)}, u32[]{:S(2)}, u32[]{:S(2)}) collective-permute-start(bf16[128,1536]{1,0:T(8,128)(2,1)S(1)} %bitcast.56), channel_id=1, source_target_pairs={{0,6},{1,7},{2,4},{3,5},{4,2},{5,3},{6,0},{7,1},{8,14},{9,15},{10,... | collective-permute-start | bytes 1179656 | tf_op jit(solution)/shard_map/ppermute | solution.py:1127
  44.8 20.3 %collective-permute-start.27 = (bf16[128,1536]{1,0:T(8,128)(2,1)S(1)}, bf16[128,1536]{1,0:T(8,128)(2,1)S(1)}, u32[]{:S(2)}, u32[]{:S(2)}) collective-permute-start(bf16[128,1536]{1,0:T(8,128)(2,1)S(1)} %bitcast.57), channel_id=1, source_target_pairs={{0,1},{1,0},{2,3},{3,2},{4,5},{5,4},{6,7},{7,6},{8,9},{9,8},{10,11... | collective-permute-start | bytes 1179656 | tf_op jit(solution)/shard_map/ppermute | solution.py:1127
  44.9 21.0 %collective-permute-start.15 = (bf16[96,1536]{1,0:T(8,128)(2,1)}, bf16[96,1536]{1,0:T(8,128)(2,1)}, u32[]{:S(2)}, u32[]{:S(2)}) collective-permute-start(bf16[96,1536]{1,0:T(8,128)(2,1)} %collective-permute-done.14.p1), channel_id=1, source_target_pairs={{0,8},{8,16},{16,24},{24,0},{1,9},{9,17},{17,25},{25,1},{2,10},{10... | collective-permute-start | bytes 884744 | tf_op jit(solution)/shard_map/ppermute | solution.py:1133
  50.0 17.8 %collective-permute-start.4 = (bf16[128,1536]{1,0:T(8,128)(2,1)}, bf16[128,1536]{1,0:T(8,128)(2,1)}, u32[]{:S(2)}, u32[]{:S(2)}) collective-permute-start(bf16[128,1536]{1,0:T(8,128)(2,1)} %collective-permute-done.t1), channel_id=1, source_target_pairs={{0,1},{1,0},{2,3},{3,2},{4,5},{5,4},{6,7},{7,6},{8,9},{9,8},{10,11... | collective-permute-start | bytes 1179656 | tf_op jit(solution)/shard_map/ppermute | solution.py:1127
  64.6 20.1 %collective-permute-start.13 = (bf16[224,1536]{1,0:T(8,128)(2,1)S(1)}, bf16[224,1536]{1,0:T(8,128)(2,1)}, u32[]{:S(2)}, u32[]{:S(2)}) collective-permute-start(bf16[224,1536]{1,0:T(8,128)(2,1)S(1)} %pad_maximum_fusion.mine_ref), channel_id=1, source_target_pairs={{0,1},{1,0},{2,3},{3,2},{4,5},{5,4},{6,7},{7,6},{8,9},{9,8},{10,11... | collective-permute-start | bytes 2064392 | tf_op jit(solution)/shard_map/ppermute | solution.py:1127
  78.0 42.3 %collective-permute-start.29 = (bf16[128,1536]{1,0:T(8,128)(2,1)S(1)}, bf16[128,1536]{1,0:T(8,128)(2,1)S(1)}, u32[]{:S(2)}, u32[]{:S(2)}) collective-permute-start(bf16[128,1536]{1,0:T(8,128)(2,1)S(1)} %collective-permute-done.25.c2), channel_id=1, source_target_pairs={{0,1},{1,0},{2,3},{3,2},{4,5},{5,4},{6,7},{7,6},{8,9},{9,8},{10,11... | collective-permute-start | bytes 1179656 | tf_op jit(solution)/shard_map/ppermute | solution.py:1127
  78.1 42.3 %collective-permute-start.30 = (bf16[128,1536]{1,0:T(8,128)(2,1)S(1)}, bf16[128,1536]{1,0:T(8,128)(2,1)S(1)}, u32[]{:S(2)}, u32[]{:S(2)}) collective-permute-start(bf16[128,1536]{1,0:T(8,128)(2,1)S(1)} %collective-permute-done.26.c3), channel_id=1, source_target_pairs={{0,1},{1,0},{2,3},{3,2},{4,5},{5,4},{6,7},{7,6},{8,9},{9,8},{10,11... | collective-permute-start | bytes 1179656 | tf_op jit(solution)/shard_map/ppermute | solution.py:1127
  84.2 36.1 %collective-permute-start.21 = (bf16[384,384]{1,0:T(8,128)(2,1)S(1)}, bf16[384,384]{1,0:T(8,128)(2,1)}, u32[]{:S(2)}, u32[]{:S(2)}) collective-permute-start(bf16[384,384]{1,0:T(8,128)(2,1)S(1)} %get-tuple-element.136.g0), channel_id=1, source_target_pairs={{0,8},{8,16},{16,24},{24,0},{1,9},{9,17},{17,25},{25,1},{2,10},{10... | collective-permute-start | bytes 884744 | tf_op jit(solution)/shard_map/ppermute | solution.py:1133
  84.7 35.7 %collective-permute-start.22 = (bf16[384,384]{1,0:T(8,128)(2,1)S(1)}, bf16[384,384]{1,0:T(8,128)(2,1)}, u32[]{:S(2)}, u32[]{:S(2)}) collective-permute-start(bf16[384,384]{1,0:T(8,128)(2,1)S(1)} %get-tuple-element.136.g0), channel_id=1, source_target_pairs={{0,16},{8,24},{16,0},{24,8},{1,17},{9,25},{17,1},{25,9},{2,18},{10... | collective-permute-start | bytes 884744 | tf_op jit(solution)/shard_map/ppermute | solution.py:1133
  91.3 29.0 %collective-permute-start.23 = (bf16[384,384]{1,0:T(8,128)(2,1)S(1)}, bf16[384,384]{1,0:T(8,128)(2,1)}, u32[]{:S(2)}, u32[]{:S(2)}) collective-permute-start(bf16[384,384]{1,0:T(8,128)(2,1)S(1)} %get-tuple-element.136.g0), channel_id=1, source_target_pairs={{0,24},{8,0},{16,8},{24,16},{1,25},{9,1},{17,9},{25,17},{2,26},{10... | collective-permute-start | bytes 884744 | tf_op jit(solution)/shard_map/ppermute | solution.py:1133
  149.7 17.3 %collective-permute-start.43 = (bf16[1024,128]{1,0:T(8,128)(2,1)}, bf16[1024,128]{1,0:T(8,128)(2,1)S(1)}, u32[]{:S(2)}, u32[]{:S(2)}) collective-permute-start(bf16[1024,128]{1,0:T(8,128)(2,1)} %get-tuple-element.103), channel_id=1, source_target_pairs={{0,1},{1,0},{2,3},{3,2},{4,5},{5,4},{6,7},{7,6},{8,9},{9,8},{10,11... | collective-permute-start | bytes 786440 | tf_op jit(solution)/shard_map/ppermute | solution.py:1127
  178.2 24.7 %collective-permute-start.45 = (bf16[768,384]{1,0:T(8,128)(2,1)}, bf16[768,384]{1,0:T(8,128)(2,1)}, u32[]{:S(2)}, u32[]{:S(2)}) collective-permute-start(bf16[768,384]{1,0:T(8,128)(2,1)} %get-tuple-element.107), channel_id=1, source_target_pairs={{0,8},{8,16},{16,24},{24,0},{1,9},{9,17},{17,25},{25,1},{2,10},{10... | collective-permute-start | bytes 1769480 | tf_op jit(solution)/shard_map/ppermute | solution.py:1133
  191.1 72.6 %collective-permute-start.31 = (bf16[512,1536]{1,0:T(8,128)(2,1)}, bf16[512,1536]{1,0:T(8,128)(2,1)}, u32[]{:S(2)}, u32[]{:S(2)}) collective-permute-start(bf16[512,1536]{1,0:T(8,128)(2,1)} %get-tuple-element.81), channel_id=1, source_target_pairs={{0,1},{1,0},{2,3},{3,2},{4,5},{5,4},{6,7},{7,6},{8,9},{9,8},{10,11... | collective-permute-start | bytes 4718600 | tf_op jit(solution)/shard_map/ppermute | solution.py:1127
  199.4 68.9 %collective-permute-start.39 = (bf16[512,1536]{1,0:T(8,128)(2,1)}, bf16[512,1536]{1,0:T(8,128)(2,1)}, u32[]{:S(2)}, u32[]{:S(2)}) collective-permute-start(bf16[512,1536]{1,0:T(8,128)(2,1)} %get-tuple-element.99), channel_id=1, source_target_pairs={{0,1},{1,0},{2,3},{3,2},{4,5},{5,4},{6,7},{7,6},{8,9},{9,8},{10,11... | collective-permute-start | bytes 4718600 | tf_op jit(solution)/shard_map/ppermute | solution.py:1127
  199.4 17.5 %collective-permute-start.44 = (bf16[768,384]{1,0:T(8,128)(2,1)}, bf16[768,384]{1,0:T(8,128)(2,1)}, u32[]{:S(2)}, u32[]{:S(2)}) collective-permute-start(bf16[768,384]{1,0:T(8,128)(2,1)} %get-tuple-element.105), channel_id=1, source_target_pairs={{0,24},{8,0},{16,8},{24,16},{1,25},{9,1},{17,9},{25,17},{2,26},{10... | collective-permute-start | bytes 1769480 | tf_op jit(solution)/shard_map/ppermute | solution.py:1133
  204.3 25.7 %collective-permute-start.46 = (bf16[768,384]{1,0:T(8,128)(2,1)S(1)}, bf16[768,384]{1,0:T(8,128)(2,1)S(1)}, u32[]{:S(2)}, u32[]{:S(2)}) collective-permute-start(bf16[768,384]{1,0:T(8,128)(2,1)S(1)} %add_convert_fusion), channel_id=1, source_target_pairs={{0,8},{8,16},{16,24},{24,0},{1,9},{9,17},{17,25},{25,1},{2,10},{10... | collective-permute-start | bytes 1769480 | tf_op jit(solution)/shard_map/ppermute | solution.py:1133
  226.7 30.3 %collective-permute-start.48 = (bf16[384,384]{1,0:T(8,128)(2,1)}, bf16[384,384]{1,0:T(8,128)(2,1)S(1)}, u32[]{:S(2)}, u32[]{:S(2)}) collective-permute-start(bf16[384,384]{1,0:T(8,128)(2,1)} %get-tuple-element.130), channel_id=1, source_target_pairs={{0,16},{8,24},{16,0},{24,8},{1,17},{9,25},{17,1},{25,9},{2,18},{10... | collective-permute-start | bytes 884744 | tf_op jit(solution)/shard_map/ppermute | solution.py:1133
  230.0 27.0 %collective-permute-start.49 = (bf16[384,384]{1,0:T(8,128)(2,1)S(1)}, bf16[384,384]{1,0:T(8,128)(2,1)S(1)}, u32[]{:S(2)}, u32[]{:S(2)}) collective-permute-start(bf16[384,384]{1,0:T(8,128)(2,1)S(1)} %get-tuple-element.129), channel_id=1, source_target_pairs={{0,8},{8,16},{16,24},{24,0},{1,9},{9,17},{17,25},{25,1},{2,10},{10... | collective-permute-start | bytes 884744 | tf_op jit(solution)/shard_map/ppermute | solution.py:1133
  236.0 36.4 %collective-permute-start.54 = (f32[56,384]{1,0:T(8,128)}, f32[56,384]{1,0:T(8,128)S(1)}, u32[]{:S(2)}, u32[]{:S(2)}) collective-permute-start(f32[56,384]{1,0:T(8,128)} %get-tuple-element.140), channel_id=1, source_target_pairs={{0,24},{8,0},{16,8},{24,16},{1,25},{9,1},{17,9},{25,17},{2,26},{10... | collective-permute-start | bytes 258056 | tf_op jit(solution)/shard_map/ppermute | solution.py:1133
  256.9 17.5 %collective-permute-start.56 = (f32[56,384]{1,0:T(8,128)}, f32[56,384]{1,0:T(8,128)}, u32[]{:S(2)}, u32[]{:S(2)}) collective-permute-start(f32[56,384]{1,0:T(8,128)} %get-tuple-element.138), channel_id=1, source_target_pairs={{0,8},{8,16},{16,24},{24,0},{1,9},{9,17},{17,25},{25,1},{2,10},{10... | collective-permute-start | bytes 258056 | tf_op jit(solution)/shard_map/ppermute | solution.py:1133
  260.1 23.4 %all-to-all-start.1 = ((bf16[8,48,768]{2,1,0:T(8,128)(2,1)}), bf16[8,48,768]{2,1,0:T(8,128)(2,1)S(1)}, u32[]{:S(2)}, u32[]{:S(2)}) async-start(bf16[8,48,768]{2,1,0:T(8,128)(2,1)} %shard_map.242), calls=%async_computation.1 | async-start | bytes 1179648 | tf_op jit(solution)/shard_map/all_to_all | solution.py:1416
  268.2 18.9 %collective-permute-start.33 = (bf16[128,1536]{1,0:T(8,128)(2,1)S(1)}, bf16[128,1536]{1,0:T(8,128)(2,1)S(1)}, u32[]{:S(2)}, u32[]{:S(2)}) collective-permute-start(bf16[128,1536]{1,0:T(8,128)(2,1)S(1)} %get-tuple-element.126), channel_id=1, source_target_pairs={{0,4},{1,5},{2,6},{3,7},{4,0},{5,1},{6,2},{7,3},{8,12},{9,13},{10,... | collective-permute-start | bytes 1179656 | tf_op jit(solution)/shard_map/ppermute | solution.py:1127
  272.4 19.1 %collective-permute-start.34 = (bf16[128,1536]{1,0:T(8,128)(2,1)S(1)}, bf16[128,1536]{1,0:T(8,128)(2,1)S(1)}, u32[]{:S(2)}, u32[]{:S(2)}) collective-permute-start(bf16[128,1536]{1,0:T(8,128)(2,1)S(1)} %get-tuple-element.125), channel_id=1, source_target_pairs={{0,6},{1,7},{2,4},{3,5},{4,2},{5,3},{6,0},{7,1},{8,14},{9,15},{10,... | collective-permute-start | bytes 1179656 | tf_op jit(solution)/shard_map/ppermute | solution.py:1127
  272.5 26.6 %collective-permute-start.40 = (bf16[128,1536]{1,0:T(8,128)(2,1)}, bf16[128,1536]{1,0:T(8,128)(2,1)}, u32[]{:S(2)}, u32[]{:S(2)}) collective-permute-start(bf16[128,1536]{1,0:T(8,128)(2,1)} %get-tuple-element.123), channel_id=1, source_target_pairs={{0,2},{1,3},{2,0},{3,1},{4,6},{5,7},{6,4},{7,5},{8,10},{9,11},{10,... | collective-permute-start | bytes 1179656 | tf_op jit(solution)/shard_map/ppermute | solution.py:1127
  274.4 24.7 %collective-permute-start.41 = (bf16[128,1536]{1,0:T(8,128)(2,1)S(1)}, bf16[128,1536]{1,0:T(8,128)(2,1)}, u32[]{:S(2)}, u32[]{:S(2)}) collective-permute-start(bf16[128,1536]{1,0:T(8,128)(2,1)S(1)} %get-tuple-element.122), channel_id=1, source_target_pairs={{0,4},{1,5},{2,6},{3,7},{4,0},{5,1},{6,2},{7,3},{8,12},{9,13},{10,... | collective-permute-start | bytes 1179656 | tf_op jit(solution)/shard_map/ppermute | solution.py:1127
  282.1 25.8 %collective-permute-start.42 = (bf16[128,1536]{1,0:T(8,128)(2,1)S(1)}, bf16[128,1536]{1,0:T(8,128)(2,1)}, u32[]{:S(2)}, u32[]{:S(2)}) collective-permute-start(bf16[128,1536]{1,0:T(8,128)(2,1)S(1)} %get-tuple-element.121), channel_id=1, source_target_pairs={{0,6},{1,7},{2,4},{3,5},{4,2},{5,3},{6,0},{7,1},{8,14},{9,15},{10,... | collective-permute-start | bytes 1179656 | tf_op jit(solution)/shard_map/ppermute | solution.py:1127
  (63 other events, 855.2 us)

commit v2 on v1

--- a/solution.py
+++ b/solution.py
@@ -388,6 +388,13 @@
 LANES = 128
 
 
+def granted(mebibytes):
+    return pltpu.CompilerParams(vmem_limit_bytes=mebibytes << 20)
+
+
+grant, wide_grant, whole_grant = granted(10), granted(18), granted(60)
+
+
 def mm(former, latter, dims=((1,), (0,))):
     return lax.dot_general(former, latter, (dims, ((), ())), preferred_element_type=f32)
 
@@ -543,10 +550,12 @@
 
 
 def gate_kernel(
-    where_ref, normed_ref, g0, g1, g2, g3, c0, c1, c2, c3, c4, c5, c6, c7, out_ref, rows_ref, ssm_ref,
-    gate_ref, ngate_ref, sums_ref, mine_ref, other_ref, weight_ref, cot_ref,
+    where_ref, normed_ref, g0, g1, g2, g3, c0, c1, c2, c3, c4, c5, c6, c7,
+    p0, p1, p2, p3, borrowed_ref, rows_ref, ssm_ref,
+    gate_ref, ngate_ref, sums_ref, gated_ref, weight_ref, cot_ref, out_ref,
 ):
     step = pl.program_id(0)
+    core, plane = lax.bitwise_and(where_ref[0], 1), where_ref[1]
     block = g0.shape[0]
     span = c0.shape[0]
 
@@ -554,6 +563,8 @@
     def _():
         for o, w in enumerate((g0, g1, g2, g3)):
             weight_ref[o * block : (o + 1) * block, :] = w[...]
+        for o, part in enumerate((p0, p1, p2, p3)):
+            place_rows(out_ref, part, borrowed_ref, o, core, lax.bitwise_and(plane - o + 4, 3))
 
     parts = (c0, c1, c2, c3, c4, c5, c6, c7)
     for half in range(4):
@@ -578,7 +589,12 @@
             sums.append(jnp.sum(folded.T, axis=0, keepdims=True))
         row = iota((8, LANES), 0)
         sums_ref[span_at(2 * step + i, where_ref[0])] = jnp.where(row == 0, sums[0], sums[1])
-    part = mm((gated * gain).astype(bf16), out_ref[...]).astype(bf16)
+    gated_ref[...] = (gated * gain).astype(bf16)
+
+
+def out_part_kernel(where_ref, gated_ref, out_ref, mine_ref, other_ref):
+    step = pl.program_id(0)
+    part = mm(gated_ref[...], out_ref[...]).astype(bf16)
 
     @pl.when(step < 2)
     def _():
@@ -625,54 +641,53 @@
                     lent_ref[:, to : to + third] = projected_ref[:, source : source + third]
 
 
-def early_grads_kernel(
-    where_ref, normed_ref, grad_gate_ref, projected_ref, borrowed_ref, c0, c1, c2, c3, c4, c5, c6, c7,
-    b0, b1, b2, b3, cot_ref, rows_ref, total_ref, *, third,
+def gate_grad_kernel(where_ref, normed_ref, grad_gate_ref, b0, b1, b2, b3):
+    total = mm(normed_ref[...], grad_gate_ref[...], ((0,), (0,))).astype(bf16)
+    for o, out_ref in enumerate((b0, b1, b2, b3)):
+
+        @pl.when(pl.program_id(0) == o)
+        def _(out_ref=out_ref):
+            out_ref[...] = total
+
+
+def out_grad_kernel(
+    where_ref, projected_ref, borrowed_ref, cot_ref, b0, b1, b2, b3, rows_ref, total_ref, *, third,
 ):
     step = pl.program_id(0)
     core, plane = lax.bitwise_and(where_ref[0], 1), where_ref[1]
-    span = c0.shape[0]
     rows = 3 * third
-    block = normed_ref.shape[1]
-    half = normed_ref.shape[0] // 2
-
-    def swap(to, lent):
-        rows_ref[:half, to] = borrowed_ref[half:, lent]
-        rows_ref[half:, to] = borrowed_ref[:half, lent]
+    block = b0.shape[1]
+    for k in range(2):
+
+        @pl.when(core == k)
+        def _(k=k):
+            for at_plane, at, _, count in local_slices(k, 2 * third):
+                to = at_plane * rows
+                lent = slice(at_plane // 2 * third, (at_plane // 2 + 1) * third)
+                if count == rows + third:
+                    own_at = at if k == 0 else at + third
+                    rows_ref[:, to : to + rows] = projected_ref[:, own_at : own_at + rows]
+                elif k == 0:
+                    rows_ref[:, to : to + count] = projected_ref[:, at : at + count]
+                    rows_ref[:, to + count : to + rows] = borrowed_ref[:, lent]
+                else:
+                    rows_ref[:, to + third : to + rows] = projected_ref[:, at : at + count]
+                    rows_ref[:, to : to + third] = borrowed_ref[:, lent]
+
+    total = mm(rows_ref[...], cot_ref[...], ((0,), (0,)))
 
     @pl.when(step == 0)
     def _():
-        for i, part in enumerate((c0, c1, c2, c3, c4, c5, c6, c7)):
-            cot_ref[i * span : (i + 1) * span, :] = part[...]
-        for k in range(2):
-
-            @pl.when(core == k)
-            def _(k=k):
-                for at_plane, at, _, count in local_slices(k, 2 * third):
-                    to = at_plane * rows
-                    lent = slice(at_plane // 2 * third, (at_plane // 2 + 1) * third)
-                    if count == rows + third:
-                        own_at = at if k == 0 else at + third
-                        rows_ref[:, to : to + rows] = projected_ref[:, own_at : own_at + rows]
-                    elif k == 0:
-                        rows_ref[:, to : to + count] = projected_ref[:, at : at + count]
-                        swap(slice(to + count, to + rows), lent)
-                    else:
-                        rows_ref[:, to + third : to + rows] = projected_ref[:, at : at + count]
-                        swap(slice(to, to + third), lent)
-
-        total_ref[...] = mm(rows_ref[...], cot_ref[...], ((0,), (0,))).astype(bf16)
-
-    gate = mm(normed_ref[...], grad_gate_ref[...], ((0,), (0,))).astype(bf16)
-    first = pl.multiple_of(rows * lax.bitwise_and(plane - step + 4, 3), third)
-    for o, out_ref in enumerate((b0, b1, b2, b3)):
-
-        @pl.when(step == o)
-        def _(out_ref=out_ref):
-            out_ref[:block, :] = gate
+        total_ref[...] = total
+
+    @pl.when(step == 1)
+    def _():
+        total_ref[...] += total
+        for o, out_ref in enumerate((b0, b1, b2, b3)):
+            first = pl.multiple_of(rows * lax.bitwise_and(plane - o + 4, 3), third)
             for g in range(4):
                 own = total_ref[pl.ds(first, rows), g * block : (g + 1) * block]
-                out_ref[block + g * rows : block + (g + 1) * rows, :] = own
+                out_ref[g * rows : (g + 1) * rows, :] = own.astype(bf16)
 
 
 def backward_kernel(
@@ -803,6 +818,7 @@
         in_specs=[pl.BlockSpec(a.shape, lambda i: (0, 0)) for a in (gate, rest)]
         + [pl.BlockSpec((block, a.shape[1]), lambda i: (i, 0)) for a in (w_gate, w_rest)],
         out_specs=[pl.BlockSpec((half, block), lambda i: (0, i))] * 2,
+        compiler_params=grant,
     )(gate, rest, w_gate, w_rest)
 
 
@@ -835,7 +851,7 @@
             out_specs=out_specs,
             scratch_shapes=list(scratch),
         ),
-        compiler_params=pltpu.CompilerParams(dimension_semantics=("arbitrary",)),
+        compiler_params=grant,
     )(where, *[a for a, _ in inputs])
 
 
@@ -855,14 +871,22 @@
     return place(7 - i, where[0])
 
 
+class Part(typing.NamedTuple):
+    shape: tuple
+    at: tuple
+
+
 class Columns(typing.NamedTuple):
     shape: tuple
-
-
-def rows_call(kernel, where, steps, rows, inputs, outputs, scratch=()):
+    first: int = 0
+
+
+def rows_call(kernel, where, steps, rows, inputs, outputs, scratch=(), params=grant):
     def spec(shape, index):
+        if isinstance(index, Part):
+            return pl.BlockSpec(index.shape, lambda i, where: index.at)
         if isinstance(index, Columns):
-            return pl.BlockSpec(index.shape, lambda i, where: (0, i))
+            return pl.BlockSpec(index.shape, lambda i, where: (0, index.first + i))
         if index is None:
             return pl.BlockSpec(shape, lambda i, where, n=len(shape): (0,) * n)
         return pl.BlockSpec((rows, *shape[1:]), lambda i, where: (index(i), 0))
@@ -877,11 +901,16 @@
             out_specs=[spec(shape, index) for shape, _, index in outputs],
             scratch_shapes=list(scratch),
         ),
+        compiler_params=params,
     )(where, *[a for a, _ in inputs])
 
 
 def each(i):
     return i
+
+
+def halves_swapped(i):
+    return 1 - i
 
 
 def lower(i):
@@ -932,7 +961,7 @@
 
 
 def setup_kernel(
-    where_ref, mine_ref, other_ref, heads_ref,
+    where_ref, s0, s1, s2, s3, s4, s5, s6, s7, heads_ref,
     shared_ref, norm_ref, taps_ref, channels_ref, head_rows_ref, pick_ref,
     gain_all, taps_all, held, *, n_taps, head_width,
 ):
@@ -946,13 +975,13 @@
     own = channels_ref.shape[1]
     for p in range(8):
         source = lax.bitwise_xor(rank, 2 * (p % 4) + p // 4)
-        part_ref, top = (mine_ref, other_ref)[p // 4], p % 4 * (rows + 8)
+        part_ref = (s0, s1, s2, s3, s4, s5, s6, s7)[p]
         for o in range(4):
             at = pl.multiple_of(o * block + source * rows, 16)
             lanes = slice(o * padded, (o + 1) * padded)
-            shared_ref[pl.ds(at, rows), :] = part_ref[top : top + rows, lanes]
+            shared_ref[pl.ds(at, rows), :] = part_ref[:rows, lanes]
             device = 8 * lax.bitwise_and(plane - o + 4, 3) + source
-            held[device] = part_ref[top + rows : top + rows + 8, o * padded : o * padded + LANES].astype(f32)
+            held[device] = part_ref[rows : rows + 8, o * padded : o * padded + LANES].astype(f32)
     for i in range(32):
         vectors = held[i]
         norm_ref[:, i * rows_in : (i + 1) * rows_in] = vectors[0:1, :rows_in]
@@ -989,40 +1018,35 @@
     channels_ref[1:2, :] = mm_exact(head_rows, head_map(own, head_width))[2:3]
 
 
-def out_rows_kernel(where_ref, p0, p1, p2, p3, borrowed_ref, out_ref):
-    rank, plane = where_ref[0], where_ref[1]
-    core = lax.bitwise_and(rank, 1)
-    rows = p0.shape[0]
-    third = rows // 3
-    for o, part in enumerate((p0, p1, p2, p3)):
-        at_plane = lax.bitwise_and(plane - o + 4, 3)
-        for k in range(2):
-            for slices_plane, at, _, count in local_slices(k, 2 * third):
-
-                @pl.when((core == k) & (at_plane == slices_plane))
-                def _(o=o, part=part, k=k, at=at, count=count):
-                    if count == rows + third and k == 0:
-                        out_ref[at : at + rows, :] = part[...]
-                        out_ref[at + rows : at + count, :] = borrowed_ref[o // 2]
-                    elif count == rows + third:
-                        out_ref[at : at + third, :] = borrowed_ref[o // 2]
-                        out_ref[at + third : at + count, :] = part[...]
-                    elif k == 0:
-                        out_ref[at : at + count, :] = part[: 2 * third, :]
-                    else:
-                        out_ref[at : at + count, :] = part[third:, :]
-
-
 def lend_kernel(where_ref, p0, p1, p2, p3, out_ref):
-    core, plane = lax.bitwise_and(where_ref[0], 1), where_ref[1]
+    core = lax.bitwise_and(where_ref[0], 1)
     third = out_ref.shape[1]
-    odd = lax.bitwise_and(plane + 1 + core, 1)
     for o, part in enumerate((p0, p1, p2, p3)):
         for k in range(2):
 
-            @pl.when((odd == o % 2) & (core == k))
+            @pl.when(core == k)
             def _(o=o, part=part, k=k):
-                out_ref[o // 2] = part[2 * third :, :] if k == 0 else part[:third, :]
+                out_ref[o] = part[2 * third :, :] if k == 0 else part[:third, :]
+
+
+def place_rows(out_ref, part_ref, borrowed_ref, o, core, at_plane):
+    rows = part_ref.shape[0]
+    third = rows // 3
+    for k in range(2):
+        for slices_plane, at, _, count in local_slices(k, 2 * third):
+
+            @pl.when((core == k) & (at_plane == slices_plane))
+            def _(k=k, at=at, count=count):
+                if count == rows + third and k == 0:
+                    out_ref[at : at + rows, :] = part_ref[...]
+                    out_ref[at + rows : at + count, :] = borrowed_ref[o]
+                elif count == rows + third:
+                    out_ref[at : at + third, :] = borrowed_ref[o]
+                    out_ref[at + third : at + count, :] = part_ref[...]
+                elif k == 0:
+                    out_ref[at : at + count, :] = part_ref[: 2 * third, :]
+                else:
+                    out_ref[at : at + count, :] = part_ref[third:, :]
 
 
 def total_of(refs, rows=slice(None)):
@@ -1036,24 +1060,23 @@
     return jnp.broadcast_to(column, (column.shape[0], LANES)).T[:1, :count]
 
 
-def early_rows_kernel(p0, p1, p2, w_ref, gain_ref, gate_ref, out_ref, dot_ref):
-    block = gate_ref.shape[0]
+def early_rows_kernel(p0, p1, p2, w_ref, gain_ref, out_ref, dot_ref):
     rows = out_ref.shape[0]
-    gate_ref[...] = total_of((p0, p1, p2), slice(0, block)).astype(bf16)
+    block = p0.shape[1]
     for g in range(4):
-        at = block + g * rows
-        out_ref[:, g * block : (g + 1) * block] = total_of((p0, p1, p2), slice(at, at + rows))
+        at = slice(g * rows, (g + 1) * rows)
+        out_ref[:, g * block : (g + 1) * block] = total_of((p0, p1, p2), at)
     dot = jnp.sum(w_ref[...].astype(f32) * out_ref[...], axis=1, keepdims=True)
     dot_ref[...] = as_row(dot, rows) / gain_ref[...].astype(f32)
 
 
-def late_rows_kernel(gate_ref, c0, c1, c2, c3, out_ref):
-    own = gate_ref.shape[1]
+def late_rows_kernel(g0, g1, g2, c0, c1, c2, out_ref):
+    own = g0.shape[1]
     rows = out_ref.shape[1]
     for r in range(8):
         at = slice(r * rows, (r + 1) * rows)
-        out_ref[r, :, :own] = gate_ref[at, :]
-        out_ref[r, :, own:] = total_of((c0, c1, c2, c3), at).astype(bf16)
+        out_ref[r, :, :own] = total_of((g0, g1, g2), at).astype(bf16)
+        out_ref[r, :, own:] = total_of((c0, c1, c2), at).astype(bf16)
 
 
 def columns_kernel(
@@ -1107,7 +1130,7 @@
     grad_ref[...] = cot_ref[...].astype(f32) + inv_rms * (grad_unit - unit * mean)
 
 
-def once(kernel, inputs, outputs, where=None, scratch=()):
+def once(kernel, inputs, outputs, where=None, scratch=(), params=grant):
     specs = lambda shapes: [pl.BlockSpec(s, lambda *_, n=len(s): (0,) * n) for s in shapes]
     out_shape = [jax.ShapeDtypeStruct(shape, dtype) for shape, dtype in outputs]
     grid_spec = pltpu.PrefetchScalarGridSpec(
@@ -1117,7 +1140,7 @@
         out_specs=specs([shape for shape, _ in outputs]),
         scratch_shapes=list(scratch),
     )
-    call = pl.pallas_call(kernel, out_shape=out_shape, grid_spec=grid_spec)
+    call = pl.pallas_call(kernel, out_shape=out_shape, grid_spec=grid_spec, compiler_params=params)
     return call(*([] if where is None else [where]), *inputs)
 
 
@@ -1152,11 +1175,6 @@
 def plane_gather(value):
     chips = [value] + [hop(value, distance) for distance in (2, 4, 6)]
     return chips + [hop(part, 1) for part in chips]
-
-
-def small_gather(value):
-    mine = jnp.concatenate([value] + [hop(value, distance) for distance in (2, 4, 6)])
-    return mine, hop(mine, 1)
 
 
 def plane_parts(mine, other):
@@ -1184,9 +1202,9 @@
     return plane, at
 
 
-def shared_back_kernel(where_ref, rows_ref, taps_ref, heads_ref, pick_ref, out_ref, *, head_width, piece, first_lane):
+def shared_back_kernel(where_ref, rows_ref, taps_ref, heads_ref, pick_ref, mine_ref, other_ref, *, head_width, piece):
     rank, plane = where_ref[0], where_ref[1]
-    rows = out_ref.shape[2] - 8
+    rows = mine_ref.shape[2] - 8
     local = taps_ref.shape[1]
     own = 6 * head_width
     inner = 8 * own
@@ -1202,18 +1220,18 @@
     head_halves = halves(heads)
     for o in range(4):
         first = 8 * lax.bitwise_and(plane - o + 4, 3)
-        for r in range(8):
+        for p in range(8):
+            r = lax.bitwise_xor(rank, 2 * (p % 4) + p // 4)
+            out_ref, q = (mine_ref, other_ref)[p // 4], p % 4
             chosen = (target == LANES * (first + r)).astype(bf16)
             spread = mm(both, chosen)
-            place_at = place(r, rank)
-            own_rows = slice((8 * o + r) * rows, (8 * o + r + 1) * rows)
-            out_ref[place_at, o, :rows, : 2 * LANES] = rows_ref[own_rows, first_lane : first_lane + 2 * LANES]
-            steps = mm(rows_ref[own_rows, first_lane + 2 * LANES :], pick_ref[...].astype(bf16))
-            out_ref[place_at, o, :rows, 2 * LANES :] = steps.astype(bf16)
+            own_rows = rows_ref[pl.ds(pl.multiple_of((8 * o + r) * rows, 16), rows), :]
+            out_ref[q, o, :rows, : 2 * LANES] = own_rows[:, : 2 * LANES]
+            out_ref[q, o, :rows, 2 * LANES :] = mm(own_rows[:, 2 * LANES :], pick_ref[...].astype(bf16)).astype(bf16)
             for half in (0, 1):
                 value = spread[8 * half : 8 * half + 8].astype(bf16) + head_halves[half]
-                out_ref[place_at, o, rows:, half * LANES : (half + 1) * LANES] = value
-            out_ref[place_at, o, rows:, 2 * LANES :] = jnp.zeros((8, out_ref.shape[3] - 2 * LANES), bf16)
+                out_ref[q, o, rows:, half * LANES : (half + 1) * LANES] = value
+            out_ref[q, o, rows:, 2 * LANES :] = jnp.zeros((8, out_ref.shape[3] - 2 * LANES), bf16)
 
 
 def split_local(
@@ -1257,19 +1275,21 @@
         functools.partial(pack_kernel, head_width=head_width),
         [w_gate_in, w_conv_in, w_step, norm_gain[None], gate_gain[None], conv_bias[None], conv_weight],
         [((ranks, rows_in, 2 * own), bf16), ((rows_in + 8, padded), bf16)],
+        params=whole_grant,
     )
     cols = lax.all_to_all(cols, "seq", 0, 0).reshape(ranks * rows_in, 2 * own)
     message = jnp.concatenate(planes_gather(message, True), axis=1)
-    tokens_rel, cot_rel = plane_gather(hidden[0]), plane_gather(cotangent[0])
-    shared_mine, shared_other = small_gather(message)
-    conv_w, gate_w = planes_gather(cols[:, :own]), planes_gather(cols[:, own:], True)
+    message = [hidden[0], message, jnp.zeros((span // 2 - rows_in - 8, width), bf16)]
+    tokens_rel, cot_rel = plane_gather(jnp.concatenate(message)), plane_gather(cotangent[0])
+    token_part, shared_part = Part((span, width), (0, 0)), Part((span // 2, width), (2, 0))
+    conv_w, gate_w = planes_gather(cols[:, :own]), planes_gather(cols[:, own:])
     head_values = jnp.pad(jnp.stack([step_bias, decay_log, skip_gain]), ((0, 5), (0, LANES - heads)))
     shared_w, norm_full, taps_rows, channel_rows, head_rows, head_table = rows_call(
         functools.partial(setup_kernel, n_taps=taps, head_width=head_width),
         where,
         1,
         None,
-        [(a, fixed) for a in (shared_mine, shared_other, head_values)],
+        [(a, shared_part) for a in tokens_rel] + [(head_values, fixed)],
         [
             ((width, padded), bf16, fixed),
             ((1, width), f32, fixed),
@@ -1284,25 +1304,25 @@
             pltpu.VMEM((devices, 8, LANES), f32),
         ],
     )
-    (lent_rows,) = once(lend_kernel, out_parts, [((2, third, width), bf16)], where)
-    borrowed = hop(lent_rows, 1)
-    (out_w,) = once(out_rows_kernel, [*out_parts, borrowed], [((own, width), bf16)], where)
+    (lent_rows,) = once(lend_kernel, out_parts, [((planes, third, width), bf16)], where)
+    out_borrowed = hop(lent_rows, 1)
 
     sizes = dict(n_taps=taps, head_width=head_width, states=states)
     rows = tokens // 4
-    norm_full, out_w = lax.optimization_barrier((norm_full, out_w))
     normed, pre, raw, rest_w = rows_call(
         functools.partial(project_kernel, states=states),
         where,
         4,
         rows,
-        [(a, fixed) for a in (*tokens_rel, norm_full, *conv_w, shared_w)],
+        [(a, token_part) for a in tokens_rel]
+        + [(a, fixed) for a in (norm_full, *conv_w, shared_w)],
         [
             ((tokens, width), bf16, each),
             ((tokens, local), bf16, each),
             ((tokens, LANES), f32, each),
             ((width, own + padded), bf16, fixed),
         ],
+        params=wide_grant,
     )
     pre, raw = pre.reshape(ranks, span, local), raw.reshape(ranks, span, LANES)
     mixed, conv, inter, ssm, entering = spans_call(
@@ -1321,25 +1341,34 @@
         [pltpu.VMEM((span + 8, local), f32), pltpu.VMEM((states, own), f32)],
     )
     ssm = ssm.reshape(tokens, own)
-    gate, ngate, sums, part_mine, part_other, gate_all = rows_call(
+    gate, ngate, sums, gated, gate_all, cot, out_w = rows_call(
         gate_kernel,
         where,
         4,
         rows,
         [(normed, each)]
-        + [(a, fixed) for a in (*gate_w, *cot_rel, out_w, channel_rows)]
+        + [(a, fixed) for a in (*gate_w, *cot_rel, *out_parts, out_borrowed, channel_rows)]
         + [(ssm, each)],
         [
             ((tokens, own), f32, each),
             ((tokens, own), f32, each),
             ((ranks, 8, LANES), f32, fixed),
-            ((tokens // 2, width), bf16, lower),
-            ((tokens // 2, width), bf16, upper),
+            ((tokens, own), bf16, each),
             ((width, own), bf16, fixed),
+            ((tokens, width), bf16, each),
+            ((own, width), bf16, fixed),
         ],
-        [pltpu.VMEM((rows, width), bf16)],
+        params=wide_grant,
     )
     sums = plane_total(sums)
+    part_mine, part_other = rows_call(
+        out_part_kernel,
+        where,
+        4,
+        rows,
+        [(gated, each), (out_w, fixed)],
+        [((tokens // 2, width), bf16, lower), ((tokens // 2, width), bf16, upper)],
+    )
     out_own = plane_parts(part_mine, part_other)
 
     grad_y, grad_gate, projected, lent = rows_call(
@@ -1356,21 +1385,25 @@
         ],
     )
     borrowed = hop(lent, 1)
-    early = rows_call(
-        functools.partial(early_grads_kernel, third=third),
+    d_gate = rows_call(
+        gate_grad_kernel,
         where,
-        4,
+        planes,
         None,
-        [(normed, Columns((tokens, block)))]
-        + [(a, fixed) for a in (grad_gate, projected, borrowed, *cot_rel)],
-        [((block + 4 * rows_out, block), bf16, fixed)] * 4,
-        [
-            pltpu.VMEM((tokens, width), bf16),
-            pltpu.VMEM((tokens, own), bf16),
-            pltpu.VMEM((own, width), bf16),
-        ],
-    )
-    early = planes_parts(early)
+        [(normed, Columns((tokens, block))), (grad_gate, fixed)],
+        [((block, own), bf16, fixed)] * 4,
+    )
+    d_gate = planes_parts(d_gate)
+    d_out = rows_call(
+        functools.partial(out_grad_kernel, third=third),
+        where,
+        2,
+        tokens // 2,
+        [(projected, each), (borrowed, halves_swapped), (cot, each)],
+        [((4 * rows_out, block), bf16, fixed)] * 4,
+        [pltpu.VMEM((tokens // 2, own), bf16), pltpu.VMEM((own, width), f32)],
+    )
+    d_out = planes_parts(d_out)
     grad_rest, grad_taps, grad_heads = spans_call(
         functools.partial(backward_kernel, **sizes),
         where,
@@ -1392,27 +1425,30 @@
     )
     grad_rest = grad_rest.reshape(tokens, own + padded)
     d_rest = jnp.dot(normed.T, grad_rest, preferred_element_type=f32).astype(bf16)
-    d_conv = planes_direct([d_rest[o * block : (o + 1) * block, :own] for o in range(planes)])
-    (d_shared,) = once(
-        functools.partial(shared_back_kernel, head_width=head_width, piece=piece, first_lane=own),
-        [d_rest, grad_taps, grad_heads, head_table],
-        [((ranks, planes, rows_in + 8, padded), bf16)],
+    d_conv = planes_parts([d_rest[o * block : (o + 1) * block, :own] for o in range(planes)])
+    d_shared = rows_call(
+        functools.partial(shared_back_kernel, head_width=head_width, piece=piece),
         where,
-    )
-    gate_all, d_shared = lax.optimization_barrier((gate_all, d_shared))
+        1,
+        None,
+        [(d_rest, Columns((width, padded), own // padded))]
+        + [(a, fixed) for a in (grad_taps, grad_heads, head_table)],
+        [((ranks // 2, planes, rows_in + 8, padded), bf16, fixed)] * 2,
+    )
+    gate_all, *d_shared = lax.optimization_barrier((gate_all, *d_shared))
     mine, other = input_grad_call(grad_gate, grad_rest, gate_all, rest_w)
     grad_own = plane_parts(mine, other)
-    d_shared = d_shared.reshape(2, ranks // 2 * planes, rows_in + 8, padded)
+    d_shared = [a.reshape(ranks // 2 * planes, rows_in + 8, padded) for a in d_shared]
     d_shared = plane_parts(d_shared[0], d_shared[1])
     d_shared = sum(part.astype(f32) for part in d_shared)
     d_shared = planes_direct([d_shared[o] for o in range(planes)])
 
-    d_gate, d_out, d_gain = once(
+    d_out, d_gain = once(
         early_rows_kernel,
-        [*early, w_out, gate_gain[None]],
-        [((block, own), bf16), ((rows_out, width), f32), ((1, rows_out), f32)],
-    )
-    (d_in,) = once(late_rows_kernel, [d_gate, *d_conv], [((ranks, rows_in, 2 * own), bf16)])
+        [*d_out, w_out, gate_gain[None]],
+        [((rows_out, width), f32), ((1, rows_out), f32)],
+    )
+    (d_in,) = once(late_rows_kernel, [*d_gate, *d_conv], [((ranks, rows_in, 2 * own), bf16)])
     d_in = lax.all_to_all(d_in, "seq", 0, 0)
     output, grad_hidden = once(
         functools.partial(tokens_out_kernel, inner=inner),

time: 314 us -> 261 us (0.83)
  Pallas kernels: 103 us -> 71.8 us
  starting transfers between devices: 76.3 us -> 65.1 us
  waiting for transfers between devices: 106 us -> 96.1 us
    pallas_call x8 -> x6, Pallas kernels: 25.4 us -> 11 us  [once(): return call(*([] if where is None else [where]), *inputs)]
    pallas_call x5 -> x8, Pallas kernels: 42.9 us -> 32.8 us  [rows_call(): pl.pallas_call(kernel, out_shape=[jax.ShapeDtypeStruct(shape, dtype) for...]
    ppermute x21 -> x24, waiting for transfers between devices: 49.2 us -> 42.5 us  [plane_hop(): return lax.ppermute(value, 'batch', pairs)]
    ppermute x21 -> x24, starting transfers between devices: 38.2 us -> 31.7 us  [plane_hop(): return lax.ppermute(value, 'batch', pairs)]
    ppermute x36 -> x32, starting transfers between devices: 31.1 us -> 25.3 us  [hop(): return lax.ppermute(value, 'seq', pairs)]
    unnamed x75 -> x78, local copies, waits for them, and re-layouts: 5.47 us -> 10.6 us
    pallas_call x2, Pallas kernels: 27.2 us -> 22.4 us  [spans_call(): pl.pallas_call(kernel, out_shape=out_shape, grid_spec=pltpu.PrefetchScala...]
    ppermute x36 -> x32, waiting for transfers between devices: 56.4 us -> 53.6 us  [hop(): return lax.ppermute(value, 'seq', pairs)]
  transfers between devices with their start and end apart: 59 -> 58, of which waited for: 26 -> 20; matrix products, arithmetic and copies ran while one was open for 6% -> 6% of each run, Pallas kernels for 22% -> 23%
where the time goes in v2:
time: 261 us; the launch traced here: 260 us
  waiting for transfers between devices  96.1 us (37%)
  Pallas kernels  71.8 us (28%)
  starting transfers between devices  65.1 us (25%)
  local copies, waits for them, and re-layouts  12.6 us (5%)
  other arithmetic  10.2 us (4%)
  matrix products  2.96 us (1%)
    ppermute x32, waiting for transfers between devices, hop(): return lax.ppermute(value, 'seq', pairs)  53.6 us
    ppermute x24, waiting for transfers between devices, plane_hop(): return lax.ppermute(value, 'batch', pairs)  42.5 us
    pallas_call x8, Pallas kernels, rows_call(): pl.pallas_call(kernel, out_shape=[jax.ShapeDtypeStruct(shape, dtype) for...  32.8 us
    ppermute x24, starting transfers between devices, plane_hop(): return lax.ppermute(value, 'batch', pairs)  31.7 us
    ppermute x32, starting transfers between devices, hop(): return lax.ppermute(value, 'seq', pairs)  25.3 us
    pallas_call x2, Pallas kernels, spans_call(): pl.pallas_call(kernel, out_shape=out_shape, grid_spec=pltpu.PrefetchScala...  22.4 us
    pallas_call x6, Pallas kernels, once(): return call(*([] if where is None else [where]), *inputs)  11 us
    unnamed x78, local copies, waits for them, and re-layouts  10.6 us
  transfers between devices with their start and end apart: 58, of which 20 were waited for; matrix products, arithmetic and copies ran while one was open for 6% of the time, Pallas kernels for 23%

profile of v2, /device:TPU:0, one launch (start us, length us, event | category | flops | bytes accessed | tf_op | source)
XLA Modules:
  0.0 259.9 jit_solution(7476704898135440538)
XLA Ops:
  0.7 5.1 %collective-permute-start.25 = (bf16[96,1536]{1,0:T(8,128)(2,1)}, bf16[96,1536]{1,0:T(8,128)(2,1)S(1)}, u32[]{:S(2)}, u32[]{:S(2)}) collective-permute-start(bf16[96,1536]{1,0:T(8,128)(2,1)} %w_ref.1), channel_id=1, source_target_pairs={{0,24},{8,0},{16,8},{24,16},{1,25},{9,1},{17,9},{25,17},{2,26},{10... | collective-permute-start | bytes 884744 | tf_op jit(solution)/shard_map/ppermute | solution.py:1156
  11.9 4.3 %all-to-all-start = ((bf16[8,48,768]{2,1,0:T(8,128)(2,1)}), bf16[8,48,768]{2,1,0:T(8,128)(2,1)}, u32[]{:S(2)}, u32[]{:S(2)}) async-start(bf16[8,48,768]{2,1,0:T(8,128)(2,1)} %get-tuple-element.76), calls=%async_computation | async-start | bytes 1179648 | tf_op jit(solution)/shard_map/all_to_all | solution.py:1280
  16.7 2.6 collective-permute-start.18
  25.6 10.2 %collective-permute-done.18.c3 = bf16[128,1536]{1,0:T(8,128)(2,1)} collective-permute-done((bf16[128,1536]{1,0:T(8,128)(2,1)S(1)}, bf16[128,1536]{1,0:T(8,128)(2,1)}, u32[]{:S(2)}, u32[]{:S(2)}) %collective-permute-start.18) | collective-permute-done | bytes 393248 | tf_op jit(solution)/shard_map/ppermute | solution.py:1150
  37.3 5.3 %collective-permute-done.17.c2 = bf16[128,1536]{1,0:T(8,128)(2,1)} collective-permute-done((bf16[128,1536]{1,0:T(8,128)(2,1)S(1)}, bf16[128,1536]{1,0:T(8,128)(2,1)}, u32[]{:S(2)}, u32[]{:S(2)}) %collective-permute-start.17) | collective-permute-done | bytes 393248 | tf_op jit(solution)/shard_map/ppermute | solution.py:1150
  48.8 7.9 %collective-permute-done.5.s3.t3 = bf16[192,1536]{1,0:T(8,128)(2,1)S(1)} collective-permute-done((bf16[192,1536]{1,0:T(8,128)(2,1)S(1)}, bf16[192,1536]{1,0:T(8,128)(2,1)S(1)}, u32[]{:S(2)}, u32[]{:S(2)}) %collective-permute-start.5) | collective-permute-done | bytes 589856 | tf_op jit(solution)/shard_map/ppermute | solution.py:1150
  58.3 10.5 %collective-permute-done.4.s2.t2 = bf16[192,1536]{1,0:T(8,128)(2,1)S(1)} collective-permute-done((bf16[192,1536]{1,0:T(8,128)(2,1)S(1)}, bf16[192,1536]{1,0:T(8,128)(2,1)S(1)}, u32[]{:S(2)}, u32[]{:S(2)}) %collective-permute-start.4) | collective-permute-done | bytes 589856 | tf_op jit(solution)/shard_map/ppermute | solution.py:1150
  74.7 5.1 %collective-permute-done.12.w3 = bf16[384,384]{1,0:T(8,128)(2,1)} collective-permute-done((bf16[384,384]{1,0:T(8,128)(2,1)}, bf16[384,384]{1,0:T(8,128)(2,1)}, u32[]{:S(2)}, u32[]{:S(2)}) %collective-permute-start.12) | collective-permute-done | bytes 294944 | tf_op jit(solution)/shard_map/ppermute | solution.py:1156
  79.8 6.8 %collective-permute-done.11.w2 = bf16[384,384]{1,0:T(8,128)(2,1)} collective-permute-done((bf16[384,384]{1,0:T(8,128)(2,1)}, bf16[384,384]{1,0:T(8,128)(2,1)}, u32[]{:S(2)}, u32[]{:S(2)}) %collective-permute-start.11) | collective-permute-done | bytes 294944 | tf_op jit(solution)/shard_map/ppermute | solution.py:1156
  89.9 2.5 shard_map.229
  92.4 7.1 %shard_map.230 = (bf16[1024,1536]{1,0:T(8,128)(2,1)S(1)}, bf16[1024,640]{1,0:T(8,128)(2,1)S(1)}, f32[1024,128]{1,0:T(8,128)S(1)}, bf16[1536,768]{1,0:T(8,128)(2,1)S(1)}) custom-call(s32[2]{0:T(128)S(1)} %pad_add_fusion.where_ref, bf16[192,1536]{1,0:T(8,128)(2,1)S(1)} %maximum_maximum_fusion.s0.t0, bf16[192,1536]{1,0:T(8,128)(2,1)S(1)} %collective-permute-done.3.s1.t1, ...), custom_call_target="tpu_custom_call" | custom-call | tf_op jit(solution)/shard_map/pallas_call | solution.py:894
  99.6 7.5 %shard_map.232 = (f32[8,128,640]{2,1,0:T(8,128)S(1)}, bf16[8,128,640]{2,1,0:T(8,128)(2,1)S(1)}, f32[8,128,384]{2,1,0:T(8,128)S(1)}, f32[8,128,384]{2,1,0:T(8,128)S(1)}, f32[8,128,384]{2,1,0:T(8,128)S(1)}) custom-call(s32[2]{0:T(128)S(1)} %pad_add_fusion.where_ref, bf16[8,128,640]{2,1,0:T(8,128)(2,1)S(1)} %bitcast.49, f32[8,128,128]{2,1,0:T(8,128)S(1)} %bitcast.51, ...), custom_call_target="tpu_custom_call" | custom-call | tf_op jit(solution)/shard_map/pallas_call | solution.py:844
  107.2 6.8 %shard_map.233 = (f32[1024,384]{1,0:T(8,128)S(1)}, f32[1024,384]{1,0:T(8,128)S(1)}, f32[8,8,128]{2,1,0:T(8,128)S(1)}, bf16[1024,384]{1,0:T(8,128)(2,1)S(1)}, bf1...) custom-call(s32[2]{0:T(128)S(1)} %pad_add_fusion.where_ref, ...), custom_call_target="tpu_custom_call" | custom-call | tf_op jit(solution)/shard_map/pallas_call | solution.py:894
  121.2 2.6 %shard_map.235 = (f32[1024,384]{1,0:T(8,128)S(1)}, bf16[1024,384]{1,0:T(8,128)(2,1)S(1)}, bf16[1024,384]{1,0:T(8,128)(2,1)S(1)}, bf16[1024,128]{1,0:T(8,128)(2,1)S(1)}) custom-call(s32[2]{0:T(128)S(1)} %pad_add_fusion.where_ref, f32[8,8,128]{2,1,0:T(8,128)S(1)} %add_add_fusion.sums_ref, f32[1024,384]{1,0:T(8,128)S(1)} %bitcast.48, ...), custom_call_target="tpu_custom_call" | custom-call | tf_op jit(solution)/shard_map/pallas_call | solution.py:894
  123.9 3.5 %shard_map.240 = (bf16[384,384]{1,0:T(8,128)(2,1)S(1)}, bf16[384,384]{1,0:T(8,128)(2,1)S(1)}, bf16[384,384]{1,0:T(8,128)(2,1)S(1)}, bf16[384,384]{1,0:T(8,128)(2,1)S(1)}) custom-call(s32[2]{0:T(128)S(1)} %pad_add_fusion.where_ref, bf16[1024,1536]{1,0:T(8,128)(2,1)S(1)} %get-tuple-element.78.normed_ref, ...), custom_call_target="tpu_custom_call" | custom-call | tf_op jit(solution)/shard_map/pallas_call | solution.py:894
  129.0 14.9 %shard_map.236 = (bf16[8,128,768]{2,1,0:T(8,128)(2,1)S(1)}, f32[8,640]{1,0:T(8,128)S(1)}, f32[8,128]{1,0:T(8,128)S(1)}) custom-call(s32[2]{0:T(128)S(1)} %pad_add_fusion.where_ref, f32[8,128,384]{2,1,0:T(8,128)S(1)} %bitcast.59, f32[8,128,384]{2,1,0:T(8,128)S(1)} %get-tuple-element.94.inter_ref, f32[8,128,384]{2,1,0:T(8,128)S(1)} %get-tuple-element.95.state_ref, ...), custom_call_target="tpu_custom_call" | custom-call | tf_op jit(solution)/shard_map/pallas_call | solution.py:844
  143.9 3.0 %convolution_convert_fusion.rows_ref = bf16[1536,768]{1,0:T(8,128)(2,1)S(1)} fusion(bf16[1024,1536]{1,0:T(8,128)(2,1)S(1)} %get-tuple-element.78.normed_ref, bf16[1024,768]{1,0:T(8,128)(2,1)S(1)} %bitcast.62), kind=kOutput, calls=%fused_computation | convolution fusion | flops 2417098752 | bytes 7077888 | tf_op jit(solution)/shard_map/dot_general | solution.py:1427
  152.0 3.8 %collective-permute-start.42 = (bf16[384,384]{1,0:T(8,128)(2,1)S(1)}, bf16[384,384]{1,0:T(8,128)(2,1)S(1)}, u32[]{:S(2)}, u32[]{:S(2)}) collective-permute-start(bf16[384,384]{1,0:T(8,128)(2,1)S(1)} %get-tuple-element.144), channel_id=1, source_target_pairs={{0,24},{8,0},{16,8},{24,16},{1,25},{9,1},{17,9},{25,17},{2,26},{10... | collective-permute-start | bytes 884744 | tf_op jit(solution)/shard_map/ppermute | solution.py:1156
  155.8 4.1 %shard_map.234 = (bf16[512,1536]{1,0:T(8,128)(2,1)S(1)}, bf16[512,1536]{1,0:T(8,128)(2,1)}) custom-call(s32[2]{0:T(128)S(1)} %pad_add_fusion.where_ref, bf16[1024,384]{1,0:T(8,128)(2,1)S(1)} %get-tuple-element.85.gated_ref, bf16[384,1536]{1,0:T(8,128)(2,1)S(1)} %get-tuple-element.86.out_ref), custom_call_target="tpu_custom_call" | custom-call | tf_op jit(solution)/shard_map/pallas_call | solution.py:894
  159.8 5.6 %shard_map.238 = (bf16[512,1536]{1,0:T(8,128)(2,1)S(1)}, bf16[512,1536]{1,0:T(8,128)(2,1)}) custom-call(bf16[1024,384]{1,0:T(8,128)(2,1)S(1)} %get-tuple-element.92.gate_ref.grad_gate_ref, bf16[1024,768]{1,0:T(8,128)(2,1)S(1)} %bitcast.63, bf16[1536,384]{1,0:T(8,128)(2,1)S(1)} %get-tuple-element.105.w_gate_ref, ...), custom_call_target="tpu_custom_call" | custom-call | tf_op jit(solution)/shard_map/pallas_call | solution.py:814
  165.4 4.0 %shard_map.243 = (bf16[384,384]{1,0:T(8,128)(2,1)S(1)}, bf16[384,384]{1,0:T(8,128)(2,1)}, bf16[384,384]{1,0:T(8,128)(2,1)S(1)}, bf16[384,384]{1,0:T(8,128)(2,1)S(1)}) custom-call(s32[2]{0:T(128)S(1)} %pad_add_fusion.where_ref, bf16[1024,384]{1,0:T(8,128)(2,1)S(1)} %get-tuple-element.126.projected_ref, ...), custom_call_target="tpu_custom_call" | custom-call | tf_op jit(solution)/shard_map/pallas_call | solution.py:894
  173.2 8.5 %collective-permute-done.54 = bf16[384,384]{1,0:T(8,128)(2,1)S(1)} collective-permute-done((bf16[384,384]{1,0:T(8,128)(2,1)S(1)}, bf16[384,384]{1,0:T(8,128)(2,1)S(1)}, u32[]{:S(2)}, u32[]{:S(2)}) %collective-permute-start.54) | collective-permute-done | bytes 294944 | tf_op jit(solution)/shard_map/ppermute | solution.py:1156
  183.2 4.8 %collective-permute-done.41.g2 = bf16[384,384]{1,0:T(8,128)(2,1)S(1)} collective-permute-done((bf16[384,384]{1,0:T(8,128)(2,1)S(1)}, bf16[384,384]{1,0:T(8,128)(2,1)S(1)}, u32[]{:S(2)}, u32[]{:S(2)}) %collective-permute-start.41) | collective-permute-done | bytes 294944 | tf_op jit(solution)/shard_map/ppermute | solution.py:1156
  189.5 4.0 %collective-permute-done.44.c2 = bf16[384,384]{1,0:T(8,128)(2,1)S(1)} collective-permute-done((bf16[384,384]{1,0:T(8,128)(2,1)S(1)}, bf16[384,384]{1,0:T(8,128)(2,1)S(1)}, u32[]{:S(2)}, u32[]{:S(2)}) %collective-permute-start.44) | collective-permute-done | bytes 294944 | tf_op jit(solution)/shard_map/ppermute | solution.py:1156
  195.8 3.8 %all-to-all-start.1 = ((bf16[8,48,768]{2,1,0:T(8,128)(2,1)}), bf16[8,48,768]{2,1,0:T(8,128)(2,1)S(1)}, u32[]{:S(2)}, u32[]{:S(2)}) async-start(bf16[8,48,768]{2,1,0:T(8,128)(2,1)} %shard_map.241), calls=%async_computation.1 | async-start | bytes 1179648 | tf_op jit(solution)/shard_map/all_to_all | solution.py:1452
  205.5 2.7 %add_convert_fusion.4 = (bf16[128,1536]{1,0:T(8,128)(2,1)S(1)}, bf16[128,1536]{1,0:T(8,128)(2,1)}, bf16[128,1536]{1,0:T(8,128)(2,1)}, bf16[128,1536]{1,0:T(8,128)(2,1)S(1)}) fusion(bf16[512,1536]{1,0:T(8,128)(2,1)} %collective-permute-done.27, bf16[512,1536]{1,0:T(8,128)(2,1)S(1)} %get-tuple-element.87), kind=kLoop, calls=%fused_computation.5 | loop fusion | flops 3145728 | bytes 4718592 | tf_op jit(solution)/shard_map/convert_element_type | solution.py:1186
  208.2 11.0 %collective-permute-done.53.p1 = bf16[384,384]{1,0:T(8,128)(2,1)S(1)} collective-permute-done((bf16[384,384]{1,0:T(8,128)(2,1)}, bf16[384,384]{1,0:T(8,128)(2,1)S(1)}, u32[]{:S(2)}, u32[]{:S(2)}) %collective-permute-start.53) | collective-permute-done | bytes 294944 | tf_op jit(solution)/shard_map/ppermute | solution.py:1156
  221.7 2.7 %add_convert_fusion = (bf16[128,1536]{1,0:T(8,128)(2,1)}, bf16[128,1536]{1,0:T(8,128)(2,1)}, bf16[128,1536]{1,0:T(8,128)(2,1)}, bf16[128,1536]{1,0:T(8,128)(2,1)S(1)}) fusion(bf16[512,1536]{1,0:T(8,128)(2,1)} %collective-permute-done.35, bf16[512,1536]{1,0:T(8,128)(2,1)S(1)} %copy-done.6), kind=kLoop, calls=%fused_computation.1 | loop fusion | flops 3145728 | bytes 4718592 | tf_op jit(solution)/shard_map/convert_element_type | solution.py:1186
  240.1 5.0 %collective-permute-done.29.o2 = bf16[128,1536]{1,0:T(8,128)(2,1)} collective-permute-done((bf16[128,1536]{1,0:T(8,128)(2,1)}, bf16[128,1536]{1,0:T(8,128)(2,1)}, u32[]{:S(2)}, u32[]{:S(2)}) %collective-permute-start.29) | collective-permute-done | bytes 393248 | tf_op jit(solution)/shard_map/ppermute | solution.py:1150
  245.1 3.7 %collective-permute-done.38.g3 = bf16[128,1536]{1,0:T(8,128)(2,1)} collective-permute-done((bf16[128,1536]{1,0:T(8,128)(2,1)}, bf16[128,1536]{1,0:T(8,128)(2,1)}, u32[]{:S(2)}, u32[]{:S(2)}) %collective-permute-start.38) | collective-permute-done | bytes 393248 | tf_op jit(solution)/shard_map/ppermute | solution.py:1150
  248.8 5.8 %collective-permute-done.37.g2 = bf16[128,1536]{1,0:T(8,128)(2,1)} collective-permute-done((bf16[128,1536]{1,0:T(8,128)(2,1)}, bf16[128,1536]{1,0:T(8,128)(2,1)}, u32[]{:S(2)}, u32[]{:S(2)}) %collective-permute-start.37) | collective-permute-done | bytes 393248 | tf_op jit(solution)/shard_map/ppermute | solution.py:1150
  256.1 3.9 %shard_map.239 = (bf16[128,1536]{1,0:T(8,128)(2,1)}, f32[128,1536]{1,0:T(8,128)}) custom-call(s32[2]{0:T(128)S(1)} %pad_add_fusion.where_ref, bf16[128,1536]{1,0:T(8,128)(2,1)S(1)} %get-tuple-element.142.o0, bf16[128,1536]{1,0:T(8,128)(2,1)} %collective-permute-done.28.o1, bf16[128,1536]{1,0:T(8,128)(2,1)} %collective-permute-done.29.o2, ...), custom_call_target="tpu_custom_call" | custom-call | tf_op jit(solution)/shard_map/pallas_call | solution.py:1144
  (197 shorter events, 79.6 us)
Async XLA Ops:
  0.7 19.2 %collective-permute-start.25 = (bf16[96,1536]{1,0:T(8,128)(2,1)}, bf16[96,1536]{1,0:T(8,128)(2,1)S(1)}, u32[]{:S(2)}, u32[]{:S(2)}) collective-permute-start(bf16[96,1536]{1,0:T(8,128)(2,1)} %w_ref.1), channel_id=1, source_target_pairs={{0,24},{8,0},{16,8},{24,16},{1,25},{9,1},{17,9},{25,17},{2,26},{10... | collective-permute-start | bytes 884744 | tf_op jit(solution)/shard_map/ppermute | solution.py:1156
  11.9 34.4 %all-to-all-start = ((bf16[8,48,768]{2,1,0:T(8,128)(2,1)}), bf16[8,48,768]{2,1,0:T(8,128)(2,1)}, u32[]{:S(2)}, u32[]{:S(2)}) async-start(bf16[8,48,768]{2,1,0:T(8,128)(2,1)} %get-tuple-element.76), calls=%async_computation | async-start | bytes 1179648 | tf_op jit(solution)/shard_map/all_to_all | solution.py:1280
  16.7 19.0 %collective-permute-start.18 = (bf16[128,1536]{1,0:T(8,128)(2,1)S(1)}, bf16[128,1536]{1,0:T(8,128)(2,1)}, u32[]{:S(2)}, u32[]{:S(2)}) collective-permute-start(bf16[128,1536]{1,0:T(8,128)(2,1)S(1)} %bitcast.54), channel_id=1, source_target_pairs={{0,6},{1,7},{2,4},{3,5},{4,2},{5,3},{6,0},{7,1},{8,14},{9,15},{10,... | collective-permute-start | bytes 1179656 | tf_op jit(solution)/shard_map/ppermute | solution.py:1150
  19.3 23.3 %collective-permute-start.17 = (bf16[128,1536]{1,0:T(8,128)(2,1)S(1)}, bf16[128,1536]{1,0:T(8,128)(2,1)}, u32[]{:S(2)}, u32[]{:S(2)}) collective-permute-start(bf16[128,1536]{1,0:T(8,128)(2,1)S(1)} %bitcast.55), channel_id=1, source_target_pairs={{0,4},{1,5},{2,6},{3,7},{4,0},{5,1},{6,2},{7,3},{8,12},{9,13},{10,... | collective-permute-start | bytes 1179656 | tf_op jit(solution)/shard_map/ppermute | solution.py:1150
  19.9 23.3 %collective-permute-start.16 = (bf16[128,1536]{1,0:T(8,128)(2,1)S(1)}, bf16[128,1536]{1,0:T(8,128)(2,1)S(1)}, u32[]{:S(2)}, u32[]{:S(2)}) collective-permute-start(bf16[128,1536]{1,0:T(8,128)(2,1)S(1)} %bitcast.56), channel_id=1, source_target_pairs={{0,2},{1,3},{2,0},{3,1},{4,6},{5,7},{6,4},{7,5},{8,10},{9,11},{10,... | collective-permute-start | bytes 1179656 | tf_op jit(solution)/shard_map/ppermute | solution.py:1150
  22.4 25.8 %collective-permute-start.6 = (bf16[192,1536]{1,0:T(8,128)(2,1)S(1)}, bf16[192,1536]{1,0:T(8,128)(2,1)S(1)}, u32[]{:S(2)}, u32[]{:S(2)}) collective-permute-start(bf16[192,1536]{1,0:T(8,128)(2,1)S(1)} %maximum_maximum_fusion.s0.t0), channel_id=1, source_target_pairs={{0,1},{1,0},{2,3},{3,2},{4,5},{5,4},{6,7},{7,6},{8,9},{9,8},{10,11... | collective-permute-start | bytes 1769480 | tf_op jit(solution)/shard_map/ppermute | solution.py:1150
  23.1 33.6 %collective-permute-start.5 = (bf16[192,1536]{1,0:T(8,128)(2,1)S(1)}, bf16[192,1536]{1,0:T(8,128)(2,1)S(1)}, u32[]{:S(2)}, u32[]{:S(2)}) collective-permute-start(bf16[192,1536]{1,0:T(8,128)(2,1)S(1)} %maximum_maximum_fusion.s0.t0), channel_id=1, source_target_pairs={{0,6},{1,7},{2,4},{3,5},{4,2},{5,3},{6,0},{7,1},{8,14},{9,15},{10,... | collective-permute-start | bytes 1769480 | tf_op jit(solution)/shard_map/ppermute | solution.py:1150
  42.6 26.1 %collective-permute-start.4 = (bf16[192,1536]{1,0:T(8,128)(2,1)S(1)}, bf16[192,1536]{1,0:T(8,128)(2,1)S(1)}, u32[]{:S(2)}, u32[]{:S(2)}) collective-permute-start(bf16[192,1536]{1,0:T(8,128)(2,1)S(1)} %maximum_maximum_fusion.s0.t0), channel_id=1, source_target_pairs={{0,4},{1,5},{2,6},{3,7},{4,0},{5,1},{6,2},{7,3},{8,12},{9,13},{10,... | collective-permute-start | bytes 1769480 | tf_op jit(solution)/shard_map/ppermute | solution.py:1150
  43.1 25.7 %collective-permute-start.3 = (bf16[192,1536]{1,0:T(8,128)(2,1)S(1)}, bf16[192,1536]{1,0:T(8,128)(2,1)S(1)}, u32[]{:S(2)}, u32[]{:S(2)}) collective-permute-start(bf16[192,1536]{1,0:T(8,128)(2,1)S(1)} %maximum_maximum_fusion.s0.t0), channel_id=1, source_target_pairs={{0,2},{1,3},{2,0},{3,1},{4,6},{5,7},{6,4},{7,5},{8,10},{9,11},{10,... | collective-permute-start | bytes 1769480 | tf_op jit(solution)/shard_map/ppermute | solution.py:1150
  46.4 22.9 %collective-permute-start.22 = (bf16[128,1536]{1,0:T(8,128)(2,1)}, bf16[128,1536]{1,0:T(8,128)(2,1)}, u32[]{:S(2)}, u32[]{:S(2)}) collective-permute-start(bf16[128,1536]{1,0:T(8,128)(2,1)} %collective-permute-done.18.c3), channel_id=1, source_target_pairs={{0,1},{1,0},{2,3},{3,2},{4,5},{5,4},{6,7},{7,6},{8,9},{9,8},{10,11... | collective-permute-start | bytes 1179656 | tf_op jit(solution)/shard_map/ppermute | solution.py:1150
  48.2 21.2 %collective-permute-start.13 = (bf16[384,384]{1,0:T(8,128)(2,1)S(1)}, bf16[384,384]{1,0:T(8,128)(2,1)S(1)}, u32[]{:S(2)}, u32[]{:S(2)}) collective-permute-start(bf16[384,384]{1,0:T(8,128)(2,1)S(1)} %get-tuple-element.149.g0), channel_id=1, source_target_pairs={{0,8},{8,16},{16,24},{24,0},{1,9},{9,17},{17,25},{25,1},{2,10},{10... | collective-permute-start | bytes 884744 | tf_op jit(solution)/shard_map/ppermute | solution.py:1156
  69.3 19.8 %collective-permute-start.7 = (bf16[192,1536]{1,0:T(8,128)(2,1)S(1)}, bf16[192,1536]{1,0:T(8,128)(2,1)}, u32[]{:S(2)}, u32[]{:S(2)}) collective-permute-start(bf16[192,1536]{1,0:T(8,128)(2,1)S(1)} %collective-permute-done.3.s1.t1), channel_id=1, source_target_pairs={{0,1},{1,0},{2,3},{3,2},{4,5},{5,4},{6,7},{7,6},{8,9},{9,8},{10,11... | collective-permute-start | bytes 1769480 | tf_op jit(solution)/shard_map/ppermute | solution.py:1150
  79.8 27.3 %collective-permute-start.21 = (bf16[128,1536]{1,0:T(8,128)(2,1)}, bf16[128,1536]{1,0:T(8,128)(2,1)S(1)}, u32[]{:S(2)}, u32[]{:S(2)}) collective-permute-start(bf16[128,1536]{1,0:T(8,128)(2,1)} %collective-permute-done.17.c2), channel_id=1, source_target_pairs={{0,1},{1,0},{2,3},{3,2},{4,5},{5,4},{6,7},{7,6},{8,9},{9,8},{10,11... | collective-permute-start | bytes 1179656 | tf_op jit(solution)/shard_map/ppermute | solution.py:1150
  86.6 20.5 %collective-permute-start.20 = (bf16[128,1536]{1,0:T(8,128)(2,1)S(1)}, bf16[128,1536]{1,0:T(8,128)(2,1)S(1)}, u32[]{:S(2)}, u32[]{:S(2)}) collective-permute-start(bf16[128,1536]{1,0:T(8,128)(2,1)S(1)} %copy-done.18), channel_id=1, source_target_pairs={{0,1},{1,0},{2,3},{3,2},{4,5},{5,4},{6,7},{7,6},{8,9},{9,8},{10,11... | collective-permute-start | bytes 1179656 | tf_op jit(solution)/shard_map/ppermute | solution.py:1150
  86.6 20.5 %collective-permute-start.26 = (bf16[4,32,1536]{2,1,0:T(8,128)(2,1)S(1)}, bf16[4,32,1536]{2,1,0:T(8,128)(2,1)S(1)}, u32[]{:S(2)}, u32[]{:S(2)}) collective-permute-start(bf16[4,32,1536]{2,1,0:T(8,128)(2,1)S(1)} %shard_map.231), channel_id=1, source_target_pairs={{0,1},{1,0},{2,3},{3,2},{4,5},{5,4},{6,7},{7,6},{8,9},{9,8},{10,11... | collective-permute-start | bytes 1179656 | tf_op jit(solution)/shard_map/ppermute | solution.py:1150
  87.2 20.0 %collective-permute-start.15 = (bf16[384,384]{1,0:T(8,128)(2,1)S(1)}, bf16[384,384]{1,0:T(8,128)(2,1)S(1)}, u32[]{:S(2)}, u32[]{:S(2)}) collective-permute-start(bf16[384,384]{1,0:T(8,128)(2,1)S(1)} %copy-done.12), channel_id=1, source_target_pairs={{0,24},{8,0},{16,8},{24,16},{1,25},{9,1},{17,9},{25,17},{2,26},{10... | collective-permute-start | bytes 884744 | tf_op jit(solution)/shard_map/ppermute | solution.py:1156
  123.8 28.1 %collective-permute-start.52 = (bf16[1024,128]{1,0:T(8,128)(2,1)S(1)}, bf16[1024,128]{1,0:T(8,128)(2,1)S(1)}, u32[]{:S(2)}, u32[]{:S(2)}) collective-permute-start(bf16[1024,128]{1,0:T(8,128)(2,1)S(1)} %get-tuple-element.127), channel_id=1, source_target_pairs={{0,1},{1,0},{2,3},{3,2},{4,5},{5,4},{6,7},{7,6},{8,9},{9,8},{10,11... | collective-permute-start | bytes 786440 | tf_op jit(solution)/shard_map/ppermute | solution.py:1150
  127.4 32.5 %collective-permute-start.40 = (bf16[384,384]{1,0:T(8,128)(2,1)S(1)}, bf16[384,384]{1,0:T(8,128)(2,1)S(1)}, u32[]{:S(2)}, u32[]{:S(2)}) collective-permute-start(bf16[384,384]{1,0:T(8,128)(2,1)S(1)} %get-tuple-element.114), channel_id=1, source_target_pairs={{0,8},{8,16},{16,24},{24,0},{1,9},{9,17},{17,25},{25,1},{2,10},{10... | collective-permute-start | bytes 884744 | tf_op jit(solution)/shard_map/ppermute | solution.py:1156
  146.9 22.7 %collective-permute-start.39 = (bf16[384,384]{1,0:T(8,128)(2,1)S(1)}, bf16[384,384]{1,0:T(8,128)(2,1)S(1)}, u32[]{:S(2)}, u32[]{:S(2)}) collective-permute-start(bf16[384,384]{1,0:T(8,128)(2,1)S(1)} %get-tuple-element.112), channel_id=1, source_target_pairs={{0,24},{8,0},{16,8},{24,16},{1,25},{9,1},{17,9},{25,17},{2,26},{10... | collective-permute-start | bytes 884744 | tf_op jit(solution)/shard_map/ppermute | solution.py:1156
  159.8 43.2 %collective-permute-start.27 = (bf16[512,1536]{1,0:T(8,128)(2,1)}, bf16[512,1536]{1,0:T(8,128)(2,1)}, u32[]{:S(2)}, u32[]{:S(2)}) collective-permute-start(bf16[512,1536]{1,0:T(8,128)(2,1)} %get-tuple-element.88), channel_id=1, source_target_pairs={{0,1},{1,0},{2,3},{3,2},{4,5},{5,4},{6,7},{7,6},{8,9},{9,8},{10,11... | collective-permute-start | bytes 4718600 | tf_op jit(solution)/shard_map/ppermute | solution.py:1150
  169.6 49.6 %collective-permute-start.35 = (bf16[512,1536]{1,0:T(8,128)(2,1)}, bf16[512,1536]{1,0:T(8,128)(2,1)}, u32[]{:S(2)}, u32[]{:S(2)}) collective-permute-start(bf16[512,1536]{1,0:T(8,128)(2,1)} %get-tuple-element.108), channel_id=1, source_target_pairs={{0,1},{1,0},{2,3},{3,2},{4,5},{5,4},{6,7},{7,6},{8,9},{9,8},{10,11... | collective-permute-start | bytes 4718600 | tf_op jit(solution)/shard_map/ppermute | solution.py:1150
  170.5 23.0 %collective-permute-start.44 = (bf16[384,384]{1,0:T(8,128)(2,1)S(1)}, bf16[384,384]{1,0:T(8,128)(2,1)S(1)}, u32[]{:S(2)}, u32[]{:S(2)}) collective-permute-start(bf16[384,384]{1,0:T(8,128)(2,1)S(1)} %add_convert_fusion.9), channel_id=1, source_target_pairs={{0,8},{8,16},{16,24},{24,0},{1,9},{9,17},{17,25},{25,1},{2,10},{10... | collective-permute-start | bytes 884744 | tf_op jit(solution)/shard_map/ppermute | solution.py:1156
  195.8 38.8 %all-to-all-start.1 = ((bf16[8,48,768]{2,1,0:T(8,128)(2,1)}), bf16[8,48,768]{2,1,0:T(8,128)(2,1)S(1)}, u32[]{:S(2)}, u32[]{:S(2)}) async-start(bf16[8,48,768]{2,1,0:T(8,128)(2,1)} %shard_map.241), calls=%async_computation.1 | async-start | bytes 1179648 | tf_op jit(solution)/shard_map/all_to_all | solution.py:1452
  199.6 19.6 %collective-permute-start.53 = (bf16[384,384]{1,0:T(8,128)(2,1)}, bf16[384,384]{1,0:T(8,128)(2,1)S(1)}, u32[]{:S(2)}, u32[]{:S(2)}) collective-permute-start(bf16[384,384]{1,0:T(8,128)(2,1)} %get-tuple-element.130), channel_id=1, source_target_pairs={{0,24},{8,0},{16,8},{24,16},{1,25},{9,1},{17,9},{25,17},{2,26},{10... | collective-permute-start | bytes 884744 | tf_op jit(solution)/shard_map/ppermute | solution.py:1156
  199.7 24.7 %collective-permute-start.55 = (bf16[384,384]{1,0:T(8,128)(2,1)}, bf16[384,384]{1,0:T(8,128)(2,1)S(1)}, u32[]{:S(2)}, u32[]{:S(2)}) collective-permute-start(bf16[384,384]{1,0:T(8,128)(2,1)} %add_convert_fusion.8), channel_id=1, source_target_pairs={{0,8},{8,16},{16,24},{24,0},{1,9},{9,17},{17,25},{25,1},{2,10},{10... | collective-permute-start | bytes 884744 | tf_op jit(solution)/shard_map/ppermute | solution.py:1156
  203.0 22.0 %collective-permute-start.51 = (f32[56,384]{1,0:T(8,128)S(1)}, f32[56,384]{1,0:T(8,128)S(1)}, u32[]{:S(2)}, u32[]{:S(2)}) collective-permute-start(f32[56,384]{1,0:T(8,128)S(1)} %get-tuple-element.151), channel_id=1, source_target_pairs={{0,8},{8,16},{16,24},{24,0},{1,9},{9,17},{17,25},{25,1},{2,10},{10... | collective-permute-start | bytes 258056 | tf_op jit(solution)/shard_map/ppermute | solution.py:1156
  203.0 23.1 %collective-permute-start.50 = (f32[56,384]{1,0:T(8,128)S(1)}, f32[56,384]{1,0:T(8,128)S(1)}, u32[]{:S(2)}, u32[]{:S(2)}) collective-permute-start(f32[56,384]{1,0:T(8,128)S(1)} %get-tuple-element.152), channel_id=1, source_target_pairs={{0,16},{8,24},{16,0},{24,8},{1,17},{9,25},{17,1},{25,9},{2,18},{10... | collective-permute-start | bytes 258056 | tf_op jit(solution)/shard_map/ppermute | solution.py:1156
  224.4 20.7 %collective-permute-start.29 = (bf16[128,1536]{1,0:T(8,128)(2,1)}, bf16[128,1536]{1,0:T(8,128)(2,1)}, u32[]{:S(2)}, u32[]{:S(2)}) collective-permute-start(bf16[128,1536]{1,0:T(8,128)(2,1)} %get-tuple-element.140), channel_id=1, source_target_pairs={{0,4},{1,5},{2,6},{3,7},{4,0},{5,1},{6,2},{7,3},{8,12},{9,13},{10,... | collective-permute-start | bytes 1179656 | tf_op jit(solution)/shard_map/ppermute | solution.py:1150
  225.6 19.5 %collective-permute-start.28 = (bf16[128,1536]{1,0:T(8,128)(2,1)}, bf16[128,1536]{1,0:T(8,128)(2,1)}, u32[]{:S(2)}, u32[]{:S(2)}) collective-permute-start(bf16[128,1536]{1,0:T(8,128)(2,1)} %get-tuple-element.141), channel_id=1, source_target_pairs={{0,2},{1,3},{2,0},{3,1},{4,6},{5,7},{6,4},{7,5},{8,10},{9,11},{10,... | collective-permute-start | bytes 1179656 | tf_op jit(solution)/shard_map/ppermute | solution.py:1150
  226.7 22.0 %collective-permute-start.38 = (bf16[128,1536]{1,0:T(8,128)(2,1)}, bf16[128,1536]{1,0:T(8,128)(2,1)}, u32[]{:S(2)}, u32[]{:S(2)}) collective-permute-start(bf16[128,1536]{1,0:T(8,128)(2,1)} %get-tuple-element.135), channel_id=1, source_target_pairs={{0,6},{1,7},{2,4},{3,5},{4,2},{5,3},{6,0},{7,1},{8,14},{9,15},{10,... | collective-permute-start | bytes 1179656 | tf_op jit(solution)/shard_map/ppermute | solution.py:1150
  229.8 24.8 %collective-permute-start.37 = (bf16[128,1536]{1,0:T(8,128)(2,1)}, bf16[128,1536]{1,0:T(8,128)(2,1)}, u32[]{:S(2)}, u32[]{:S(2)}) collective-permute-start(bf16[128,1536]{1,0:T(8,128)(2,1)} %get-tuple-element.136), channel_id=1, source_target_pairs={{0,4},{1,5},{2,6},{3,7},{4,0},{5,1},{6,2},{7,3},{8,12},{9,13},{10,... | collective-permute-start | bytes 1179656 | tf_op jit(solution)/shard_map/ppermute | solution.py:1150
  231.8 22.8 %collective-permute-start.36 = (bf16[128,1536]{1,0:T(8,128)(2,1)}, bf16[128,1536]{1,0:T(8,128)(2,1)}, u32[]{:S(2)}, u32[]{:S(2)}) collective-permute-start(bf16[128,1536]{1,0:T(8,128)(2,1)} %get-tuple-element.137), channel_id=1, source_target_pairs={{0,2},{1,3},{2,0},{3,1},{4,6},{5,7},{6,4},{7,5},{8,10},{9,11},{10,... | collective-permute-start | bytes 1179656 | tf_op jit(solution)/shard_map/ppermute | solution.py:1150
  (65 other events, 797.2 us)

commit v3 on v2

--- a/solution.py
+++ b/solution.py
@@ -871,11 +871,6 @@
     return place(7 - i, where[0])
 
 
-class Part(typing.NamedTuple):
-    shape: tuple
-    at: tuple
-
-
 class Columns(typing.NamedTuple):
     shape: tuple
     first: int = 0
@@ -883,8 +878,6 @@
 
 def rows_call(kernel, where, steps, rows, inputs, outputs, scratch=(), params=grant):
     def spec(shape, index):
-        if isinstance(index, Part):
-            return pl.BlockSpec(index.shape, lambda i, where: index.at)
         if isinstance(index, Columns):
             return pl.BlockSpec(index.shape, lambda i, where: (0, index.first + i))
         if index is None:
@@ -961,7 +954,7 @@
 
 
 def setup_kernel(
-    where_ref, s0, s1, s2, s3, s4, s5, s6, s7, heads_ref,
+    where_ref, mine_ref, other_ref, heads_ref,
     shared_ref, norm_ref, taps_ref, channels_ref, head_rows_ref, pick_ref,
     gain_all, taps_all, held, *, n_taps, head_width,
 ):
@@ -975,13 +968,13 @@
     own = channels_ref.shape[1]
     for p in range(8):
         source = lax.bitwise_xor(rank, 2 * (p % 4) + p // 4)
-        part_ref = (s0, s1, s2, s3, s4, s5, s6, s7)[p]
+        part_ref, top = (mine_ref, other_ref)[p // 4], p % 4 * (rows + 8)
         for o in range(4):
             at = pl.multiple_of(o * block + source * rows, 16)
             lanes = slice(o * padded, (o + 1) * padded)
-            shared_ref[pl.ds(at, rows), :] = part_ref[:rows, lanes]
+            shared_ref[pl.ds(at, rows), :] = part_ref[top : top + rows, lanes]
             device = 8 * lax.bitwise_and(plane - o + 4, 3) + source
-            held[device] = part_ref[rows : rows + 8, o * padded : o * padded + LANES].astype(f32)
+            held[device] = part_ref[top + rows : top + rows + 8, o * padded : o * padded + LANES].astype(f32)
     for i in range(32):
         vectors = held[i]
         norm_ref[:, i * rows_in : (i + 1) * rows_in] = vectors[0:1, :rows_in]
@@ -1175,6 +1168,12 @@
 def plane_gather(value):
     chips = [value] + [hop(value, distance) for distance in (2, 4, 6)]
     return chips + [hop(part, 1) for part in chips]
+
+
+def small_gather(value):
+    parts = [value] + [hop(value, distance) for distance in (2, 4, 6)]
+    mine = jnp.concatenate(parts)
+    return mine, hop(mine, 1)
 
 
 def plane_parts(mine, other):
@@ -1278,18 +1277,19 @@
         params=whole_grant,
     )
     cols = lax.all_to_all(cols, "seq", 0, 0).reshape(ranks * rows_in, 2 * own)
-    message = jnp.concatenate(planes_gather(message, True), axis=1)
-    message = [hidden[0], message, jnp.zeros((span // 2 - rows_in - 8, width), bf16)]
-    tokens_rel, cot_rel = plane_gather(jnp.concatenate(message)), plane_gather(cotangent[0])
-    token_part, shared_part = Part((span, width), (0, 0)), Part((span // 2, width), (2, 0))
-    conv_w, gate_w = planes_gather(cols[:, :own]), planes_gather(cols[:, own:])
+    message = planes_gather(message, True)
+    message = jnp.concatenate(message, axis=1)
+    tokens_rel, cot_rel = plane_gather(hidden[0]), plane_gather(cotangent[0])
+    shared_mine, shared_other = small_gather(message)
+    conv_cols, gate_cols = cols[:, :own], cols[:, own:]
+    conv_w, gate_w = planes_gather(conv_cols), planes_gather(gate_cols)
     head_values = jnp.pad(jnp.stack([step_bias, decay_log, skip_gain]), ((0, 5), (0, LANES - heads)))
     shared_w, norm_full, taps_rows, channel_rows, head_rows, head_table = rows_call(
         functools.partial(setup_kernel, n_taps=taps, head_width=head_width),
         where,
         1,
         None,
-        [(a, shared_part) for a in tokens_rel] + [(head_values, fixed)],
+        [(a, fixed) for a in (shared_mine, shared_other, head_values)],
         [
             ((width, padded), bf16, fixed),
             ((1, width), f32, fixed),
@@ -1314,8 +1314,7 @@
         where,
         4,
         rows,
-        [(a, token_part) for a in tokens_rel]
-        + [(a, fixed) for a in (norm_full, *conv_w, shared_w)],
+        [(a, fixed) for a in (*tokens_rel, norm_full, *conv_w, shared_w)],
         [
             ((tokens, width), bf16, each),
             ((tokens, local), bf16, each),
@@ -1456,6 +1455,7 @@
         [((span, width), bf16), ((span, width), f32)],
         where,
         [pltpu.VMEM((span, width), f32)],
+        params=whole_grant,
     )
     d_gate, d_conv, d_norm, d_step, *small = once(
         functools.partial(columns_kernel, head_width=head_width),

time: 261 us -> 277 us (1.061)
  waiting for transfers between devices: 96.1 us -> 112 us
    ppermute x24, waiting for transfers between devices: 42.5 us -> 63.6 us  [plane_hop(): return lax.ppermute(value, 'batch', pairs)]
    ppermute x32 -> x36, starting transfers between devices: 25.3 us -> 31.3 us  [hop(): return lax.ppermute(value, 'seq', pairs)]
    ppermute x32 -> x36, waiting for transfers between devices: 53.6 us -> 47.9 us  [hop(): return lax.ppermute(value, 'seq', pairs)]
    ppermute x24, starting transfers between devices: 31.7 us -> 28.8 us  [plane_hop(): return lax.ppermute(value, 'batch', pairs)]
    unnamed x78 -> x93, local copies, waits for them, and re-layouts: 10.6 us -> 9.89 us
  transfers between devices with their start and end apart: 58 -> 62, of which waited for: 20 -> 25; matrix products, arithmetic and copies ran while one was open for 6% -> 5% of each run, Pallas kernels for 23% -> 20%
where the time goes in v3:
time: 277 us; the launch traced here: 276 us
  waiting for transfers between devices  112 us (40%)
  Pallas kernels  71.2 us (26%)
  starting transfers between devices  67.8 us (24%)
  local copies, waits for them, and re-layouts  11.1 us (4%)
  other arithmetic  9.88 us (4%)
  matrix products  2.96 us (1%)
    ppermute x24, waiting for transfers between devices, plane_hop(): return lax.ppermute(value, 'batch', pairs)  63.6 us
    ppermute x36, waiting for transfers between devices, hop(): return lax.ppermute(value, 'seq', pairs)  47.9 us
    pallas_call x8, Pallas kernels, rows_call(): pl.pallas_call(kernel, out_shape=[jax.ShapeDtypeStruct(shape, dtype) for...  32 us
    ppermute x36, starting transfers between devices, hop(): return lax.ppermute(value, 'seq', pairs)  31.3 us
    ppermute x24, starting transfers between devices, plane_hop(): return lax.ppermute(value, 'batch', pairs)  28.8 us
    pallas_call x2, Pallas kernels, spans_call(): pl.pallas_call(kernel, out_shape=out_shape, grid_spec=pltpu.PrefetchScala...  22.7 us
    pallas_call x6, Pallas kernels, once(): return call(*([] if where is None else [where]), *inputs)  10.8 us
    unnamed x93, local copies, waits for them, and re-layouts  9.89 us
  transfers between devices with their start and end apart: 62, of which 25 were waited for; matrix products, arithmetic and copies ran while one was open for 5% of the time, Pallas kernels for 20%

profile of v3, /device:TPU:0, one launch (start us, length us, event | category | flops | bytes accessed | tf_op | source)
XLA Modules:
  0.0 275.8 jit_solution(13966527694744420169)
XLA Ops:
  2.9 5.1 %collective-permute-start.9 = (bf16[56,384]{1,0:T(8,128)(2,1)}, bf16[56,384]{1,0:T(8,128)(2,1)S(1)}, u32[]{:S(2)}, u32[]{:S(2)}) collective-permute-start(bf16[56,384]{1,0:T(8,128)(2,1)} %get-tuple-element.74), channel_id=1, source_target_pairs={{0,24},{8,0},{16,8},{24,16},{1,25},{9,1},{17,9},{25,17},{2,26},{10... | collective-permute-start | bytes 129032 | tf_op jit(solution)/shard_map/ppermute | solution.py:1149
  9.8 4.2 %collective-permute-done.7 = bf16[56,384]{1,0:T(8,128)(2,1)S(1)} collective-permute-done((bf16[56,384]{1,0:T(8,128)(2,1)}, bf16[56,384]{1,0:T(8,128)(2,1)S(1)}, u32[]{:S(2)}, u32[]{:S(2)}) %collective-permute-start.7) | collective-permute-done | bytes 43040 | tf_op jit(solution)/shard_map/ppermute | solution.py:1149
  28.0 3.7 %collective-permute-done.27.p1 = bf16[96,1536]{1,0:T(8,128)(2,1)S(1)} collective-permute-done((bf16[96,1536]{1,0:T(8,128)(2,1)}, bf16[96,1536]{1,0:T(8,128)(2,1)S(1)}, u32[]{:S(2)}, u32[]{:S(2)}) %collective-permute-start.27) | collective-permute-done | bytes 294944 | tf_op jit(solution)/shard_map/ppermute | solution.py:1149
  31.8 4.2 %all-to-all-start = ((bf16[8,48,768]{2,1,0:T(8,128)(2,1)}), bf16[8,48,768]{2,1,0:T(8,128)(2,1)}, u32[]{:S(2)}, u32[]{:S(2)}) async-start(bf16[8,48,768]{2,1,0:T(8,128)(2,1)} %get-tuple-element.76), calls=%async_computation | async-start | bytes 1179648 | tf_op jit(solution)/shard_map/all_to_all | solution.py:1279
  40.1 3.4 %collective-permute-done.1.t2 = bf16[128,1536]{1,0:T(8,128)(2,1)S(1)} collective-permute-done((bf16[128,1536]{1,0:T(8,128)(2,1)}, bf16[128,1536]{1,0:T(8,128)(2,1)S(1)}, u32[]{:S(2)}, u32[]{:S(2)}) %collective-permute-start.1) | collective-permute-done | bytes 393248 | tf_op jit(solution)/shard_map/ppermute | solution.py:1143
  47.9 11.9 %collective-permute-done.22.c3 = bf16[128,1536]{1,0:T(8,128)(2,1)S(1)} collective-permute-done((bf16[128,1536]{1,0:T(8,128)(2,1)S(1)}, bf16[128,1536]{1,0:T(8,128)(2,1)S(1)}, u32[]{:S(2)}, u32[]{:S(2)}) %collective-permute-start.22) | collective-permute-done | bytes 393248 | tf_op jit(solution)/shard_map/ppermute | solution.py:1143
  59.8 6.7 %collective-permute-done.21.c2 = bf16[128,1536]{1,0:T(8,128)(2,1)S(1)} collective-permute-done((bf16[128,1536]{1,0:T(8,128)(2,1)S(1)}, bf16[128,1536]{1,0:T(8,128)(2,1)S(1)}, u32[]{:S(2)}, u32[]{:S(2)}) %collective-permute-start.21) | collective-permute-done | bytes 393248 | tf_op jit(solution)/shard_map/ppermute | solution.py:1143
  73.8 7.3 %collective-permute-done.14.w1 = bf16[384,384]{1,0:T(8,128)(2,1)} collective-permute-done((bf16[384,384]{1,0:T(8,128)(2,1)S(1)}, bf16[384,384]{1,0:T(8,128)(2,1)}, u32[]{:S(2)}, u32[]{:S(2)}) %collective-permute-start.14) | collective-permute-done | bytes 294944 | tf_op jit(solution)/shard_map/ppermute | solution.py:1149
  82.1 5.2 %collective-permute-done.17.g1 = bf16[384,384]{1,0:T(8,128)(2,1)S(1)} collective-permute-done((bf16[384,384]{1,0:T(8,128)(2,1)S(1)}, bf16[384,384]{1,0:T(8,128)(2,1)S(1)}, u32[]{:S(2)}, u32[]{:S(2)}) %collective-permute-start.17) | collective-permute-done | bytes 294944 | tf_op jit(solution)/shard_map/ppermute | solution.py:1149
  87.3 6.3 %collective-permute-done.16.w3 = bf16[384,384]{1,0:T(8,128)(2,1)} collective-permute-done((bf16[384,384]{1,0:T(8,128)(2,1)S(1)}, bf16[384,384]{1,0:T(8,128)(2,1)}, u32[]{:S(2)}, u32[]{:S(2)}) %collective-permute-start.16) | collective-permute-done | bytes 294944 | tf_op jit(solution)/shard_map/ppermute | solution.py:1149
  94.3 5.8 %collective-permute-done.15.w2 = bf16[384,384]{1,0:T(8,128)(2,1)} collective-permute-done((bf16[384,384]{1,0:T(8,128)(2,1)}, bf16[384,384]{1,0:T(8,128)(2,1)}, u32[]{:S(2)}, u32[]{:S(2)}) %collective-permute-start.15) | collective-permute-done | bytes 294944 | tf_op jit(solution)/shard_map/ppermute | solution.py:1149
  103.5 7.2 %shard_map.230 = (bf16[1024,1536]{1,0:T(8,128)(2,1)S(1)}, bf16[1024,640]{1,0:T(8,128)(2,1)S(1)}, f32[1024,128]{1,0:T(8,128)S(1)}, bf16[1536,768]{1,0:T(8,128)(2,1)S(1)}) custom-call(s32[2]{0:T(128)S(1)} %pad_add_fusion.where_ref, bf16[128,1536]{1,0:T(8,128)(2,1)S(1)} %bitcast.65, bf16[128,1536]{1,0:T(8,128)(2,1)S(1)} %copy-done.20, ...), custom_call_target="tpu_custom_call" | custom-call | tf_op jit(solution)/shard_map/pallas_call | solution.py:887
  110.7 7.5 %shard_map.232 = (f32[8,128,640]{2,1,0:T(8,128)S(1)}, bf16[8,128,640]{2,1,0:T(8,128)(2,1)S(1)}, f32[8,128,384]{2,1,0:T(8,128)S(1)}, f32[8,128,384]{2,1,0:T(8,128)S(1)}, f32[8,128,384]{2,1,0:T(8,128)S(1)}) custom-call(s32[2]{0:T(128)S(1)} %pad_add_fusion.where_ref, bf16[8,128,640]{2,1,0:T(8,128)(2,1)S(1)} %bitcast.49, f32[8,128,128]{2,1,0:T(8,128)S(1)} %bitcast.51, ...), custom_call_target="tpu_custom_call" | custom-call | tf_op jit(solution)/shard_map/pallas_call | solution.py:844
  118.3 6.5 %shard_map.233 = (f32[1024,384]{1,0:T(8,128)S(1)}, f32[1024,384]{1,0:T(8,128)S(1)}, f32[8,8,128]{2,1,0:T(8,128)S(1)}, bf16[1024,384]{1,0:T(8,128)(2,1)S(1)}, bf1...) custom-call(s32[2]{0:T(128)S(1)} %pad_add_fusion.where_ref, ...), custom_call_target="tpu_custom_call" | custom-call | tf_op jit(solution)/shard_map/pallas_call | solution.py:887
  126.1 4.9 %collective-permute-start.38 = (f32[8,8,128]{2,1,0:T(8,128)S(1)}, f32[8,8,128]{2,1,0:T(8,128)S(1)}, u32[]{:S(2)}, u32[]{:S(2)}) collective-permute-start(f32[8,8,128]{2,1,0:T(8,128)S(1)} %add.72), channel_id=1, source_target_pairs={{0,6},{1,7},{2,4},{3,5},{4,2},{5,3},{6,0},{7,1},{8,14},{9,15},{10,... | collective-permute-start | bytes 98312 | tf_op jit(solution)/shard_map/ppermute | solution.py:1143
  138.9 3.5 %shard_map.240 = (bf16[384,384]{1,0:T(8,128)(2,1)S(1)}, bf16[384,384]{1,0:T(8,128)(2,1)S(1)}, bf16[384,384]{1,0:T(8,128)(2,1)S(1)}, bf16[384,384]{1,0:T(8,128)(2,1)S(1)}) custom-call(s32[2]{0:T(128)S(1)} %pad_add_fusion.where_ref, bf16[1024,1536]{1,0:T(8,128)(2,1)S(1)} %get-tuple-element.78.normed_ref, ...), custom_call_target="tpu_custom_call" | custom-call | tf_op jit(solution)/shard_map/pallas_call | solution.py:887
  142.4 3.1 %collective-permute-start.44 = (bf16[384,384]{1,0:T(8,128)(2,1)S(1)}, bf16[384,384]{1,0:T(8,128)(2,1)S(1)}, u32[]{:S(2)}, u32[]{:S(2)}) collective-permute-start(bf16[384,384]{1,0:T(8,128)(2,1)S(1)} %get-tuple-element.114), channel_id=1, source_target_pairs={{0,8},{8,16},{16,24},{24,0},{1,9},{9,17},{17,25},{25,1},{2,10},{10... | collective-permute-start | bytes 884744 | tf_op jit(solution)/shard_map/ppermute | solution.py:1149
  145.5 15.2 %shard_map.236 = (bf16[8,128,768]{2,1,0:T(8,128)(2,1)S(1)}, f32[8,640]{1,0:T(8,128)S(1)}, f32[8,128]{1,0:T(8,128)S(1)}) custom-call(s32[2]{0:T(128)S(1)} %pad_add_fusion.where_ref, f32[8,128,384]{2,1,0:T(8,128)S(1)} %bitcast.59, f32[8,128,384]{2,1,0:T(8,128)S(1)} %get-tuple-element.94.inter_ref, f32[8,128,384]{2,1,0:T(8,128)S(1)} %get-tuple-element.95.state_ref, ...), custom_call_target="tpu_custom_call" | custom-call | tf_op jit(solution)/shard_map/pallas_call | solution.py:844
  160.7 3.0 %convolution_convert_fusion.rows_ref = bf16[1536,768]{1,0:T(8,128)(2,1)S(1)} fusion(bf16[1024,1536]{1,0:T(8,128)(2,1)S(1)} %get-tuple-element.78.normed_ref, bf16[1024,768]{1,0:T(8,128)(2,1)S(1)} %bitcast.66), kind=kOutput, calls=%fused_computation | convolution fusion | flops 2417098752 | bytes 7077888 | tf_op jit(solution)/shard_map/dot_general | solution.py:1426
  171.0 4.1 %shard_map.234 = (bf16[512,1536]{1,0:T(8,128)(2,1)S(1)}, bf16[512,1536]{1,0:T(8,128)(2,1)}) custom-call(s32[2]{0:T(128)S(1)} %pad_add_fusion.where_ref, bf16[1024,384]{1,0:T(8,128)(2,1)S(1)} %get-tuple-element.85.gated_ref, bf16[384,1536]{1,0:T(8,128)(2,1)S(1)} %get-tuple-element.86.out_ref), custom_call_target="tpu_custom_call" | custom-call | tf_op jit(solution)/shard_map/pallas_call | solution.py:887
  176.3 5.7 %shard_map.238 = (bf16[512,1536]{1,0:T(8,128)(2,1)S(1)}, bf16[512,1536]{1,0:T(8,128)(2,1)}) custom-call(bf16[1024,384]{1,0:T(8,128)(2,1)S(1)} %get-tuple-element.92.gate_ref.grad_gate_ref, bf16[1024,768]{1,0:T(8,128)(2,1)S(1)} %bitcast.67, bf16[1536,384]{1,0:T(8,128)(2,1)S(1)} %get-tuple-element.105.w_gate_ref, ...), custom_call_target="tpu_custom_call" | custom-call | tf_op jit(solution)/shard_map/pallas_call | solution.py:814
  182.0 3.3 %shard_map.243 = (bf16[384,384]{1,0:T(8,128)(2,1)S(1)}, bf16[384,384]{1,0:T(8,128)(2,1)S(1)}, bf16[384,384]{1,0:T(8,128)(2,1)S(1)}, bf16[384,384]{1,0:T(8,128)(2,1)S(1)}) custom-call(s32[2]{0:T(128)S(1)} %pad_add_fusion.where_ref, bf16[1024,384]{1,0:T(8,128)(2,1)S(1)} %get-tuple-element.126.projected_ref, ...), custom_call_target="tpu_custom_call" | custom-call | tf_op jit(solution)/shard_map/pallas_call | solution.py:887
  188.0 9.5 %collective-permute-done.58 = bf16[384,384]{1,0:T(8,128)(2,1)S(1)} collective-permute-done((bf16[384,384]{1,0:T(8,128)(2,1)S(1)}, bf16[384,384]{1,0:T(8,128)(2,1)S(1)}, u32[]{:S(2)}, u32[]{:S(2)}) %collective-permute-start.58) | collective-permute-done | bytes 294944 | tf_op jit(solution)/shard_map/ppermute | solution.py:1149
  197.6 6.3 %collective-permute-done.45.g2 = bf16[384,384]{1,0:T(8,128)(2,1)S(1)} collective-permute-done((bf16[384,384]{1,0:T(8,128)(2,1)S(1)}, bf16[384,384]{1,0:T(8,128)(2,1)S(1)}, u32[]{:S(2)}, u32[]{:S(2)}) %collective-permute-start.45) | collective-permute-done | bytes 294944 | tf_op jit(solution)/shard_map/ppermute | solution.py:1149
  205.3 4.1 %collective-permute-done.48.c2 = bf16[384,384]{1,0:T(8,128)(2,1)S(1)} collective-permute-done((bf16[384,384]{1,0:T(8,128)(2,1)S(1)}, bf16[384,384]{1,0:T(8,128)(2,1)S(1)}, u32[]{:S(2)}, u32[]{:S(2)}) %collective-permute-start.48) | collective-permute-done | bytes 294944 | tf_op jit(solution)/shard_map/ppermute | solution.py:1149
  212.1 3.5 %all-to-all-start.1 = ((bf16[8,48,768]{2,1,0:T(8,128)(2,1)}), bf16[8,48,768]{2,1,0:T(8,128)(2,1)S(1)}, u32[]{:S(2)}, u32[]{:S(2)}) async-start(bf16[8,48,768]{2,1,0:T(8,128)(2,1)} %shard_map.241), calls=%async_computation.1 | async-start | bytes 1179648 | tf_op jit(solution)/shard_map/all_to_all | solution.py:1451
  224.2 11.0 %collective-permute-done.57.p1 = bf16[384,384]{1,0:T(8,128)(2,1)S(1)} collective-permute-done((bf16[384,384]{1,0:T(8,128)(2,1)}, bf16[384,384]{1,0:T(8,128)(2,1)S(1)}, u32[]{:S(2)}, u32[]{:S(2)}) %collective-permute-start.57) | collective-permute-done | bytes 294944 | tf_op jit(solution)/shard_map/ppermute | solution.py:1149
  237.7 2.8 %add_convert_fusion = (bf16[128,1536]{1,0:T(8,128)(2,1)}, bf16[128,1536]{1,0:T(8,128)(2,1)}, bf16[128,1536]{1,0:T(8,128)(2,1)}, bf16[128,1536]{1,0:T(8,128)(2,1)}) fusion(bf16[512,1536]{1,0:T(8,128)(2,1)} %collective-permute-done.39, bf16[512,1536]{1,0:T(8,128)(2,1)S(1)} %get-tuple-element.107), kind=kLoop, calls=%fused_computation.1 | loop fusion | flops 3145728 | bytes 4718592 | tf_op jit(solution)/shard_map/convert_element_type | solution.py:1185
  254.8 6.3 %collective-permute-done.33.o2 = bf16[128,1536]{1,0:T(8,128)(2,1)S(1)} collective-permute-done((bf16[128,1536]{1,0:T(8,128)(2,1)}, bf16[128,1536]{1,0:T(8,128)(2,1)S(1)}, u32[]{:S(2)}, u32[]{:S(2)}) %collective-permute-start.33) | collective-permute-done | bytes 393248 | tf_op jit(solution)/shard_map/ppermute | solution.py:1143
  261.2 3.4 %collective-permute-done.42.g3 = bf16[128,1536]{1,0:T(8,128)(2,1)S(1)} collective-permute-done((bf16[128,1536]{1,0:T(8,128)(2,1)}, bf16[128,1536]{1,0:T(8,128)(2,1)S(1)}, u32[]{:S(2)}, u32[]{:S(2)}) %collective-permute-start.42) | collective-permute-done | bytes 393248 | tf_op jit(solution)/shard_map/ppermute | solution.py:1143
  264.5 6.0 %collective-permute-done.41.g2 = bf16[128,1536]{1,0:T(8,128)(2,1)S(1)} collective-permute-done((bf16[128,1536]{1,0:T(8,128)(2,1)}, bf16[128,1536]{1,0:T(8,128)(2,1)S(1)}, u32[]{:S(2)}, u32[]{:S(2)}) %collective-permute-start.41) | collective-permute-done | bytes 393248 | tf_op jit(solution)/shard_map/ppermute | solution.py:1143
  271.3 4.6 %shard_map.239 = (bf16[128,1536]{1,0:T(8,128)(2,1)}, f32[128,1536]{1,0:T(8,128)}) custom-call(s32[2]{0:T(128)} %copy-done.28, bf16[128,1536]{1,0:T(8,128)(2,1)} %get-tuple-element.142.o0, bf16[128,1536]{1,0:T(8,128)(2,1)} %copy-done.37, bf16[128,1536]{1,0:T(8,128)(2,1)} %copy-done.36, bf16[128,1536]{1,0:T(8,128)(2,1)} %copy-done.35, ...), custom_call_target="tpu_custom_call" | custom-call | tf_op jit(solution)/shard_map/pallas_call | solution.py:1137
  (219 shorter events, 89.2 us)
Async XLA Ops:
  26.5 19.0 %collective-permute-start = (bf16[128,1536]{1,0:T(8,128)(2,1)}, bf16[128,1536]{1,0:T(8,128)(2,1)S(1)}, u32[]{:S(2)}, u32[]{:S(2)}) collective-permute-start(bf16[128,1536]{1,0:T(8,128)(2,1)} %bitcast.63), channel_id=1, source_target_pairs={{0,2},{1,3},{2,0},{3,1},{4,6},{5,7},{6,4},{7,5},{8,10},{9,11},{10,... | collective-permute-start | bytes 1179656 | tf_op jit(solution)/shard_map/ppermute | solution.py:1143
  31.8 36.3 %all-to-all-start = ((bf16[8,48,768]{2,1,0:T(8,128)(2,1)}), bf16[8,48,768]{2,1,0:T(8,128)(2,1)}, u32[]{:S(2)}, u32[]{:S(2)}) async-start(bf16[8,48,768]{2,1,0:T(8,128)(2,1)} %get-tuple-element.76), calls=%async_computation | async-start | bytes 1179648 | tf_op jit(solution)/shard_map/all_to_all | solution.py:1279
  36.7 23.0 %collective-permute-start.22 = (bf16[128,1536]{1,0:T(8,128)(2,1)S(1)}, bf16[128,1536]{1,0:T(8,128)(2,1)S(1)}, u32[]{:S(2)}, u32[]{:S(2)}) collective-permute-start(bf16[128,1536]{1,0:T(8,128)(2,1)S(1)} %bitcast.55), channel_id=1, source_target_pairs={{0,6},{1,7},{2,4},{3,5},{4,2},{5,3},{6,0},{7,1},{8,14},{9,15},{10,... | collective-permute-start | bytes 1179656 | tf_op jit(solution)/shard_map/ppermute | solution.py:1143
  39.6 27.0 %collective-permute-start.21 = (bf16[128,1536]{1,0:T(8,128)(2,1)S(1)}, bf16[128,1536]{1,0:T(8,128)(2,1)S(1)}, u32[]{:S(2)}, u32[]{:S(2)}) collective-permute-start(bf16[128,1536]{1,0:T(8,128)(2,1)S(1)} %bitcast.56), channel_id=1, source_target_pairs={{0,4},{1,5},{2,6},{3,7},{4,0},{5,1},{6,2},{7,3},{8,12},{9,13},{10,... | collective-permute-start | bytes 1179656 | tf_op jit(solution)/shard_map/ppermute | solution.py:1143
  43.5 23.0 %collective-permute-start.20 = (bf16[128,1536]{1,0:T(8,128)(2,1)S(1)}, bf16[128,1536]{1,0:T(8,128)(2,1)S(1)}, u32[]{:S(2)}, u32[]{:S(2)}) collective-permute-start(bf16[128,1536]{1,0:T(8,128)(2,1)S(1)} %bitcast.57), channel_id=1, source_target_pairs={{0,2},{1,3},{2,0},{3,1},{4,6},{5,7},{6,4},{7,5},{8,10},{9,11},{10,... | collective-permute-start | bytes 1179656 | tf_op jit(solution)/shard_map/ppermute | solution.py:1143
  45.6 23.6 %collective-permute-start.28 = (bf16[96,1536]{1,0:T(8,128)(2,1)S(1)}, bf16[96,1536]{1,0:T(8,128)(2,1)S(1)}, u32[]{:S(2)}, u32[]{:S(2)}) collective-permute-start(bf16[96,1536]{1,0:T(8,128)(2,1)S(1)} %collective-permute-done.27.p1), channel_id=1, source_target_pairs={{0,8},{8,16},{16,24},{24,0},{1,9},{9,17},{17,25},{25,1},{2,10},{10... | collective-permute-start | bytes 884744 | tf_op jit(solution)/shard_map/ppermute | solution.py:1149
  46.6 23.2 %collective-permute-start.6 = (bf16[128,1536]{1,0:T(8,128)(2,1)}, bf16[128,1536]{1,0:T(8,128)(2,1)}, u32[]{:S(2)}, u32[]{:S(2)}) collective-permute-start(bf16[128,1536]{1,0:T(8,128)(2,1)} %collective-permute-done.2.t3), channel_id=1, source_target_pairs={{0,1},{1,0},{2,3},{3,2},{4,5},{5,4},{6,7},{7,6},{8,9},{9,8},{10,11... | collective-permute-start | bytes 1179656 | tf_op jit(solution)/shard_map/ppermute | solution.py:1143
  59.8 33.8 %collective-permute-start.13 = (bf16[224,1536]{1,0:T(8,128)(2,1)S(1)}, bf16[224,1536]{1,0:T(8,128)(2,1)}, u32[]{:S(2)}, u32[]{:S(2)}) collective-permute-start(bf16[224,1536]{1,0:T(8,128)(2,1)S(1)} %pad_maximum_fusion.mine_ref), channel_id=1, source_target_pairs={{0,1},{1,0},{2,3},{3,2},{4,5},{5,4},{6,7},{7,6},{8,9},{9,8},{10,11... | collective-permute-start | bytes 2064392 | tf_op jit(solution)/shard_map/ppermute | solution.py:1143
  71.8 21.8 %collective-permute-start.16 = (bf16[384,384]{1,0:T(8,128)(2,1)S(1)}, bf16[384,384]{1,0:T(8,128)(2,1)}, u32[]{:S(2)}, u32[]{:S(2)}) collective-permute-start(bf16[384,384]{1,0:T(8,128)(2,1)S(1)} %get-tuple-element.150.w0), channel_id=1, source_target_pairs={{0,24},{8,0},{16,8},{24,16},{1,25},{9,1},{17,9},{25,17},{2,26},{10... | collective-permute-start | bytes 884744 | tf_op jit(solution)/shard_map/ppermute | solution.py:1149
  81.1 18.9 %collective-permute-start.15 = (bf16[384,384]{1,0:T(8,128)(2,1)}, bf16[384,384]{1,0:T(8,128)(2,1)}, u32[]{:S(2)}, u32[]{:S(2)}) collective-permute-start(bf16[384,384]{1,0:T(8,128)(2,1)} %collective-permute-done.14.w1), channel_id=1, source_target_pairs={{0,8},{8,16},{16,24},{24,0},{1,9},{9,17},{17,25},{25,1},{2,10},{10... | collective-permute-start | bytes 884744 | tf_op jit(solution)/shard_map/ppermute | solution.py:1149
  82.1 36.2 %collective-permute-start.25 = (bf16[128,1536]{1,0:T(8,128)(2,1)S(1)}, bf16[128,1536]{1,0:T(8,128)(2,1)S(1)}, u32[]{:S(2)}, u32[]{:S(2)}) collective-permute-start(bf16[128,1536]{1,0:T(8,128)(2,1)S(1)} %copy-done.12), channel_id=1, source_target_pairs={{0,1},{1,0},{2,3},{3,2},{4,5},{5,4},{6,7},{7,6},{8,9},{9,8},{10,11... | collective-permute-start | bytes 1179656 | tf_op jit(solution)/shard_map/ppermute | solution.py:1143
  87.3 31.0 %collective-permute-start.24 = (bf16[128,1536]{1,0:T(8,128)(2,1)S(1)}, bf16[128,1536]{1,0:T(8,128)(2,1)S(1)}, u32[]{:S(2)}, u32[]{:S(2)}) collective-permute-start(bf16[128,1536]{1,0:T(8,128)(2,1)S(1)} %copy-done.14), channel_id=1, source_target_pairs={{0,1},{1,0},{2,3},{3,2},{4,5},{5,4},{6,7},{7,6},{8,9},{9,8},{10,11... | collective-permute-start | bytes 1179656 | tf_op jit(solution)/shard_map/ppermute | solution.py:1143
  93.6 24.7 %collective-permute-start.30 = (bf16[4,32,1536]{2,1,0:T(8,128)(2,1)S(1)}, bf16[4,32,1536]{2,1,0:T(8,128)(2,1)S(1)}, u32[]{:S(2)}, u32[]{:S(2)}) collective-permute-start(bf16[4,32,1536]{2,1,0:T(8,128)(2,1)S(1)} %shard_map.231), channel_id=1, source_target_pairs={{0,1},{1,0},{2,3},{3,2},{4,5},{5,4},{6,7},{7,6},{8,9},{9,8},{10,11... | collective-permute-start | bytes 1179656 | tf_op jit(solution)/shard_map/ppermute | solution.py:1143
  93.6 24.7 %collective-permute-start.19 = (bf16[384,384]{1,0:T(8,128)(2,1)S(1)}, bf16[384,384]{1,0:T(8,128)(2,1)S(1)}, u32[]{:S(2)}, u32[]{:S(2)}) collective-permute-start(bf16[384,384]{1,0:T(8,128)(2,1)S(1)} %get-tuple-element.149.g0), channel_id=1, source_target_pairs={{0,24},{8,0},{16,8},{24,16},{1,25},{9,1},{17,9},{25,17},{2,26},{10... | collective-permute-start | bytes 884744 | tf_op jit(solution)/shard_map/ppermute | solution.py:1149
  138.8 29.5 %collective-permute-start.56 = (bf16[1024,128]{1,0:T(8,128)(2,1)S(1)}, bf16[1024,128]{1,0:T(8,128)(2,1)S(1)}, u32[]{:S(2)}, u32[]{:S(2)}) collective-permute-start(bf16[1024,128]{1,0:T(8,128)(2,1)S(1)} %get-tuple-element.127), channel_id=1, source_target_pairs={{0,1},{1,0},{2,3},{3,2},{4,5},{5,4},{6,7},{7,6},{8,9},{9,8},{10,11... | collective-permute-start | bytes 786440 | tf_op jit(solution)/shard_map/ppermute | solution.py:1143
  142.4 33.9 %collective-permute-start.44 = (bf16[384,384]{1,0:T(8,128)(2,1)S(1)}, bf16[384,384]{1,0:T(8,128)(2,1)S(1)}, u32[]{:S(2)}, u32[]{:S(2)}) collective-permute-start(bf16[384,384]{1,0:T(8,128)(2,1)S(1)} %get-tuple-element.114), channel_id=1, source_target_pairs={{0,8},{8,16},{16,24},{24,0},{1,9},{9,17},{17,25},{25,1},{2,10},{10... | collective-permute-start | bytes 884744 | tf_op jit(solution)/shard_map/ppermute | solution.py:1149
  163.7 21.7 %collective-permute-start.43 = (bf16[384,384]{1,0:T(8,128)(2,1)S(1)}, bf16[384,384]{1,0:T(8,128)(2,1)S(1)}, u32[]{:S(2)}, u32[]{:S(2)}) collective-permute-start(bf16[384,384]{1,0:T(8,128)(2,1)S(1)} %get-tuple-element.112), channel_id=1, source_target_pairs={{0,24},{8,0},{16,8},{24,16},{1,25},{9,1},{17,9},{25,17},{2,26},{10... | collective-permute-start | bytes 884744 | tf_op jit(solution)/shard_map/ppermute | solution.py:1149
  166.9 19.1 %collective-permute-start.49 = (bf16[16,56,384]{2,1,0:T(8,128)(2,1)S(1)}, bf16[16,56,384]{2,1,0:T(8,128)(2,1)S(1)}, u32[]{:S(2)}, u32[]{:S(2)}) collective-permute-start(bf16[16,56,384]{2,1,0:T(8,128)(2,1)S(1)} %bitcast.72), channel_id=1, source_target_pairs={{0,1},{1,0},{2,3},{3,2},{4,5},{5,4},{6,7},{7,6},{8,9},{9,8},{10,11... | collective-permute-start | bytes 2064392 | tf_op jit(solution)/shard_map/ppermute | solution.py:1143
  167.1 18.8 %collective-permute-start.47 = (bf16[384,384]{1,0:T(8,128)(2,1)S(1)}, bf16[384,384]{1,0:T(8,128)(2,1)S(1)}, u32[]{:S(2)}, u32[]{:S(2)}) collective-permute-start(bf16[384,384]{1,0:T(8,128)(2,1)S(1)} %get-tuple-element.143), channel_id=1, source_target_pairs={{0,8},{8,16},{16,24},{24,0},{1,9},{9,17},{17,25},{25,1},{2,10},{10... | collective-permute-start | bytes 884744 | tf_op jit(solution)/shard_map/ppermute | solution.py:1149
  176.3 42.9 %collective-permute-start.31 = (bf16[512,1536]{1,0:T(8,128)(2,1)}, bf16[512,1536]{1,0:T(8,128)(2,1)}, u32[]{:S(2)}, u32[]{:S(2)}) collective-permute-start(bf16[512,1536]{1,0:T(8,128)(2,1)} %get-tuple-element.88), channel_id=1, source_target_pairs={{0,1},{1,0},{2,3},{3,2},{4,5},{5,4},{6,7},{7,6},{8,9},{9,8},{10,11... | collective-permute-start | bytes 4718600 | tf_op jit(solution)/shard_map/ppermute | solution.py:1143
  185.4 49.8 %collective-permute-start.39 = (bf16[512,1536]{1,0:T(8,128)(2,1)}, bf16[512,1536]{1,0:T(8,128)(2,1)}, u32[]{:S(2)}, u32[]{:S(2)}) collective-permute-start(bf16[512,1536]{1,0:T(8,128)(2,1)} %get-tuple-element.108), channel_id=1, source_target_pairs={{0,1},{1,0},{2,3},{3,2},{4,5},{5,4},{6,7},{7,6},{8,9},{9,8},{10,11... | collective-permute-start | bytes 4718600 | tf_op jit(solution)/shard_map/ppermute | solution.py:1143
  186.1 23.3 %collective-permute-start.48 = (bf16[384,384]{1,0:T(8,128)(2,1)S(1)}, bf16[384,384]{1,0:T(8,128)(2,1)S(1)}, u32[]{:S(2)}, u32[]{:S(2)}) collective-permute-start(bf16[384,384]{1,0:T(8,128)(2,1)S(1)} %add_convert_fusion.9), channel_id=1, source_target_pairs={{0,8},{8,16},{16,24},{24,0},{1,9},{9,17},{17,25},{25,1},{2,10},{10... | collective-permute-start | bytes 884744 | tf_op jit(solution)/shard_map/ppermute | solution.py:1149
  212.1 38.6 %all-to-all-start.1 = ((bf16[8,48,768]{2,1,0:T(8,128)(2,1)}), bf16[8,48,768]{2,1,0:T(8,128)(2,1)S(1)}, u32[]{:S(2)}, u32[]{:S(2)}) async-start(bf16[8,48,768]{2,1,0:T(8,128)(2,1)} %shard_map.241), calls=%async_computation.1 | async-start | bytes 1179648 | tf_op jit(solution)/shard_map/all_to_all | solution.py:1451
  215.7 19.6 %collective-permute-start.57 = (bf16[384,384]{1,0:T(8,128)(2,1)}, bf16[384,384]{1,0:T(8,128)(2,1)S(1)}, u32[]{:S(2)}, u32[]{:S(2)}) collective-permute-start(bf16[384,384]{1,0:T(8,128)(2,1)} %copy-done.33), channel_id=1, source_target_pairs={{0,24},{8,0},{16,8},{24,16},{1,25},{9,1},{17,9},{25,17},{2,26},{10... | collective-permute-start | bytes 884744 | tf_op jit(solution)/shard_map/ppermute | solution.py:1149
  215.8 24.8 %collective-permute-start.59 = (bf16[384,384]{1,0:T(8,128)(2,1)}, bf16[384,384]{1,0:T(8,128)(2,1)S(1)}, u32[]{:S(2)}, u32[]{:S(2)}) collective-permute-start(bf16[384,384]{1,0:T(8,128)(2,1)} %add_convert_fusion.8), channel_id=1, source_target_pairs={{0,8},{8,16},{16,24},{24,0},{1,9},{9,17},{17,25},{25,1},{2,10},{10... | collective-permute-start | bytes 884744 | tf_op jit(solution)/shard_map/ppermute | solution.py:1149
  219.1 22.0 %collective-permute-start.55 = (f32[56,384]{1,0:T(8,128)S(1)}, f32[56,384]{1,0:T(8,128)S(1)}, u32[]{:S(2)}, u32[]{:S(2)}) collective-permute-start(f32[56,384]{1,0:T(8,128)S(1)} %get-tuple-element.151), channel_id=1, source_target_pairs={{0,8},{8,16},{16,24},{24,0},{1,9},{9,17},{17,25},{25,1},{2,10},{10... | collective-permute-start | bytes 258056 | tf_op jit(solution)/shard_map/ppermute | solution.py:1149
  219.1 23.1 %collective-permute-start.54 = (f32[56,384]{1,0:T(8,128)S(1)}, f32[56,384]{1,0:T(8,128)S(1)}, u32[]{:S(2)}, u32[]{:S(2)}) collective-permute-start(f32[56,384]{1,0:T(8,128)S(1)} %get-tuple-element.152), channel_id=1, source_target_pairs={{0,16},{8,24},{16,0},{24,8},{1,17},{9,25},{17,1},{25,9},{2,18},{10... | collective-permute-start | bytes 258056 | tf_op jit(solution)/shard_map/ppermute | solution.py:1149
  240.6 20.6 %collective-permute-start.33 = (bf16[128,1536]{1,0:T(8,128)(2,1)}, bf16[128,1536]{1,0:T(8,128)(2,1)S(1)}, u32[]{:S(2)}, u32[]{:S(2)}) collective-permute-start(bf16[128,1536]{1,0:T(8,128)(2,1)} %get-tuple-element.140), channel_id=1, source_target_pairs={{0,4},{1,5},{2,6},{3,7},{4,0},{5,1},{6,2},{7,3},{8,12},{9,13},{10,... | collective-permute-start | bytes 1179656 | tf_op jit(solution)/shard_map/ppermute | solution.py:1143
  241.8 19.4 %collective-permute-start.32 = (bf16[128,1536]{1,0:T(8,128)(2,1)}, bf16[128,1536]{1,0:T(8,128)(2,1)S(1)}, u32[]{:S(2)}, u32[]{:S(2)}) collective-permute-start(bf16[128,1536]{1,0:T(8,128)(2,1)} %get-tuple-element.141), channel_id=1, source_target_pairs={{0,2},{1,3},{2,0},{3,1},{4,6},{5,7},{6,4},{7,5},{8,10},{9,11},{10,... | collective-permute-start | bytes 1179656 | tf_op jit(solution)/shard_map/ppermute | solution.py:1143
  242.9 21.6 %collective-permute-start.42 = (bf16[128,1536]{1,0:T(8,128)(2,1)}, bf16[128,1536]{1,0:T(8,128)(2,1)S(1)}, u32[]{:S(2)}, u32[]{:S(2)}) collective-permute-start(bf16[128,1536]{1,0:T(8,128)(2,1)} %get-tuple-element.135), channel_id=1, source_target_pairs={{0,6},{1,7},{2,4},{3,5},{4,2},{5,3},{6,0},{7,1},{8,14},{9,15},{10,... | collective-permute-start | bytes 1179656 | tf_op jit(solution)/shard_map/ppermute | solution.py:1143
  246.0 24.5 %collective-permute-start.41 = (bf16[128,1536]{1,0:T(8,128)(2,1)}, bf16[128,1536]{1,0:T(8,128)(2,1)S(1)}, u32[]{:S(2)}, u32[]{:S(2)}) collective-permute-start(bf16[128,1536]{1,0:T(8,128)(2,1)} %get-tuple-element.136), channel_id=1, source_target_pairs={{0,4},{1,5},{2,6},{3,7},{4,0},{5,1},{6,2},{7,3},{8,12},{9,13},{10,... | collective-permute-start | bytes 1179656 | tf_op jit(solution)/shard_map/ppermute | solution.py:1143
  247.6 23.0 %collective-permute-start.40 = (bf16[128,1536]{1,0:T(8,128)(2,1)}, bf16[128,1536]{1,0:T(8,128)(2,1)}, u32[]{:S(2)}, u32[]{:S(2)}) collective-permute-start(bf16[128,1536]{1,0:T(8,128)(2,1)} %get-tuple-element.137), channel_id=1, source_target_pairs={{0,2},{1,3},{2,0},{3,1},{4,6},{5,7},{6,4},{7,5},{8,10},{9,11},{10,... | collective-permute-start | bytes 1179656 | tf_op jit(solution)/shard_map/ppermute | solution.py:1143
  (75 other events, 1018.3 us)

commit v4 on v3

--- a/solution.py
+++ b/solution.py
@@ -1011,17 +1011,6 @@
     channels_ref[1:2, :] = mm_exact(head_rows, head_map(own, head_width))[2:3]
 
 
-def lend_kernel(where_ref, p0, p1, p2, p3, out_ref):
-    core = lax.bitwise_and(where_ref[0], 1)
-    third = out_ref.shape[1]
-    for o, part in enumerate((p0, p1, p2, p3)):
-        for k in range(2):
-
-            @pl.when(core == k)
-            def _(o=o, part=part, k=k):
-                out_ref[o] = part[2 * third :, :] if k == 0 else part[:third, :]
-
-
 def place_rows(out_ref, part_ref, borrowed_ref, o, core, at_plane):
     rows = part_ref.shape[0]
     third = rows // 3
@@ -1101,18 +1090,17 @@
     dot_ref[...] = as_row(total, rows) / gain_ref[...].astype(f32)
 
 
-def tokens_out_kernel(
-    where_ref, o0, o1, o2, o3, g0, g1, g2, g3, hidden_ref, cot_ref, sums_ref, norm_ref,
-    output_ref, grad_ref, held, *, inner,
-):
-    rank, plane = where_ref[0], where_ref[1]
+def output_kernel(where_ref, o0, o1, o2, o3, hidden_ref, sums_ref, output_ref, *, inner):
+    sums = jnp.concatenate([sums_ref[where_ref[0]], jnp.zeros((LANES - 8, LANES), f32)], axis=0).T
+    inv_gate = lax.rsqrt(sums[:, 0:1] / inner + norm_epsilon)
+    output_ref[...] = (hidden_ref[...].astype(f32) + inv_gate * total_of((o0, o1, o2, o3))).astype(bf16)
+
+
+def hidden_grad_kernel(where_ref, g0, g1, g2, g3, hidden_ref, cot_ref, norm_ref, grad_ref, held):
+    plane = where_ref[1]
     tokens = hidden_ref[...].astype(f32)
-    sums = jnp.concatenate([sums_ref[rank], jnp.zeros((LANES - 8, LANES), f32)], axis=0).T
-    inv_gate = lax.rsqrt(sums[:, 0:1] / inner + norm_epsilon)
-    output_ref[...] = (tokens + inv_gate * total_of((o0, o1, o2, o3))).astype(bf16)
     inv_rms = lax.rsqrt(jnp.mean(tokens * tokens, axis=1, keepdims=True) + norm_epsilon)
-    width = tokens.shape[1]
-    block = width // 4
+    block = tokens.shape[1] // 4
     grad_ref[...] = total_of((g0, g1, g2, g3))
     for p in range(4):
         at = pl.multiple_of(block * lax.bitwise_and(plane - p + 4, 3), LANES)
@@ -1249,6 +1237,7 @@
     cotangent,
 ):
     plane, rank = lax.axis_index("batch"), lax.axis_index("seq")
+    core = rank % 2
     planes, ranks = lax.axis_size("batch"), lax.axis_size("seq")
     _, span, width = hidden.shape
     rows_in, inner = w_gate_in.shape
@@ -1304,7 +1293,7 @@
             pltpu.VMEM((devices, 8, LANES), f32),
         ],
     )
-    (lent_rows,) = once(lend_kernel, out_parts, [((planes, third, width), bf16)], where)
+    lent_rows = jnp.stack([jnp.where(core == 1, part[:third], part[2 * third :]) for part in out_parts])
     out_borrowed = hop(lent_rows, 1)
 
     sizes = dict(n_taps=taps, head_width=head_width, states=states)
@@ -1449,10 +1438,17 @@
     )
     (d_in,) = once(late_rows_kernel, [*d_gate, *d_conv], [((ranks, rows_in, 2 * own), bf16)])
     d_in = lax.all_to_all(d_in, "seq", 0, 0)
-    output, grad_hidden = once(
-        functools.partial(tokens_out_kernel, inner=inner),
-        [*out_own, *grad_own, hidden[0], cotangent[0], sums, norm_full],
-        [((span, width), bf16), ((span, width), f32)],
+    (output,) = once(
+        functools.partial(output_kernel, inner=inner),
+        [*out_own, hidden[0], sums],
+        [((span, width), bf16)],
+        where,
+        params=whole_grant,
+    )
+    (grad_hidden,) = once(
+        hidden_grad_kernel,
+        [*grad_own, hidden[0], cotangent[0], norm_full],
+        [((span, width), f32)],
         where,
         [pltpu.VMEM((span, width), f32)],
         params=whole_grant,

time: 277 us -> 279 us (level)
  waiting for transfers between devices: 112 us -> 106 us
  local copies, waits for them, and re-layouts: 11.1 us -> 15.3 us
    ppermute x24, waiting for transfers between devices: 63.6 us -> 51.2 us  [plane_hop(): return lax.ppermute(value, 'batch', pairs)]
    ppermute x36, waiting for transfers between devices: 47.9 us -> 54.4 us  [hop(): return lax.ppermute(value, 'seq', pairs)]
    unnamed x93, local copies, waits for them, and re-layouts: 9.89 us -> 14 us
    another operation x0 -> x5, other arithmetic: none -> 3.79 us  [split_local(): jnp.stack([jnp.where(core == 1, part[:third], part[2 * third:]) for part...]
  transfers between devices with their start and end apart: 62 -> 62, of which waited for: 25 -> 20; matrix products, arithmetic and copies ran while one was open for 5% -> 6% of each run, Pallas kernels for 20% -> 20%
where the time goes in v4:
time: 279 us
  waiting for transfers between devices  106 us (38%)
  Pallas kernels  72.6 us (26%)
  starting transfers between devices  68.3 us (24%)
  local copies, waits for them, and re-layouts  15.3 us (5%)
  other arithmetic  12.5 us (4%)
  matrix products  2.96 us (1%)
    ppermute x36, waiting for transfers between devices, hop(): return lax.ppermute(value, 'seq', pairs)  54.4 us
    ppermute x24, waiting for transfers between devices, plane_hop(): return lax.ppermute(value, 'batch', pairs)  51.2 us
    pallas_call x8, Pallas kernels, rows_call(): pl.pallas_call(kernel, out_shape=[jax.ShapeDtypeStruct(shape, dtype) for...  31.6 us
    ppermute x24, starting transfers between devices, plane_hop(): return lax.ppermute(value, 'batch', pairs)  30.5 us
    ppermute x36, starting transfers between devices, hop(): return lax.ppermute(value, 'seq', pairs)  30 us
    pallas_call x2, Pallas kernels, spans_call(): pl.pallas_call(kernel, out_shape=out_shape, grid_spec=pltpu.PrefetchScala...  22.7 us
    unnamed x93, local copies, waits for them, and re-layouts  14 us
    pallas_call x6, Pallas kernels, once(): return call(*([] if where is None else [where]), *inputs)  12.7 us
  transfers between devices with their start and end apart: 62, of which 20 were waited for; matrix products, arithmetic and copies ran while one was open for 6% of the time, Pallas kernels for 20%

profile of v4, /device:TPU:0, one launch (start us, length us, event | category | flops | bytes accessed | tf_op | source)
XLA Modules:
  0.0 278.6 jit_solution(1101112266953482030)
XLA Ops:
  2.9 5.1 %collective-permute-start.9 = (bf16[56,384]{1,0:T(8,128)(2,1)}, bf16[56,384]{1,0:T(8,128)(2,1)S(1)}, u32[]{:S(2)}, u32[]{:S(2)}) collective-permute-start(bf16[56,384]{1,0:T(8,128)(2,1)} %get-tuple-element.72), channel_id=1, source_target_pairs={{0,24},{8,0},{16,8},{24,16},{1,25},{9,1},{17,9},{25,17},{2,26},{10... | collective-permute-start | bytes 129032 | tf_op jit(solution)/shard_map/ppermute | solution.py:1137
  9.8 4.2 %collective-permute-done.7 = bf16[56,384]{1,0:T(8,128)(2,1)S(1)} collective-permute-done((bf16[56,384]{1,0:T(8,128)(2,1)}, bf16[56,384]{1,0:T(8,128)(2,1)S(1)}, u32[]{:S(2)}, u32[]{:S(2)}) %collective-permute-start.7) | collective-permute-done | bytes 43040 | tf_op jit(solution)/shard_map/ppermute | solution.py:1137
  19.1 4.2 %all-to-all-start = ((bf16[8,48,768]{2,1,0:T(8,128)(2,1)}), bf16[8,48,768]{2,1,0:T(8,128)(2,1)}, u32[]{:S(2)}, u32[]{:S(2)}) async-start(bf16[8,48,768]{2,1,0:T(8,128)(2,1)} %get-tuple-element.74), calls=%async_computation | async-start | bytes 1179648 | tf_op jit(solution)/shard_map/all_to_all | solution.py:1268
  23.4 2.9 %collective-permute-start.2 = (bf16[128,1536]{1,0:T(8,128)(2,1)S(1)}, bf16[128,1536]{1,0:T(8,128)(2,1)}, u32[]{:S(2)}, u32[]{:S(2)}) collective-permute-start(bf16[128,1536]{1,0:T(8,128)(2,1)S(1)} %bitcast.62), channel_id=1, source_target_pairs={{0,6},{1,7},{2,4},{3,5},{4,2},{5,3},{6,0},{7,1},{8,14},{9,15},{10,... | collective-permute-start | bytes 1179656 | tf_op jit(solution)/shard_map/ppermute | solution.py:1131
  27.5 17.4 %collective-permute-done.10 = bf16[56,1536]{1,0:T(8,128)(2,1)S(1)} collective-permute-done((bf16[56,1536]{1,0:T(8,128)(2,1)S(1)}, bf16[56,1536]{1,0:T(8,128)(2,1)S(1)}, u32[]{:S(2)}, u32[]{:S(2)}) %collective-permute-start.10) | collective-permute-done | bytes 172064 | tf_op jit(solution)/shard_map/ppermute | solution.py:1131
  51.5 7.2 %collective-permute-done.1.t2 = bf16[128,1536]{1,0:T(8,128)(2,1)} collective-permute-done((bf16[128,1536]{1,0:T(8,128)(2,1)S(1)}, bf16[128,1536]{1,0:T(8,128)(2,1)}, u32[]{:S(2)}, u32[]{:S(2)}) %collective-permute-start.1) | collective-permute-done | bytes 393248 | tf_op jit(solution)/shard_map/ppermute | solution.py:1131
  59.5 7.5 %collective-permute-done.22.c3 = bf16[128,1536]{1,0:T(8,128)(2,1)S(1)} collective-permute-done((bf16[128,1536]{1,0:T(8,128)(2,1)S(1)}, bf16[128,1536]{1,0:T(8,128)(2,1)S(1)}, u32[]{:S(2)}, u32[]{:S(2)}) %collective-permute-start.22) | collective-permute-done | bytes 393248 | tf_op jit(solution)/shard_map/ppermute | solution.py:1131
  67.0 5.4 %collective-permute-done.21.c2 = bf16[128,1536]{1,0:T(8,128)(2,1)} collective-permute-done((bf16[128,1536]{1,0:T(8,128)(2,1)S(1)}, bf16[128,1536]{1,0:T(8,128)(2,1)}, u32[]{:S(2)}, u32[]{:S(2)}) %collective-permute-start.21) | collective-permute-done | bytes 393248 | tf_op jit(solution)/shard_map/ppermute | solution.py:1131
  77.5 14.1 %collective-permute-done.14.w1 = bf16[384,384]{1,0:T(8,128)(2,1)S(1)} collective-permute-done((bf16[384,384]{1,0:T(8,128)(2,1)S(1)}, bf16[384,384]{1,0:T(8,128)(2,1)S(1)}, u32[]{:S(2)}, u32[]{:S(2)}) %collective-permute-start.14) | collective-permute-done | bytes 294944 | tf_op jit(solution)/shard_map/ppermute | solution.py:1137
  109.8 7.1 %shard_map.230 = (bf16[1024,1536]{1,0:T(8,128)(2,1)S(1)}, bf16[1024,640]{1,0:T(8,128)(2,1)S(1)}, f32[1024,128]{1,0:T(8,128)S(1)}, bf16[1536,768]{1,0:T(8,128)(2,1)S(1)}) custom-call(s32[2]{0:T(128)S(1)} %pad_add_fusion.where_ref, bf16[128,1536]{1,0:T(8,128)(2,1)S(1)} %bitcast.65, bf16[128,1536]{1,0:T(8,128)(2,1)} %collective-permute-done.t1, ...), custom_call_target="tpu_custom_call" | custom-call | tf_op jit(solution)/shard_map/pallas_call | solution.py:887
  117.0 7.6 %shard_map.231 = (f32[8,128,640]{2,1,0:T(8,128)S(1)}, bf16[8,128,640]{2,1,0:T(8,128)(2,1)S(1)}, f32[8,128,384]{2,1,0:T(8,128)S(1)}, f32[8,128,384]{2,1,0:T(8,128)S(1)}, f32[8,128,384]{2,1,0:T(8,128)S(1)}) custom-call(s32[2]{0:T(128)S(1)} %pad_add_fusion.where_ref, bf16[8,128,640]{2,1,0:T(8,128)(2,1)S(1)} %bitcast.57, f32[8,128,128]{2,1,0:T(8,128)S(1)} %bitcast.66, ...), custom_call_target="tpu_custom_call" | custom-call | tf_op jit(solution)/shard_map/pallas_call | solution.py:844
  124.6 7.2 %shard_map.232 = (f32[1024,384]{1,0:T(8,128)S(1)}, f32[1024,384]{1,0:T(8,128)S(1)}, f32[8,8,128]{2,1,0:T(8,128)S(1)}, bf16[1024,384]{1,0:T(8,128)(2,1)S(1)}, bf1...) custom-call(s32[2]{0:T(128)S(1)} %pad_add_fusion.where_ref, ...), custom_call_target="tpu_custom_call" | custom-call | tf_op jit(solution)/shard_map/pallas_call | solution.py:887
  139.3 2.7 shard_map.235
  142.1 3.5 %shard_map.240 = (bf16[384,384]{1,0:T(8,128)(2,1)S(1)}, bf16[384,384]{1,0:T(8,128)(2,1)S(1)}, bf16[384,384]{1,0:T(8,128)(2,1)S(1)}, bf16[384,384]{1,0:T(8,128)(2,1)S(1)}) custom-call(s32[2]{0:T(128)S(1)} %pad_add_fusion.where_ref, bf16[1024,1536]{1,0:T(8,128)(2,1)S(1)} %get-tuple-element.76.normed_ref, ...), custom_call_target="tpu_custom_call" | custom-call | tf_op jit(solution)/shard_map/pallas_call | solution.py:887
  145.8 15.2 %shard_map.236 = (bf16[8,128,768]{2,1,0:T(8,128)(2,1)S(1)}, f32[8,640]{1,0:T(8,128)S(1)}, f32[8,128]{1,0:T(8,128)S(1)}) custom-call(s32[2]{0:T(128)S(1)} %pad_add_fusion.where_ref, f32[8,128,384]{2,1,0:T(8,128)S(1)} %bitcast.74, f32[8,128,384]{2,1,0:T(8,128)S(1)} %get-tuple-element.92.inter_ref, f32[8,128,384]{2,1,0:T(8,128)S(1)} %get-tuple-element.93.state_ref, ...), custom_call_target="tpu_custom_call" | custom-call | tf_op jit(solution)/shard_map/pallas_call | solution.py:844
  161.0 3.0 %convolution_convert_fusion.rows_ref = bf16[1536,768]{1,0:T(8,128)(2,1)S(1)} fusion(bf16[1024,1536]{1,0:T(8,128)(2,1)S(1)} %get-tuple-element.76.normed_ref, bf16[1024,768]{1,0:T(8,128)(2,1)S(1)} %bitcast.75), kind=kOutput, calls=%fused_computation | convolution fusion | flops 2417098752 | bytes 7077888 | tf_op jit(solution)/shard_map/dot_general | solution.py:1415
  164.0 3.9 %collective-permute-start.43 = (bf16[384,384]{1,0:T(8,128)(2,1)S(1)}, bf16[384,384]{1,0:T(8,128)(2,1)S(1)}, u32[]{:S(2)}, u32[]{:S(2)}) collective-permute-start(bf16[384,384]{1,0:T(8,128)(2,1)S(1)} %get-tuple-element.108), channel_id=1, source_target_pairs={{0,24},{8,0},{16,8},{24,16},{1,25},{9,1},{17,9},{25,17},{2,26},{10... | collective-permute-start | bytes 884744 | tf_op jit(solution)/shard_map/ppermute | solution.py:1137
  170.3 3.8 %collective-permute-start.46 = (bf16[384,384]{1,0:T(8,128)(2,1)S(1)}, bf16[384,384]{1,0:T(8,128)(2,1)S(1)}, u32[]{:S(2)}, u32[]{:S(2)}) collective-permute-start(bf16[384,384]{1,0:T(8,128)(2,1)S(1)} %get-tuple-element.140), channel_id=1, source_target_pairs={{0,24},{8,0},{16,8},{24,16},{1,25},{9,1},{17,9},{25,17},{2,26},{10... | collective-permute-start | bytes 884744 | tf_op jit(solution)/shard_map/ppermute | solution.py:1137
  174.1 4.1 %shard_map.233 = (bf16[512,1536]{1,0:T(8,128)(2,1)S(1)}, bf16[512,1536]{1,0:T(8,128)(2,1)}) custom-call(s32[2]{0:T(128)S(1)} %pad_add_fusion.where_ref, bf16[1024,384]{1,0:T(8,128)(2,1)S(1)} %get-tuple-element.83.gated_ref, bf16[384,1536]{1,0:T(8,128)(2,1)S(1)} %get-tuple-element.84.out_ref), custom_call_target="tpu_custom_call" | custom-call | tf_op jit(solution)/shard_map/pallas_call | solution.py:887
  179.4 5.6 %shard_map.238 = (bf16[512,1536]{1,0:T(8,128)(2,1)S(1)}, bf16[512,1536]{1,0:T(8,128)(2,1)}) custom-call(bf16[1024,384]{1,0:T(8,128)(2,1)S(1)} %get-tuple-element.90.gate_ref.grad_gate_ref, bf16[1024,768]{1,0:T(8,128)(2,1)S(1)} %bitcast.76, bf16[1536,384]{1,0:T(8,128)(2,1)S(1)} %get-tuple-element.103.w_gate_ref, ...), custom_call_target="tpu_custom_call" | custom-call | tf_op jit(solution)/shard_map/pallas_call | solution.py:814
  185.0 3.3 %shard_map.243 = (bf16[384,384]{1,0:T(8,128)(2,1)S(1)}, bf16[384,384]{1,0:T(8,128)(2,1)S(1)}, bf16[384,384]{1,0:T(8,128)(2,1)S(1)}, bf16[384,384]{1,0:T(8,128)(2,1)S(1)}) custom-call(s32[2]{0:T(128)S(1)} %pad_add_fusion.where_ref, bf16[1024,384]{1,0:T(8,128)(2,1)S(1)} %get-tuple-element.122.projected_ref, ...), custom_call_target="tpu_custom_call" | custom-call | tf_op jit(solution)/shard_map/pallas_call | solution.py:887
  191.1 9.5 %collective-permute-done.58 = bf16[384,384]{1,0:T(8,128)(2,1)S(1)} collective-permute-done((bf16[384,384]{1,0:T(8,128)(2,1)S(1)}, bf16[384,384]{1,0:T(8,128)(2,1)S(1)}, u32[]{:S(2)}, u32[]{:S(2)}) %collective-permute-start.58) | collective-permute-done | bytes 294944 | tf_op jit(solution)/shard_map/ppermute | solution.py:1137
  201.8 5.1 %collective-permute-done.45.g2 = bf16[384,384]{1,0:T(8,128)(2,1)S(1)} collective-permute-done((bf16[384,384]{1,0:T(8,128)(2,1)S(1)}, bf16[384,384]{1,0:T(8,128)(2,1)S(1)}, u32[]{:S(2)}, u32[]{:S(2)}) %collective-permute-start.45) | collective-permute-done | bytes 294944 | tf_op jit(solution)/shard_map/ppermute | solution.py:1137
  209.1 3.3 %collective-permute-done.48.c2 = bf16[384,384]{1,0:T(8,128)(2,1)S(1)} collective-permute-done((bf16[384,384]{1,0:T(8,128)(2,1)S(1)}, bf16[384,384]{1,0:T(8,128)(2,1)S(1)}, u32[]{:S(2)}, u32[]{:S(2)}) %collective-permute-start.48) | collective-permute-done | bytes 294944 | tf_op jit(solution)/shard_map/ppermute | solution.py:1137
  215.5 3.5 %all-to-all-start.1 = ((bf16[8,48,768]{2,1,0:T(8,128)(2,1)}), bf16[8,48,768]{2,1,0:T(8,128)(2,1)S(1)}, u32[]{:S(2)}, u32[]{:S(2)}) async-start(bf16[8,48,768]{2,1,0:T(8,128)(2,1)} %shard_map.241), calls=%async_computation.1 | async-start | bytes 1179648 | tf_op jit(solution)/shard_map/all_to_all | solution.py:1440
  225.0 2.7 add_convert_fusion.4
  227.6 11.0 %collective-permute-done.57.p1 = bf16[384,384]{1,0:T(8,128)(2,1)S(1)} collective-permute-done((bf16[384,384]{1,0:T(8,128)(2,1)}, bf16[384,384]{1,0:T(8,128)(2,1)S(1)}, u32[]{:S(2)}, u32[]{:S(2)}) %collective-permute-start.57) | collective-permute-done | bytes 294944 | tf_op jit(solution)/shard_map/ppermute | solution.py:1137
  241.1 2.9 %add_convert_fusion = (bf16[128,1536]{1,0:T(8,128)(2,1)}, bf16[128,1536]{1,0:T(8,128)(2,1)}, bf16[128,1536]{1,0:T(8,128)(2,1)}, bf16[128,1536]{1,0:T(8,128)(2,1)}) fusion(bf16[512,1536]{1,0:T(8,128)(2,1)} %collective-permute-done.39, bf16[512,1536]{1,0:T(8,128)(2,1)S(1)} %get-tuple-element.105), kind=kLoop, calls=%fused_computation.1 | loop fusion | flops 3145728 | bytes 4718592 | tf_op jit(solution)/shard_map/convert_element_type | solution.py:1173
  258.2 6.4 %collective-permute-done.33.o2 = bf16[128,1536]{1,0:T(8,128)(2,1)S(1)} collective-permute-done((bf16[128,1536]{1,0:T(8,128)(2,1)}, bf16[128,1536]{1,0:T(8,128)(2,1)S(1)}, u32[]{:S(2)}, u32[]{:S(2)}) %collective-permute-start.33) | collective-permute-done | bytes 393248 | tf_op jit(solution)/shard_map/ppermute | solution.py:1131
  265.3 3.2 %shard_map.234 = bf16[128,1536]{1,0:T(8,128)(2,1)} custom-call(s32[2]{0:T(128)} %copy-done.30, bf16[128,1536]{1,0:T(8,128)(2,1)} %get-tuple-element.138.o0, bf16[128,1536]{1,0:T(8,128)(2,1)} %collective-permute-done.32.o1, bf16[128,1536]{1,0:T(8,128)(2,1)} %copy-done.41, bf16[128,1536]{1,0:T(8,128)(2,1)} %copy-done.40, bf16[128,1536]{1,0:T(8,128)(2,1)} %bitcast.60, ...), custom_call_target="tpu_custom_call" | custom-call | tf_op jit(solution)/shard_map/pallas_call | solution.py:1125
  268.6 5.4 %collective-permute-done.41.g2 = bf16[128,1536]{1,0:T(8,128)(2,1)S(1)} collective-permute-done((bf16[128,1536]{1,0:T(8,128)(2,1)}, bf16[128,1536]{1,0:T(8,128)(2,1)S(1)}, u32[]{:S(2)}, u32[]{:S(2)}) %collective-permute-start.41) | collective-permute-done | bytes 393248 | tf_op jit(solution)/shard_map/ppermute | solution.py:1131
  274.8 3.8 %shard_map.239 = f32[128,1536]{1,0:T(8,128)} custom-call(s32[2]{0:T(128)} %copy-done.30, bf16[128,1536]{1,0:T(8,128)(2,1)} %get-tuple-element.134.g0, bf16[128,1536]{1,0:T(8,128)(2,1)} %copy-done.39, bf16[128,1536]{1,0:T(8,128)(2,1)} %copy-done.38, bf16[128,1536]{1,0:T(8,128)(2,1)} %copy-done.37, bf16[128,1536]{1,0:T(8,128)(2,1)} %bitcast.61, ...), custom_call_target="tpu_custom_call" | custom-call | tf_op jit(solution)/shard_map/pallas_call | solution.py:1125
  (224 shorter events, 85.6 us)
Async XLA Ops:
  17.1 29.3 %collective-permute-start.29 = (bf16[96,1536]{1,0:T(8,128)(2,1)}, bf16[96,1536]{1,0:T(8,128)(2,1)S(1)}, u32[]{:S(2)}, u32[]{:S(2)}) collective-permute-start(bf16[96,1536]{1,0:T(8,128)(2,1)} %w_ref.1), channel_id=1, source_target_pairs={{0,24},{8,0},{16,8},{24,16},{1,25},{9,1},{17,9},{25,17},{2,26},{10... | collective-permute-start | bytes 884744 | tf_op jit(solution)/shard_map/ppermute | solution.py:1137
  17.9 29.2 %collective-permute-start.27 = (bf16[96,1536]{1,0:T(8,128)(2,1)}, bf16[96,1536]{1,0:T(8,128)(2,1)S(1)}, u32[]{:S(2)}, u32[]{:S(2)}) collective-permute-start(bf16[96,1536]{1,0:T(8,128)(2,1)} %w_ref.1), channel_id=1, source_target_pairs={{0,8},{8,16},{16,24},{24,0},{1,9},{9,17},{17,25},{25,1},{2,10},{10... | collective-permute-start | bytes 884744 | tf_op jit(solution)/shard_map/ppermute | solution.py:1137
  19.1 27.9 %collective-permute-start.3 = (bf16[128,1536]{1,0:T(8,128)(2,1)}, bf16[128,1536]{1,0:T(8,128)(2,1)S(1)}, u32[]{:S(2)}, u32[]{:S(2)}) collective-permute-start(bf16[128,1536]{1,0:T(8,128)(2,1)} %bitcast.59), channel_id=1, source_target_pairs={{0,1},{1,0},{2,3},{3,2},{4,5},{5,4},{6,7},{7,6},{8,9},{9,8},{10,11... | collective-permute-start | bytes 1179656 | tf_op jit(solution)/shard_map/ppermute | solution.py:1131
  19.1 53.9 %all-to-all-start = ((bf16[8,48,768]{2,1,0:T(8,128)(2,1)}), bf16[8,48,768]{2,1,0:T(8,128)(2,1)}, u32[]{:S(2)}, u32[]{:S(2)}) async-start(bf16[8,48,768]{2,1,0:T(8,128)(2,1)} %get-tuple-element.74), calls=%async_computation | async-start | bytes 1179648 | tf_op jit(solution)/shard_map/all_to_all | solution.py:1268
  23.4 25.9 %collective-permute-start.2 = (bf16[128,1536]{1,0:T(8,128)(2,1)S(1)}, bf16[128,1536]{1,0:T(8,128)(2,1)}, u32[]{:S(2)}, u32[]{:S(2)}) collective-permute-start(bf16[128,1536]{1,0:T(8,128)(2,1)S(1)} %bitcast.62), channel_id=1, source_target_pairs={{0,6},{1,7},{2,4},{3,5},{4,2},{5,3},{6,0},{7,1},{8,14},{9,15},{10,... | collective-permute-start | bytes 1179656 | tf_op jit(solution)/shard_map/ppermute | solution.py:1131
  47.9 19.1 %collective-permute-start.22 = (bf16[128,1536]{1,0:T(8,128)(2,1)S(1)}, bf16[128,1536]{1,0:T(8,128)(2,1)S(1)}, u32[]{:S(2)}, u32[]{:S(2)}) collective-permute-start(bf16[128,1536]{1,0:T(8,128)(2,1)S(1)} %bitcast.70), channel_id=1, source_target_pairs={{0,6},{1,7},{2,4},{3,5},{4,2},{5,3},{6,0},{7,1},{8,14},{9,15},{10,... | collective-permute-start | bytes 1179656 | tf_op jit(solution)/shard_map/ppermute | solution.py:1131
  49.3 23.1 %collective-permute-start.21 = (bf16[128,1536]{1,0:T(8,128)(2,1)S(1)}, bf16[128,1536]{1,0:T(8,128)(2,1)}, u32[]{:S(2)}, u32[]{:S(2)}) collective-permute-start(bf16[128,1536]{1,0:T(8,128)(2,1)S(1)} %bitcast.71), channel_id=1, source_target_pairs={{0,4},{1,5},{2,6},{3,7},{4,0},{5,1},{6,2},{7,3},{8,12},{9,13},{10,... | collective-permute-start | bytes 1179656 | tf_op jit(solution)/shard_map/ppermute | solution.py:1131
  74.2 25.0 %collective-permute-start.13 = (bf16[224,1536]{1,0:T(8,128)(2,1)S(1)}, bf16[224,1536]{1,0:T(8,128)(2,1)S(1)}, u32[]{:S(2)}, u32[]{:S(2)}) collective-permute-start(bf16[224,1536]{1,0:T(8,128)(2,1)S(1)} %pad_maximum_fusion.mine_ref), channel_id=1, source_target_pairs={{0,1},{1,0},{2,3},{3,2},{4,5},{5,4},{6,7},{7,6},{8,9},{9,8},{10,11... | collective-permute-start | bytes 2064392 | tf_op jit(solution)/shard_map/ppermute | solution.py:1131
  74.8 20.7 %collective-permute-start.26 = (bf16[128,1536]{1,0:T(8,128)(2,1)}, bf16[128,1536]{1,0:T(8,128)(2,1)S(1)}, u32[]{:S(2)}, u32[]{:S(2)}) collective-permute-start(bf16[128,1536]{1,0:T(8,128)(2,1)} %copy-done.11), channel_id=1, source_target_pairs={{0,1},{1,0},{2,3},{3,2},{4,5},{5,4},{6,7},{7,6},{8,9},{9,8},{10,11... | collective-permute-start | bytes 1179656 | tf_op jit(solution)/shard_map/ppermute | solution.py:1131
  74.8 23.1 %collective-permute-start.16 = (bf16[384,384]{1,0:T(8,128)(2,1)S(1)}, bf16[384,384]{1,0:T(8,128)(2,1)S(1)}, u32[]{:S(2)}, u32[]{:S(2)}) collective-permute-start(bf16[384,384]{1,0:T(8,128)(2,1)S(1)} %get-tuple-element.146.w0), channel_id=1, source_target_pairs={{0,24},{8,0},{16,8},{24,16},{1,25},{9,1},{17,9},{25,17},{2,26},{10... | collective-permute-start | bytes 884744 | tf_op jit(solution)/shard_map/ppermute | solution.py:1137
  77.4 20.5 %collective-permute-start.17 = (bf16[384,384]{1,0:T(8,128)(2,1)S(1)}, bf16[384,384]{1,0:T(8,128)(2,1)S(1)}, u32[]{:S(2)}, u32[]{:S(2)}) collective-permute-start(bf16[384,384]{1,0:T(8,128)(2,1)S(1)} %get-tuple-element.145.g0), channel_id=1, source_target_pairs={{0,8},{8,16},{16,24},{24,0},{1,9},{9,17},{17,25},{25,1},{2,10},{10... | collective-permute-start | bytes 884744 | tf_op jit(solution)/shard_map/ppermute | solution.py:1137
  96.2 28.3 %collective-permute-start.25 = (bf16[128,1536]{1,0:T(8,128)(2,1)}, bf16[128,1536]{1,0:T(8,128)(2,1)}, u32[]{:S(2)}, u32[]{:S(2)}) collective-permute-start(bf16[128,1536]{1,0:T(8,128)(2,1)} %collective-permute-done.21.c2), channel_id=1, source_target_pairs={{0,1},{1,0},{2,3},{3,2},{4,5},{5,4},{6,7},{7,6},{8,9},{9,8},{10,11... | collective-permute-start | bytes 1179656 | tf_op jit(solution)/shard_map/ppermute | solution.py:1131
  97.9 26.6 %collective-permute-start.24 = (bf16[128,1536]{1,0:T(8,128)(2,1)}, bf16[128,1536]{1,0:T(8,128)(2,1)}, u32[]{:S(2)}, u32[]{:S(2)}) collective-permute-start(bf16[128,1536]{1,0:T(8,128)(2,1)} %collective-permute-done.20.c1), channel_id=1, source_target_pairs={{0,1},{1,0},{2,3},{3,2},{4,5},{5,4},{6,7},{7,6},{8,9},{9,8},{10,11... | collective-permute-start | bytes 1179656 | tf_op jit(solution)/shard_map/ppermute | solution.py:1131
  98.7 25.9 %collective-permute-start.30 = (bf16[4,32,1536]{2,1,0:T(8,128)(2,1)}, bf16[4,32,1536]{2,1,0:T(8,128)(2,1)}, u32[]{:S(2)}, u32[]{:S(2)}) collective-permute-start(bf16[4,32,1536]{2,1,0:T(8,128)(2,1)} %pad_maximum_fusion.1), channel_id=1, source_target_pairs={{0,1},{1,0},{2,3},{3,2},{4,5},{5,4},{6,7},{7,6},{8,9},{9,8},{10,11... | collective-permute-start | bytes 1179656 | tf_op jit(solution)/shard_map/ppermute | solution.py:1131
  100.0 24.5 %collective-permute-start.19 = (bf16[384,384]{1,0:T(8,128)(2,1)S(1)}, bf16[384,384]{1,0:T(8,128)(2,1)}, u32[]{:S(2)}, u32[]{:S(2)}) collective-permute-start(bf16[384,384]{1,0:T(8,128)(2,1)S(1)} %get-tuple-element.145.g0), channel_id=1, source_target_pairs={{0,24},{8,0},{16,8},{24,16},{1,25},{9,1},{17,9},{25,17},{2,26},{10... | collective-permute-start | bytes 884744 | tf_op jit(solution)/shard_map/ppermute | solution.py:1137
  105.0 19.5 %collective-permute-start.18 = (bf16[384,384]{1,0:T(8,128)(2,1)S(1)}, bf16[384,384]{1,0:T(8,128)(2,1)}, u32[]{:S(2)}, u32[]{:S(2)}) collective-permute-start(bf16[384,384]{1,0:T(8,128)(2,1)S(1)} %collective-permute-done.17.g1), channel_id=1, source_target_pairs={{0,8},{8,16},{16,24},{24,0},{1,9},{9,17},{17,25},{25,1},{2,10},{10... | collective-permute-start | bytes 884744 | tf_op jit(solution)/shard_map/ppermute | solution.py:1137
  142.0 28.3 %collective-permute-start.56 = (bf16[1024,128]{1,0:T(8,128)(2,1)S(1)}, bf16[1024,128]{1,0:T(8,128)(2,1)S(1)}, u32[]{:S(2)}, u32[]{:S(2)}) collective-permute-start(bf16[1024,128]{1,0:T(8,128)(2,1)S(1)} %get-tuple-element.123), channel_id=1, source_target_pairs={{0,1},{1,0},{2,3},{3,2},{4,5},{5,4},{6,7},{7,6},{8,9},{9,8},{10,11... | collective-permute-start | bytes 786440 | tf_op jit(solution)/shard_map/ppermute | solution.py:1131
  145.6 33.8 %collective-permute-start.44 = (bf16[384,384]{1,0:T(8,128)(2,1)S(1)}, bf16[384,384]{1,0:T(8,128)(2,1)S(1)}, u32[]{:S(2)}, u32[]{:S(2)}) collective-permute-start(bf16[384,384]{1,0:T(8,128)(2,1)S(1)} %get-tuple-element.110), channel_id=1, source_target_pairs={{0,8},{8,16},{16,24},{24,0},{1,9},{9,17},{17,25},{25,1},{2,10},{10... | collective-permute-start | bytes 884744 | tf_op jit(solution)/shard_map/ppermute | solution.py:1137
  164.0 24.5 %collective-permute-start.43 = (bf16[384,384]{1,0:T(8,128)(2,1)S(1)}, bf16[384,384]{1,0:T(8,128)(2,1)S(1)}, u32[]{:S(2)}, u32[]{:S(2)}) collective-permute-start(bf16[384,384]{1,0:T(8,128)(2,1)S(1)} %get-tuple-element.108), channel_id=1, source_target_pairs={{0,24},{8,0},{16,8},{24,16},{1,25},{9,1},{17,9},{25,17},{2,26},{10... | collective-permute-start | bytes 884744 | tf_op jit(solution)/shard_map/ppermute | solution.py:1137
  179.4 43.1 %collective-permute-start.31 = (bf16[512,1536]{1,0:T(8,128)(2,1)}, bf16[512,1536]{1,0:T(8,128)(2,1)}, u32[]{:S(2)}, u32[]{:S(2)}) collective-permute-start(bf16[512,1536]{1,0:T(8,128)(2,1)} %get-tuple-element.86), channel_id=1, source_target_pairs={{0,1},{1,0},{2,3},{3,2},{4,5},{5,4},{6,7},{7,6},{8,9},{9,8},{10,11... | collective-permute-start | bytes 4718600 | tf_op jit(solution)/shard_map/ppermute | solution.py:1131
  188.5 50.2 %collective-permute-start.39 = (bf16[512,1536]{1,0:T(8,128)(2,1)}, bf16[512,1536]{1,0:T(8,128)(2,1)}, u32[]{:S(2)}, u32[]{:S(2)}) collective-permute-start(bf16[512,1536]{1,0:T(8,128)(2,1)} %get-tuple-element.106), channel_id=1, source_target_pairs={{0,1},{1,0},{2,3},{3,2},{4,5},{5,4},{6,7},{7,6},{8,9},{9,8},{10,11... | collective-permute-start | bytes 4718600 | tf_op jit(solution)/shard_map/ppermute | solution.py:1131
  189.1 23.3 %collective-permute-start.48 = (bf16[384,384]{1,0:T(8,128)(2,1)S(1)}, bf16[384,384]{1,0:T(8,128)(2,1)S(1)}, u32[]{:S(2)}, u32[]{:S(2)}) collective-permute-start(bf16[384,384]{1,0:T(8,128)(2,1)S(1)} %add_convert_fusion.9), channel_id=1, source_target_pairs={{0,8},{8,16},{16,24},{24,0},{1,9},{9,17},{17,25},{25,1},{2,10},{10... | collective-permute-start | bytes 884744 | tf_op jit(solution)/shard_map/ppermute | solution.py:1137
  215.5 38.6 %all-to-all-start.1 = ((bf16[8,48,768]{2,1,0:T(8,128)(2,1)}), bf16[8,48,768]{2,1,0:T(8,128)(2,1)S(1)}, u32[]{:S(2)}, u32[]{:S(2)}) async-start(bf16[8,48,768]{2,1,0:T(8,128)(2,1)} %shard_map.241), calls=%async_computation.1 | async-start | bytes 1179648 | tf_op jit(solution)/shard_map/all_to_all | solution.py:1440
  219.1 19.6 %collective-permute-start.57 = (bf16[384,384]{1,0:T(8,128)(2,1)}, bf16[384,384]{1,0:T(8,128)(2,1)S(1)}, u32[]{:S(2)}, u32[]{:S(2)}) collective-permute-start(bf16[384,384]{1,0:T(8,128)(2,1)} %copy-done.35), channel_id=1, source_target_pairs={{0,24},{8,0},{16,8},{24,16},{1,25},{9,1},{17,9},{25,17},{2,26},{10... | collective-permute-start | bytes 884744 | tf_op jit(solution)/shard_map/ppermute | solution.py:1137
  219.2 24.8 %collective-permute-start.59 = (bf16[384,384]{1,0:T(8,128)(2,1)}, bf16[384,384]{1,0:T(8,128)(2,1)S(1)}, u32[]{:S(2)}, u32[]{:S(2)}) collective-permute-start(bf16[384,384]{1,0:T(8,128)(2,1)} %add_convert_fusion.8), channel_id=1, source_target_pairs={{0,8},{8,16},{16,24},{24,0},{1,9},{9,17},{17,25},{25,1},{2,10},{10... | collective-permute-start | bytes 884744 | tf_op jit(solution)/shard_map/ppermute | solution.py:1137
  222.5 22.1 %collective-permute-start.55 = (f32[56,384]{1,0:T(8,128)S(1)}, f32[56,384]{1,0:T(8,128)S(1)}, u32[]{:S(2)}, u32[]{:S(2)}) collective-permute-start(f32[56,384]{1,0:T(8,128)S(1)} %get-tuple-element.147), channel_id=1, source_target_pairs={{0,8},{8,16},{16,24},{24,0},{1,9},{9,17},{17,25},{25,1},{2,10},{10... | collective-permute-start | bytes 258056 | tf_op jit(solution)/shard_map/ppermute | solution.py:1137
  222.6 23.1 %collective-permute-start.54 = (f32[56,384]{1,0:T(8,128)S(1)}, f32[56,384]{1,0:T(8,128)S(1)}, u32[]{:S(2)}, u32[]{:S(2)}) collective-permute-start(f32[56,384]{1,0:T(8,128)S(1)} %get-tuple-element.148), channel_id=1, source_target_pairs={{0,16},{8,24},{16,0},{24,8},{1,17},{9,25},{17,1},{25,9},{2,18},{10... | collective-permute-start | bytes 258056 | tf_op jit(solution)/shard_map/ppermute | solution.py:1137
  244.0 20.6 %collective-permute-start.33 = (bf16[128,1536]{1,0:T(8,128)(2,1)}, bf16[128,1536]{1,0:T(8,128)(2,1)S(1)}, u32[]{:S(2)}, u32[]{:S(2)}) collective-permute-start(bf16[128,1536]{1,0:T(8,128)(2,1)} %get-tuple-element.136), channel_id=1, source_target_pairs={{0,4},{1,5},{2,6},{3,7},{4,0},{5,1},{6,2},{7,3},{8,12},{9,13},{10,... | collective-permute-start | bytes 1179656 | tf_op jit(solution)/shard_map/ppermute | solution.py:1131
  245.2 19.4 %collective-permute-start.32 = (bf16[128,1536]{1,0:T(8,128)(2,1)}, bf16[128,1536]{1,0:T(8,128)(2,1)}, u32[]{:S(2)}, u32[]{:S(2)}) collective-permute-start(bf16[128,1536]{1,0:T(8,128)(2,1)} %get-tuple-element.137), channel_id=1, source_target_pairs={{0,2},{1,3},{2,0},{3,1},{4,6},{5,7},{6,4},{7,5},{8,10},{9,11},{10,... | collective-permute-start | bytes 1179656 | tf_op jit(solution)/shard_map/ppermute | solution.py:1131
  246.3 22.2 %collective-permute-start.42 = (bf16[128,1536]{1,0:T(8,128)(2,1)}, bf16[128,1536]{1,0:T(8,128)(2,1)S(1)}, u32[]{:S(2)}, u32[]{:S(2)}) collective-permute-start(bf16[128,1536]{1,0:T(8,128)(2,1)} %get-tuple-element.131), channel_id=1, source_target_pairs={{0,6},{1,7},{2,4},{3,5},{4,2},{5,3},{6,0},{7,1},{8,14},{9,15},{10,... | collective-permute-start | bytes 1179656 | tf_op jit(solution)/shard_map/ppermute | solution.py:1131
  249.4 24.5 %collective-permute-start.41 = (bf16[128,1536]{1,0:T(8,128)(2,1)}, bf16[128,1536]{1,0:T(8,128)(2,1)S(1)}, u32[]{:S(2)}, u32[]{:S(2)}) collective-permute-start(bf16[128,1536]{1,0:T(8,128)(2,1)} %get-tuple-element.132), channel_id=1, source_target_pairs={{0,4},{1,5},{2,6},{3,7},{4,0},{5,1},{6,2},{7,3},{8,12},{9,13},{10,... | collective-permute-start | bytes 1179656 | tf_op jit(solution)/shard_map/ppermute | solution.py:1131
  251.0 22.9 %collective-permute-start.40 = (bf16[128,1536]{1,0:T(8,128)(2,1)}, bf16[128,1536]{1,0:T(8,128)(2,1)S(1)}, u32[]{:S(2)}, u32[]{:S(2)}) collective-permute-start(bf16[128,1536]{1,0:T(8,128)(2,1)} %get-tuple-element.133), channel_id=1, source_target_pairs={{0,2},{1,3},{2,0},{3,1},{4,6},{5,7},{6,4},{7,5},{8,10},{9,11},{10,... | collective-permute-start | bytes 1179656 | tf_op jit(solution)/shard_map/ppermute | solution.py:1131
  (75 other events, 893.2 us)
